TPU v7x, 32 devices: a whole 2x2x4 slice. The times are simulated.
32 devices in a mesh: gx: 8 (over z, x), yz: 4 (over y, core).
Axes of the slice: x: 2, y: 2, z: 4, core: 2. Of those that a mesh axis runs over, the one named last changes fastest.
Arguments:
- pops_start: float32 [64, 19, 16, 512], P(('gx', 'yz'))
- tile_pos: int32 [64], replicated, may hold values from -1 to 7, as said below
- wall_mask: int32 [64, 16, 512], P(('gx', 'yz')), may hold values 0 or 1
- wall_frac: float32 [64, 16, 512], P(('gx', 'yz')), may hold values from 0.2 to 0.9
- patch_id: int32 [64, 16, 512], P(('gx', 'yz')), may hold values from 0 to 2047
- probe: float32 [64, 16, 512], P(('gx', 'yz')), may hold values from -4 to 4
Outputs:
- pops_final: float32 [64, 19, 16, 512], P(('gx', 'yz'))
- adjoint_start: float32 [64, 19, 16, 512], P(('gx', 'yz'))
- patch_sens: float32 [2048], P(('gx', 'yz'))
Inputs may be any that keep to these rules, and one draw needn't show every extreme that they name: Slots with tile_pos -1 are empty. Each device's live slots come first; every device holds 1 to 2 tiles and some device holds 2. Within one gx index no position appears twice.
All inputs are finite; a program needn't handle non-finite values. No bound on the sum of `wall_mask` on one device may be relied on, other than what follows from the above.
Results may differ from a plain program's by a relative error of at most 0.0003.
Values sent between devices are 32-bit elements; how exact they have to be, the bound alone decides.
No kernel may reach another device: no remote copies, remote signals or barrier semaphores. Data moves between devices by JAX's collectives and lax.ppermute only.
A program may use at most 256 MiB of HBM per device.

v0:
```python
import jax
import jax.numpy as jnp
import numpy as np
from jax import lax
from jax.sharding import PartitionSpec as P

TL = 16
TA = 16
TB = 32
STEPS = 2
PATCH_DEV = 64


VELOCITY = np.array(
    [
        [0, 0, 0],
        [1, 0, 0],
        [-1, 0, 0],
        [0, 1, 0],
        [0, -1, 0],
        [0, 0, 1],
        [0, 0, -1],
        [1, 1, 0],
        [-1, -1, 0],
        [1, -1, 0],
        [-1, 1, 0],
        [1, 0, 1],
        [-1, 0, -1],
        [1, 0, -1],
        [-1, 0, 1],
        [0, 1, 1],
        [0, -1, -1],
        [0, 1, -1],
        [0, -1, 1],
    ]
)
WEIGHTS = [1.0 / 3.0] + [1.0 / 18.0] * 6 + [1.0 / 36.0] * 12
REVERSE = [0, 2, 1, 4, 3, 6, 5, 8, 7, 10, 9, 12, 11, 14, 13, 16, 15, 18, 17]
OMEGA = 1.25


def padded(x, sides, width):
    for axis, dim in sides:
        count, length = (lax.axis_size(axis), x.shape[dim])
        up = [(i, (i + 1) % count) for i in range(count - 1)]
        down = [(j, i) for i, j in up]
        last = lax.slice_in_dim(x, length - width, length, axis=dim)
        initial = lax.slice_in_dim(x, 0, width, axis=dim)
        before = lax.ppermute(last, axis, up)
        after = lax.ppermute(initial, axis, down)
        x = jnp.concatenate([before, x, after], axis=dim)
    return x


def members_of(dim, value):
    return [i for i in range(19) if int(VELOCITY[i, dim]) == value]


def collide(field, solid):
    shape = (19,) + (1,) * (field.ndim - 1)
    vel_l = jnp.asarray(VELOCITY[:, 0], jnp.float32).reshape(shape)
    vel_a = jnp.asarray(VELOCITY[:, 1], jnp.float32).reshape(shape)
    vel_b = jnp.asarray(VELOCITY[:, 2], jnp.float32).reshape(shape)
    weight = jnp.asarray(WEIGHTS, jnp.float32).reshape(shape)
    density = jnp.sum(field, axis=0)
    speed_l = jnp.sum(field * vel_l, axis=0) / density
    speed_a = jnp.sum(field * vel_a, axis=0) / density
    speed_b = jnp.sum(field * vel_b, axis=0) / density
    square = speed_l * speed_l + speed_a * speed_a + speed_b * speed_b
    along = vel_l * speed_l + vel_a * speed_a + vel_b * speed_b
    equil = weight * density * (1.0 + 3.0 * along + 4.5 * along * along - 1.5 * square)
    relaxed = field - OMEGA * (field - equil)
    reverse = jnp.concatenate([field[i : i + 1] for i in REVERSE], axis=0)
    return (1.0 - solid) * relaxed + solid * reverse


def faces(field, sign):
    count = field.shape[0]
    cube = field.reshape(count, 19, TL, TA, TB)

    def select(plane, dim, side):
        return jnp.stack([plane[:, i] for i in members_of(dim, sign * side)], axis=1)

    l_faces = jnp.stack(
        [
            select(cube[:, :, 0], 0, -1).reshape(count, 5, TA * TB),
            select(cube[:, :, TL - 1], 0, 1).reshape(count, 5, TA * TB),
        ],
        axis=1,
    )
    a_faces = jnp.stack(
        [
            select(cube[:, :, :, 0], 1, -1).reshape(count, 5, TL * TB),
            select(cube[:, :, :, TA - 1], 1, 1).reshape(count, 5, TL * TB),
        ],
        axis=1,
    )
    b_faces = jnp.stack(
        [
            select(cube[:, :, :, :, 0], 2, -1).reshape(count, 5, TL * TA),
            select(cube[:, :, :, :, TB - 1], 2, 1).reshape(count, 5, TL * TA),
        ],
        axis=1,
    )
    return (l_faces, a_faces, b_faces)


def stream(field, sign, fill, tile_pos):
    count = field.shape[0]
    l_faces, a_faces, b_faces = faces(field, sign)
    group_l, group_a, group_b = (
        lax.all_gather(l_faces, "yz", axis=0, tiled=True),
        lax.all_gather(a_faces, "yz", axis=0, tiled=True),
        lax.all_gather(b_faces, "yz", axis=0, tiled=True),
    )
    beside_all = padded(group_l, (("gx", 1),), 1)
    lower_high = beside_all[:, 0]
    upper_low = beside_all[:, 3]
    n_layers = lax.axis_size("gx")
    n_cross = lax.axis_size("yz")
    group = n_cross * count
    layer = lax.axis_index("gx")
    cross = lax.axis_index("yz")

    def layer_positions(offset):
        target = layer + offset
        valid = (target >= 0) & (target < n_layers)
        block_pos = lax.dynamic_slice_in_dim(
            tile_pos, jnp.clip(target, 0, n_layers - 1) * group, group
        )
        return jnp.where(valid, block_pos, -1)

    own_pos = lax.dynamic_slice_in_dim(tile_pos, (layer * n_cross + cross) * count, count)
    cross_a = own_pos // count
    cross_b = own_pos % count
    positions = {-1: layer_positions(-1), 0: layer_positions(0), 1: layer_positions(1)}
    fill_vec = jnp.asarray(fill, jnp.float32)
    always = jnp.ones((count,), bool)

    def source_of(dim, side):
        if dim == 0:
            return lower_high if side < 0 else upper_low
        if dim == 1:
            return group_a[:, 1 if side < 0 else 0]
        return group_b[:, 1 if side < 0 else 0]

    def pick(towards, source):
        target_a = cross_a + towards[1]
        target_b = cross_b + towards[2]
        inside = (
            (own_pos >= 0)
            & (target_a >= 0)
            & (target_a < n_cross)
            & (target_b >= 0)
            & (target_b < count)
        )
        wanted = target_a * count + target_b
        matches = (positions[towards[0]][None, :] == wanted[:, None]) & inside[:, None]
        found = jnp.any(matches, axis=1)
        selector = matches.astype(jnp.float32)
        picked = jnp.einsum("cg,gkp->ckp", selector, source, precision=lax.Precision.HIGHEST)
        return (picked, found)

    def widen(picked, members, found, tail):
        flag = found.reshape((count,) + (1,) * len(tail))
        rows = []
        for i in range(19):
            if i in members:
                rows.append(jnp.where(flag, picked[:, members.index(i)], fill[i]))
            else:
                rows.append(jnp.full((count,) + tail, fill[i], jnp.float32))
        return jnp.stack(rows, axis=1)

    def face_slab(dim, side, tail):
        towards = [0, 0, 0]
        towards[dim] = side
        members = members_of(dim, -side * sign)
        picked, found = pick(towards, source_of(dim, side))
        return widen(picked.reshape((count, 5) + tail), members, found, tail)

    def edge_line(dim_one, side_one, dim_two, side_two):
        towards = [0, 0, 0]
        towards[dim_one] = side_one
        towards[dim_two] = side_two
        members = members_of(dim_one, -side_one * sign)
        target = [i for i in members if int(VELOCITY[i, dim_two]) == -side_two * sign][0]
        picked, found = pick(towards, source_of(dim_one, side_one))
        value = picked[:, members.index(target)]
        extents = (TL, TA, TB)
        index = extents[dim_two] - 1 if side_two < 0 else 0
        if dim_one == 0:
            plane = value.reshape(count, TA, TB)
            line = plane[:, index, :] if dim_two == 1 else plane[:, :, index]
        else:
            plane = value.reshape(count, TL, TB)
            line = plane[:, :, index]
        line = jnp.where(found[:, None], line, fill[target])
        return widen(line[:, None], [target], always, (line.shape[1],))

    cube = field.reshape(count, 19, TL, TA, TB)
    extended = jnp.concatenate(
        [face_slab(0, -1, (1, TA, TB)), cube, face_slab(0, 1, (1, TA, TB))], axis=2
    )

    def a_slab(side):
        middle = face_slab(1, side, (TL, 1, TB))
        low_edge = edge_line(0, -1, 1, side).reshape(count, 19, 1, 1, TB)
        high_edge = edge_line(0, 1, 1, side).reshape(count, 19, 1, 1, TB)
        return jnp.concatenate([low_edge, middle, high_edge], axis=2)

    extended = jnp.concatenate([a_slab(-1), extended, a_slab(1)], axis=3)
    corner = jnp.broadcast_to(fill_vec.reshape(1, 19, 1, 1, 1), (count, 19, 1, 1, 1))

    def b_slab(side):
        middle = face_slab(2, side, (TL, TA, 1))
        side_low = edge_line(1, -1, 2, side).reshape(count, 19, TL, 1, 1)
        side_high = edge_line(1, 1, 2, side).reshape(count, 19, TL, 1, 1)
        middle = jnp.concatenate([side_low, middle, side_high], axis=3)
        row_low = edge_line(0, -1, 2, side).reshape(count, 19, 1, TA, 1)
        row_high = edge_line(0, 1, 2, side).reshape(count, 19, 1, TA, 1)
        row_low = jnp.concatenate([corner, row_low, corner], axis=3)
        row_high = jnp.concatenate([corner, row_high, corner], axis=3)
        return jnp.concatenate([row_low, middle, row_high], axis=2)

    extended = jnp.concatenate([b_slab(-1), extended, b_slab(1)], axis=4)
    parts = []
    for i in range(19):
        move_l, move_a, move_b = [sign * int(VELOCITY[i, d]) for d in range(3)]
        piece = extended[
            :,
            i,
            1 - move_l : 1 - move_l + TL,
            1 - move_a : 1 - move_a + TA,
            1 - move_b : 1 - move_b + TB,
        ]
        parts.append(piece.reshape(count, TL, TA * TB))
    return jnp.stack(parts, axis=1)


def body(pops_start, tile_pos, wall_mask, wall_frac, patch_id, probe):
    count = pops_start.shape[0]
    n_cross = lax.axis_size("yz")
    own_pos = lax.dynamic_slice_in_dim(
        tile_pos, (lax.axis_index("gx") * n_cross + lax.axis_index("yz")) * count, count
    )
    alive = own_pos >= 0
    mask_float = wall_mask.astype(jnp.float32)
    solid = mask_float * wall_frac
    zeros_list = [0.0] * 19

    def collide_all(field, solid_part):
        return jax.vmap(collide)(field, solid_part)

    states = [pops_start]
    current = pops_start
    for k in range(STEPS):
        current = stream(collide_all(current, solid), 1, WEIGHTS, tile_pos)
        states.append(current)
    vel_l = jnp.asarray(VELOCITY[:, 0], jnp.float32)
    adjoint = probe[:, None] * vel_l[None, :, None, None]
    sens = jnp.zeros_like(solid)
    for k in reversed(range(STEPS)):
        state = states[k]
        pulled = stream(adjoint, -1, zeros_list, tile_pos)
        _, backward = jax.vjp(collide_all, state, solid)
        adjoint, dsolid = backward(pulled)
        sens = sens + dsolid
    pops_final = jnp.where(alive[:, None, None, None], current, 0.0)
    adjoint_start = jnp.where(alive[:, None, None, None], adjoint, 0.0)
    weighted = jnp.where(alive[:, None, None], mask_float * sens, 0.0)
    total_patches = PATCH_DEV * lax.axis_size("gx") * n_cross
    partial_sums = jax.ops.segment_sum(
        weighted.reshape(-1), patch_id.reshape(-1), num_segments=total_patches
    )
    patch_sens = lax.psum_scatter(partial_sums, ("gx", "yz"), scatter_dimension=0, tiled=True)
    return (pops_final, adjoint_start, patch_sens)


def solution(mesh):
    in_specs = (
        P(("gx", "yz"), None, None, None),
        P(),
        P(("gx", "yz"), None, None),
        P(("gx", "yz"), None, None),
        P(("gx", "yz"), None, None),
        P(("gx", "yz"), None, None),
    )
    out_specs = (
        P(("gx", "yz"), None, None, None),
        P(("gx", "yz"), None, None, None),
        P(("gx", "yz")),
    )
    return jax.shard_map(body, mesh=mesh, in_specs=in_specs, out_specs=out_specs, check_vma=False)
```

profile of v0, /device:TPU:0, one launch (start us, length us, event | category | flops | bytes accessed | tf_op | source)
XLA Modules:
  0.0 1166.9 jit_solution(3217125510009957358)
XLA Ops:
  5.8 6.7 all_gather.42
  21.8 5.6 all_gather.36
  30.1 5.7 collective-permute-start.5
  52.5 5.5 all_gather.43
  58.5 5.8 all_gather.37
  68.5 9.1 fusion.324
  91.5 9.1 fusion.329
  107.6 5.4 copy.7025
  161.7 5.3 all_gather.44
  173.6 5.3 all_gather.38
  212.9 5.3 copy.7965
  356.8 18.0 %fusion.14 = f32[2,19,18,18,33]{4,3,2,1,0:T(8,128)S(1)} fusion(f32[2,19,1,1,1]{4,3,2,1,0:T(1,128)S(1)} %broadcast_in_dim.1342, f32[2,19,1,16,1]{4,3,2,1,0:T(8,128)} %copy.7072, f32[2,19,16,1,1]{4,3,2,1,0:T(1,128)} %copy.7068, f32[2,19,16,16,1]{4,3,2,1,0:T(8,128)} %constant_dynamic-update-slice_fusion.125, f32[2,19,16,1,1]{4,3,2,1,0:T(1,128)} %copy.7067, ...), kind=kLoop, calls=%fused_computation.47 | loop fusion | flops 6907032 | bytes 3249912 | tf_op jit(solution)/shard_map/concatenate | solution.py:225
  376.8 17.3 %fusion.20 = f32[2,19,18,18,33]{4,3,2,1,0:T(8,128)S(1)} fusion(f32[2,19,1,1,1]{4,3,2,1,0:T(1,128)S(1)} %broadcast_in_dim.1342, f32[2,19,1,1,32]{4,3,2,1,0:T(1,128)S(1)} %copy-done.75, f32[2,19,16,1,32]{4,3,2,1,0:T(1,128)S(1)} %copy-done.14, f32[2,19,1,1,32]{4,3,2,1,0:T(1,128)S(1)} %copy-done.78, ...), kind=kLoop, calls=%fused_computation.53 | loop fusion | flops 6907032 | bytes 3249912 | tf_op jit(solution)/shard_map/concatenate | solution.py:225
  440.2 18.1 %fusion.8 = f32[2,19,18,18,33]{4,3,2,1,0:T(8,128)S(1)} fusion(f32[2,19,1,1,1]{4,3,2,1,0:T(1,128)S(1)} %broadcast_in_dim.1359, f32[2,19,1,16,1]{4,3,2,1,0:T(8,128)} %copy.7273, f32[2,19,16,1,1]{4,3,2,1,0:T(1,128)} %copy.7268, f32[2,19,16,16,1]{4,3,2,1,0:T(8,128)} %constant_dynamic-update-slice_fusion.407, f32[2,19,16,1,1]{4,3,2,1,0:T(1,128)} %copy.7267, ...), kind=kLoop, calls=%fused_computation.41 | loop fusion | flops 6907032 | bytes 3249912 | tf_op jit(solution)/shard_map/concatenate | solution.py:225
  470.4 17.2 %fusion.2 = f32[2,19,18,18,33]{4,3,2,1,0:T(8,128)S(1)} fusion(f32[2,19,1,1,1]{4,3,2,1,0:T(1,128)S(1)} %broadcast_in_dim.1359, f32[2,19,1,1,32]{4,3,2,1,0:T(1,128)S(1)} %copy.7230, f32[2,19,16,1,32]{4,3,2,1,0:T(1,128)} %copy-done.35, f32[2,19,1,1,32]{4,3,2,1,0:T(1,128)} %copy-done.100, f32[2,19,1,16,32]{4,3,2,1,0:T(8,128)S(1)} %copy-done.8, ...), kind=kLoop, calls=%fused_computation.35 | loop fusion | flops 6907032 | bytes 3249912 | tf_op jit(solution)/shard_map/concatenate | solution.py:225
  618.6 6.2 fusion.31
  628.0 5.5 all_gather.46
  635.5 5.5 all_gather.40
  642.0 9.2 fusion.322
  664.3 9.2 fusion.326
  700.3 5.5 all_gather.45
  711.8 5.5 all_gather.39
  720.0 5.2 collective-permute-start.7
  725.9 5.2 collective-permute-start.2
  746.4 5.3 all_gather.47
  755.2 5.3 all_gather.41
  859.0 17.2 %fusion.23 = f32[2,19,18,18,33]{4,3,2,1,0:T(8,128)S(1)} fusion(f32[2,19,1,1,1]{4,3,2,1,0:T(1,128)S(1)} %copy-done.97, f32[2,19,1,1,32]{4,3,2,1,0:T(1,128)S(1)} %copy.7130, f32[2,19,16,1,32]{4,3,2,1,0:T(1,128)S(1)} %constant_dynamic-update-slice_fusion.269, f32[2,19,1,1,32]{4,3,2,1,0:T(1,128)S(1)} %copy.7129, ...), kind=kLoop, calls=%fused_computation.56 | loop fusion | flops 6907032 | bytes 3249912 | tf_op jit(solution)/shard_map/concatenate | solution.py:225
  881.8 17.4 %fusion.17 = f32[2,19,18,18,33]{4,3,2,1,0:T(8,128)S(1)} fusion(f32[2,19,1,1,1]{4,3,2,1,0:T(1,128)S(1)} %copy-done.97, f32[2,19,1,16,1]{4,3,2,1,0:T(8,128)S(1)} %copy.7185, f32[2,19,16,1,1]{4,3,2,1,0:T(1,128)S(1)} %copy-done.46, f32[2,19,16,16,1]{4,3,2,1,0:T(8,128)} %constant_dynamic-update-slice_fusion.300, f32[2,19,16,1,1]{4,3,2,1,0:T(1,128)} %copy.7180, ...), kind=kLoop, calls=%fused_computation.50 | loop fusion | flops 6907032 | bytes 3249912 | tf_op jit(solution)/shard_map/concatenate | solution.py:225
  962.7 17.8 %fusion.11 = f32[2,19,18,18,33]{4,3,2,1,0:T(8,128)S(1)} fusion(f32[2,19,1,1,1]{4,3,2,1,0:T(1,128)S(1)} %copy-done.95, f32[2,19,1,16,1]{4,3,2,1,0:T(8,128)} %copy.7387, f32[2,19,16,1,1]{4,3,2,1,0:T(1,128)S(1)} %copy-done.44, f32[2,19,16,16,1]{4,3,2,1,0:T(8,128)} %constant_dynamic-update-slice_fusion.524, f32[2,19,16,1,1]{4,3,2,1,0:T(1,128)} %copy.7381, ...), kind=kLoop, calls=%fused_computation.44 | loop fusion | flops 6907032 | bytes 3249912 | tf_op jit(solution)/shard_map/concatenate | solution.py:225
  984.4 17.1 %fusion.5 = f32[2,19,18,18,33]{4,3,2,1,0:T(8,128)S(1)} fusion(f32[2,19,1,1,1]{4,3,2,1,0:T(1,128)S(1)} %copy-done.95, f32[2,19,1,1,32]{4,3,2,1,0:T(1,128)S(1)} %copy.7344, f32[2,19,16,1,32]{4,3,2,1,0:T(1,128)S(1)} %copy-done.33, f32[2,19,1,1,32]{4,3,2,1,0:T(1,128)S(1)} %copy-done.99, f32[2,19,1,16,32]{4,3,2,1,0:T(8,128)S(1)} %constant_dynamic-update-slice_fusion.458, ...), kind=kLoop, calls=%fused_computation.38 | loop fusion | flops 6907032 | bytes 3249912 | tf_op jit(solution)/shard_map/concatenate | solution.py:225
  1038.6 86.8 %scatter_custom_fusion = f32[2048]{0:T(1024)S(1)} fusion(s32[16384]{0:T(1024)} %bitcast.1059, f32[16384]{0:T(1024)S(1)} %bitcast.1060, f32[]{:T(128)} %constant.67.clone), kind=kCustom, calls=%fused_computation.1151 | custom fusion | flops 16384 | bytes 8704 | tf_op jit(solution)/shard_map/scatter-add | solution.py:272
  1125.4 40.7 %all-reduce.36 = f32[2048]{0:T(1024)S(1)} all-reduce(f32[2048]{0:T(1024)S(1)} %scatter_custom_fusion), channel_id=2, replica_groups=mesh['gx'=8,'yz'=4] {'gx','yz'}, use_global_device_ids=true, to_apply=%region_46.47.clone | all-reduce | flops 2048 | bytes 16384
  (1723 shorter events, 757.0 us)
Async XLA Ops:
  13.3 264.8 %collective-permute-start.4 = (f32[8,1,5,512]{3,0,2,1:T(8,128)}, f32[8,1,5,512]{3,0,2,1:T(8,128)}, u32[]{:S(2)}, u32[]{:S(2)}) collective-permute-start(f32[8,1,5,512]{3,0,2,1:T(8,128)} %copy.7481), channel_id=1, source_target_pairs={{4,0},{8,4},{12,8},{16,12},{20,16},{24,20},{28,24},{5,1},{9,5},{13... | collective-permute-start | bytes 245768 | tf_op jit(solution)/shard_map/ppermute | solution.py:50
  20.3 44.2 %copy-start.187 = (s32[64]{0:T(128)S(1)}, s32[64]{0:T(128)}, u32[]{:S(2)}) copy-start(s32[64]{0:T(128)} %param.28) | copy-start | bytes 772
  28.2 251.7 %collective-permute-start.1 = (f32[8,1,5,512]{3,0,2,1:T(8,128)}, f32[8,1,5,512]{3,0,2,1:T(8,128)}, u32[]{:S(2)}, u32[]{:S(2)}) collective-permute-start(f32[8,1,5,512]{3,0,2,1:T(8,128)} %copy.7446), channel_id=1, source_target_pairs={{4,0},{8,4},{12,8},{16,12},{20,16},{24,20},{28,24},{5,1},{9,5},{13... | collective-permute-start | bytes 245768 | tf_op jit(solution)/shard_map/ppermute | solution.py:50
  30.1 251.5 %collective-permute-start.5 = (f32[8,1,5,512]{3,0,2,1:T(8,128)}, f32[8,1,5,512]{3,0,2,1:T(8,128)}, u32[]{:S(2)}, u32[]{:S(2)}) collective-permute-start(f32[8,1,5,512]{3,0,2,1:T(8,128)} %copy.7482), channel_id=1, source_target_pairs={{0,4},{4,8},{8,12},{12,16},{16,20},{20,24},{24,28},{1,5},{5,9},{9,... | collective-permute-start | bytes 245768 | tf_op jit(solution)/shard_map/ppermute | solution.py:49
  36.4 250.8 %collective-permute-start = (f32[8,1,5,512]{3,0,2,1:T(8,128)}, f32[8,1,5,512]{3,0,2,1:T(8,128)}, u32[]{:S(2)}, u32[]{:S(2)}) collective-permute-start(f32[8,1,5,512]{3,0,2,1:T(8,128)} %copy.7445), channel_id=1, source_target_pairs={{0,4},{4,8},{8,12},{12,16},{16,20},{20,24},{24,28},{1,5},{5,9},{9,... | collective-permute-start | bytes 245768 | tf_op jit(solution)/shard_map/ppermute | solution.py:49
  66.3 74.0 %copy-start.176 = (pred[2,8]{1,0:T(4,128)(4,1)}, pred[2,8]{1,0:T(4,128)(4,1)S(1)}, u32[]{:S(2)}) copy-start(pred[2,8]{1,0:T(4,128)(4,1)S(1)} %get-tuple-element.596) | copy-start | bytes 52
  220.4 33.7 %copy-start.42 = (f32[2,8,16]{1,2,0:T(8,128)}, f32[2,8,16]{1,2,0:T(8,128)S(1)}, u32[]{:S(2)}) copy-start(f32[2,8,16]{1,2,0:T(8,128)S(1)} %broadcast.2169) | copy-start | bytes 3076
  299.5 33.7 %copy-start.153 = (f32[2,19,32]{2,0,1:T(2,128)S(1)}, f32[2,19,32]{2,0,1:T(2,128)}, u32[]{:S(2)}) copy-start(f32[2,19,32]{2,0,1:T(2,128)} %constant_dynamic-update-slice_fusion.82) | copy-start | bytes 14596
  299.5 33.7 %copy-start.207 = (pred[2]{0:T(512)(128)(4,1)S(1)}, pred[2]{0:T(512)(128)(4,1)}, u32[]{:S(2)}) copy-start(pred[2]{0:T(512)(128)(4,1)} %get-tuple-element.593) | copy-start | bytes 10
  299.5 34.4 %copy-start.155 = (f32[2,19,32]{2,0,1:T(2,128)S(1)}, f32[2,19,32]{2,0,1:T(2,128)}, u32[]{:S(2)}) copy-start(f32[2,19,32]{2,0,1:T(2,128)} %constant_dynamic-update-slice_fusion.59) | copy-start | bytes 14596
  299.5 34.4 %copy-start.206 = (pred[2]{0:T(512)(128)(4,1)S(1)}, pred[2]{0:T(512)(128)(4,1)}, u32[]{:S(2)}) copy-start(pred[2]{0:T(512)(128)(4,1)} %get-tuple-element.577) | copy-start | bytes 10
  299.5 35.0 %copy-start.10 = (f32[2,19,16,1,32]{4,3,2,1,0:T(1,128)S(1)}, f32[2,19,16,1,32]{4,3,2,1,0:T(1,128)}, u32[]{:S(2)}) copy-start(f32[2,19,16,1,32]{4,3,2,1,0:T(1,128)} %copy-done.9) | copy-start | bytes 233476
  343.3 33.4 %slice-start.2 = ((s8[4980736]{0:T(1024)(128)(4,1)}), s8[786432]{0:T(1024)(128)(4,1)S(1)}, s32[]{:S(2)}) async-start(s8[4980736]{0:T(1024)(128)(4,1)} %bitcast.963), calls=%async_computation.2 | async-start | bytes 1572864
  684.8 51.6 %copy-start.34 = (f32[2,19,16,1,32]{4,3,2,1,0:T(1,128)S(1)}, f32[2,19,16,1,32]{4,3,2,1,0:T(1,128)}, u32[]{:S(2)}) copy-start(f32[2,19,16,1,32]{4,3,2,1,0:T(1,128)} %constant_dynamic-update-slice_fusion.253) | copy-start | bytes 233476
  684.8 53.0 %copy-start.177 = (pred[2,8]{1,0:T(4,128)(4,1)S(1)}, pred[2,8]{1,0:T(4,128)(4,1)}, u32[]{:S(2)}) copy-start(pred[2,8]{1,0:T(4,128)(4,1)} %copy-done.176) | copy-start | bytes 52
  684.8 56.1 %copy-start.30 = (f32[2,19,16,1,32]{4,3,2,1,0:T(1,128)S(1)}, f32[2,19,16,1,32]{4,3,2,1,0:T(1,128)}, u32[]{:S(2)}) copy-start(f32[2,19,16,1,32]{4,3,2,1,0:T(1,128)} %constant_dynamic-update-slice_fusion.279) | copy-start | bytes 233476
  684.8 56.4 %copy-start.162 = (f32[2,1,512]{2,0,1:T(2,128)S(1)}, f32[2,1,512]{2,0,1:T(2,128)}, u32[]{:S(2)}) copy-start(f32[2,1,512]{2,0,1:T(2,128)} %fusion.88) | copy-start | bytes 12292
  685.8 57.2 %copy-start.43 = (f32[2,8,16]{1,2,0:T(8,128)S(1)}, f32[2,8,16]{1,2,0:T(8,128)}, u32[]{:S(2)}) copy-start(f32[2,8,16]{1,2,0:T(8,128)} %copy-done.42) | copy-start | bytes 3076
  686.7 56.8 %copy-start.73 = (f32[2,1,16,16]{1,3,2,0:T(8,128)S(1)}, f32[2,1,16,16]{1,3,2,0:T(8,128)}, u32[]{:S(2)}) copy-start(f32[2,1,16,16]{1,3,2,0:T(8,128)} %slice.2345) | copy-start | bytes 6148
  706.6 120.1 %collective-permute-start.6 = (f32[8,1,5,512]{3,0,2,1:T(8,128)}, f32[8,1,5,512]{3,0,2,1:T(8,128)S(1)}, u32[]{:S(2)}, u32[]{:S(2)}) collective-permute-start(f32[8,1,5,512]{3,0,2,1:T(8,128)} %copy.7499), channel_id=1, source_target_pairs={{4,0},{8,4},{12,8},{16,12},{20,16},{24,20},{28,24},{5,1},{9,5},{13... | collective-permute-start | bytes 245768 | tf_op jit(solution)/shard_map/ppermute | solution.py:50
  717.4 34.5 %copy-start.175 = (pred[2,8]{1,0:T(4,128)(4,1)S(1)}, pred[2,8]{1,0:T(4,128)(4,1)}, u32[]{:S(2)}) copy-start(pred[2,8]{1,0:T(4,128)(4,1)} %get-tuple-element.590) | copy-start | bytes 52
  718.1 109.0 %collective-permute-start.3 = (f32[8,1,5,512]{3,0,2,1:T(8,128)}, f32[8,1,5,512]{3,0,2,1:T(8,128)S(1)}, u32[]{:S(2)}, u32[]{:S(2)}) collective-permute-start(f32[8,1,5,512]{3,0,2,1:T(8,128)} %copy.7464), channel_id=1, source_target_pairs={{4,0},{8,4},{12,8},{16,12},{20,16},{24,20},{28,24},{5,1},{9,5},{13... | collective-permute-start | bytes 245768 | tf_op jit(solution)/shard_map/ppermute | solution.py:50
  720.0 111.7 %collective-permute-start.7 = (f32[8,1,5,512]{3,0,2,1:T(8,128)}, f32[8,1,5,512]{3,0,2,1:T(8,128)S(1)}, u32[]{:S(2)}, u32[]{:S(2)}) collective-permute-start(f32[8,1,5,512]{3,0,2,1:T(8,128)} %copy.7500), channel_id=1, source_target_pairs={{0,4},{4,8},{8,12},{12,16},{16,20},{20,24},{24,28},{1,5},{5,9},{9,... | collective-permute-start | bytes 245768 | tf_op jit(solution)/shard_map/ppermute | solution.py:49
  725.9 106.4 %collective-permute-start.2 = (f32[8,1,5,512]{3,0,2,1:T(8,128)}, f32[8,1,5,512]{3,0,2,1:T(8,128)S(1)}, u32[]{:S(2)}, u32[]{:S(2)}) collective-permute-start(f32[8,1,5,512]{3,0,2,1:T(8,128)} %copy.7463), channel_id=1, source_target_pairs={{0,4},{4,8},{8,12},{12,16},{16,20},{20,24},{24,28},{1,5},{5,9},{9,... | collective-permute-start | bytes 245768 | tf_op jit(solution)/shard_map/ppermute | solution.py:49
  826.6 123.7 %copy-start.32 = (f32[2,19,16,1,32]{4,3,2,1,0:T(1,128)}, f32[2,19,16,1,32]{4,3,2,1,0:T(1,128)S(1)}, u32[]{:S(2)}) copy-start(f32[2,19,16,1,32]{4,3,2,1,0:T(1,128)S(1)} %constant_dynamic-update-slice_fusion.488) | copy-start | bytes 233476
  899.3 36.4 %copy-start.189 = (pred[2]{0:T(512)(128)(4,1)S(1)}, pred[2]{0:T(512)(128)(4,1)}, u32[]{:S(2)}) copy-start(pred[2]{0:T(512)(128)(4,1)} %copy-done.188) | copy-start | bytes 10
  899.3 50.1 %slice-start.4 = ((s8[4980736]{0:T(1024)(128)(4,1)}), s8[786432]{0:T(1024)(128)(4,1)S(1)}, s32[]{:S(2)}) async-start(s8[4980736]{0:T(1024)(128)(4,1)} %bitcast.965), calls=%async_computation.4 | async-start | bytes 1572864
  908.2 32.6 %copy-start.7 = (f32[2,19,1,16,32]{4,3,2,1,0:T(8,128)S(1)}, f32[2,19,1,16,32]{4,3,2,1,0:T(8,128)}, u32[]{:S(2)}) copy-start(f32[2,19,1,16,32]{4,3,2,1,0:T(8,128)} %constant_dynamic-update-slice_fusion.470) | copy-start | bytes 233476
  910.0 34.5 %copy-start.114 = (f32[2,8,32]{2,0,1:T(2,128)S(1)}, f32[2,8,32]{2,0,1:T(2,128)}, u32[]{:S(2)}) copy-start(f32[2,8,32]{2,0,1:T(2,128)} %copy-done.113) | copy-start | bytes 6148
  910.0 34.5 %copy-start.157 = (f32[2,2,32]{2,0,1:T(2,128)S(1)}, f32[2,2,32]{2,0,1:T(2,128)}, u32[]{:S(2)}) copy-start(f32[2,2,32]{2,0,1:T(2,128)} %copy-done.156) | copy-start | bytes 1540
  911.7 34.1 %copy-start.6 = (f32[2,19,1,16,32]{4,3,2,1,0:T(8,128)S(1)}, f32[2,19,1,16,32]{4,3,2,1,0:T(8,128)}, u32[]{:S(2)}) copy-start(f32[2,19,1,16,32]{4,3,2,1,0:T(8,128)} %constant_dynamic-update-slice_fusion.482) | copy-start | bytes 233476
  1001.5 31.4 %copy-start.5 = (f32[2,19,16,512]{3,2,1,0:T(8,128)S(1)}, f32[2,19,16,512]{3,2,1,0:T(8,128)}, u32[]{:S(2)}) copy-start(f32[2,19,16,512]{3,2,1,0:T(8,128)} %param.27) | copy-start | bytes 3735556
  (206 other events, 3321.2 us)
where the time goes:
time: 1180 us; the launch traced here: 1170 us
  local copies, waits for them, and re-layouts  642 us (54%)
  other arithmetic  334 us (28%)
  blocking collectives  108 us (9%)
  matrix products  51.6 us (4%)
  starting transfers between devices  26 us (2%)
    unnamed x1005, local copies, waits for them, and re-layouts  276 us
    concatenate x8, other arithmetic, stream(): extended = jnp.concatenate([b_slab(-1), extended, b_slab(1)], axis=4)  140 us
    scatter-add x1, other arithmetic, body(): jax.ops.segment_sum(weighted.reshape(-1), patch_id.reshape(-1), num_segme...  86.8 us
    another operation x62, local copies, waits for them, and re-layouts, stream(): return jnp.stack(parts, axis=1)  80.4 us
    slice x8, local copies, waits for them, and re-layouts, faces(): cube[:, :, :, :, 0]  57.1 us
    unnamed x1, blocking collectives  40.7 us
    slice x48, matrix products, edge_line(): value = picked[:, members.index(target)]  31.3 us
    reduce_sum x22, local copies, waits for them, and re-layouts, collide(): density = jnp.sum(field, axis=0)  24.5 us
  transfers between devices with their start and end apart: 8, of which 0 were waited for; matrix products, arithmetic and copies ran while one was open for 28% of the time, Pallas kernels for 0%

commit v1 on v0

v1 whole, which is shorter than its diff:
```python
import functools

import jax
import jax.numpy as jnp
import numpy as np
from jax import lax
from jax.experimental import pallas as pl
from jax.experimental.pallas import tpu as pltpu
from jax.sharding import PartitionSpec as P

TL = 16
TA = 16
TB = 32
CELLS = TA * TB
LANES = 128
COLS = CELLS // LANES
OMEGA = 1.25

VELOCITY = np.array(
    [
        [0, 0, 0],
        [1, 0, 0],
        [-1, 0, 0],
        [0, 1, 0],
        [0, -1, 0],
        [0, 0, 1],
        [0, 0, -1],
        [1, 1, 0],
        [-1, -1, 0],
        [1, -1, 0],
        [-1, 1, 0],
        [1, 0, 1],
        [-1, 0, -1],
        [1, 0, -1],
        [-1, 0, 1],
        [0, 1, 1],
        [0, -1, -1],
        [0, 1, -1],
        [0, -1, 1],
    ]
)
Q = 19
WEIGHTS = [1.0 / 3.0] + [1.0 / 18.0] * 6 + [1.0 / 36.0] * 12
PAIRS = [(2 * k + 1, 2 * k + 2) for k in range(9)]
AXIAL = [i for i in range(Q) if VELOCITY[i, 0] != 0]


def vel(i):
    return tuple(int(v) for v in VELOCITY[i])


def members_of(dim, value):
    return [i for i in range(Q) if vel(i)[dim] == value]


def face_list(stage, dim, side):
    if stage == 1:
        return [("post", i) for i in members_of(dim, side)] + [("probe", 0)]
    return [("post", i) for i in members_of(dim, side)] + [
        ("adj", i) for i in members_of(dim, -side)
    ]


class Pack:
    def __init__(self, stage):
        self.n = len(face_list(stage, 0, 1))
        self.lists = {
            (d, s): face_list(stage, d, s) for d in range(3) for s in (-1, 1)
        }
        self.fold = 2 if 2 * self.n <= TB // 2 else 1
        self.a_cols = -(-2 * self.n * TB // LANES)
        self.b_cols = COLS // self.fold
        self.a_row = 0
        self.b_row = TL * self.a_cols
        self.ab_rows = self.b_row + TL * self.b_cols
        self.l_rows = self.n * COLS
        self.up_row = self.ab_rows
        self.dn_row = self.up_row + self.l_rows
        self.rows = self.dn_row + self.l_rows

    def slot(self, dim, side, key):
        j = self.lists[(dim, side)].index(key)
        return j if dim == 0 or side < 0 else j + self.n


PACK1 = Pack(1)
PACK2 = Pack(2)


def lane_roll(x, shift):
    shift = shift % x.shape[-1]
    return x if shift == 0 else pltpu.roll(x, shift, axis=x.ndim - 1)


def row_roll(x, shift):
    shift = shift % x.shape[0]
    return x if shift == 0 else pltpu.roll(x, shift, axis=0)


def lane_iota(shape):
    return lax.broadcasted_iota(jnp.int32, shape, len(shape) - 1)


def row_iota(shape):
    return lax.broadcasted_iota(jnp.int32, shape, 0)


def combine(c, parts):
    total = None
    for v, p in zip(c, parts):
        if v == 0:
            continue
        if total is None:
            total = p if v > 0 else -p
        else:
            total = total + p if v > 0 else total - p
    return total


def flow(f):
    rho = f[0]
    momentum = [None, None, None]
    for i, j in PAIRS:
        rho = rho + (f[i] + f[j])
        diff = f[i] - f[j]
        for d, v in enumerate(vel(i)):
            if v == 0:
                continue
            if momentum[d] is None:
                momentum[d] = diff if v > 0 else -diff
            else:
                momentum[d] = momentum[d] + diff if v > 0 else momentum[d] - diff
    inv = 1.0 / rho
    u = [m * inv for m in momentum]
    square = u[0] * u[0] + u[1] * u[1] + u[2] * u[2]
    return rho, u, 1.0 - 1.5 * square


def collide(f, solid, rho, u, base):
    fluid = 1.0 - solid
    keep = (1.0 - OMEGA) * fluid
    scale = OMEGA * fluid * rho
    out = [None] * Q
    out[0] = (keep + solid) * f[0] + WEIGHTS[0] * scale * base
    for i, j in PAIRS:
        along = combine(vel(i), u)
        ws = WEIGHTS[i] * scale
        even = ws * (base + 4.5 * along * along)
        odd = ws * (3.0 * along)
        out[i] = keep * f[i] + solid * f[j] + (even + odd)
        out[j] = keep * f[j] + solid * f[i] + (even - odd)
    return out


def pullback(f, solid, rho, u, base, g):
    fluid = 1.0 - solid
    keep = (1.0 - OMEGA) * fluid
    gain = OMEGA * fluid
    lin = [None, None, None]
    total = None
    dens = None
    cross = None

    def plus(a, b):
        return b if a is None else a + b

    if g[0] is not None:
        e = WEIGHTS[0] * g[0]
        total = e
        dens = e * base
        cross = OMEGA * (g[0] * f[0])
    for i, j in PAIRS:
        if g[i] is None:
            continue
        along = combine(vel(i), u)
        w = WEIGHTS[i]
        even = w * (g[i] + g[j])
        odd = w * (g[i] - g[j])
        total = plus(total, even)
        dens = plus(dens, even * (base + 4.5 * along * along) + 3.0 * along * odd)
        push = 3.0 * odd + 9.0 * along * even
        for d, v in enumerate(vel(i)):
            if v:
                lin[d] = plus(lin[d], push if v > 0 else -push)
        cross = plus(
            cross,
            g[i] * (f[j] - (1.0 - OMEGA) * f[i]) + g[j] * (f[i] - (1.0 - OMEGA) * f[j]),
        )
    lin = [
        (-3.0 * u[d] * total if lin[d] is None else lin[d] - 3.0 * u[d] * total)
        for d in range(3)
    ]
    dsolid = cross - OMEGA * rho * dens
    shared = gain * (dens - (lin[0] * u[0] + lin[1] * u[1] + lin[2] * u[2]))
    lin = [gain * v for v in lin]
    out = [None] * Q
    out[0] = shared if g[0] is None else (keep + solid) * g[0] + shared
    for i, j in PAIRS:
        slope = combine(vel(i), lin)
        if g[i] is None:
            out[i] = shared + slope
            out[j] = shared - slope
        else:
            out[i] = keep * g[i] + solid * g[j] + (shared + slope)
            out[j] = keep * g[j] + solid * g[i] + (shared - slope)
    return out, dsolid


def load_chunk(ref, t, i, r, c):
    return ref[t, i, pl.ds(8 * r, 8), pl.ds(c, LANES)]


def for_chunks(count, run):
    def step(k, carry):
        t = k // (2 * COLS)
        r = (k // COLS) % 2
        c = pl.multiple_of((k % COLS) * LANES, LANES)
        run(t, pl.multiple_of(r * 8, 8), c)
        return carry

    lax.fori_loop(0, count * 2 * COLS, step, 0)


def chunk(ref, t, i, r, c):
    return ref[t, i, pl.ds(r, 8), pl.ds(c, LANES)]


def plane_chunk(ref, t, r, c):
    return ref[t, pl.ds(r, 8), pl.ds(c, LANES)]


def write_faces(pack, t, get, ab_ref, up_ref, dn_ref):
    lane = lane_iota((TL, LANES))
    for col in range(pack.a_cols):
        acc = jnp.zeros((TL, LANES), jnp.float32)
        for side in (-1, 1):
            for key in pack.lists[(1, side)]:
                j = pack.slot(1, side, key)
                if j // 4 != col:
                    continue
                to = TB * (j % 4)
                if side < 0:
                    part = lane_roll(get(key, slice(None), slice(0, LANES)), to)
                else:
                    part = lane_roll(
                        get(key, slice(None), slice(CELLS - LANES, CELLS)),
                        to - (LANES - TB),
                    )
                acc = jnp.where(lane // TB == j % 4, part, acc)
        ab_ref[t, pack.a_row + TL * col : pack.a_row + TL * (col + 1), :] = acc
    for col in range(pack.b_cols):
        acc = jnp.zeros((TL, LANES), jnp.float32)
        for half in range(pack.fold):
            src = col + half * pack.b_cols
            for side in (-1, 1):
                for key in pack.lists[(2, side)]:
                    j = pack.slot(2, side, key) + half * (TB // 2)
                    part = get(key, slice(None), slice(LANES * src, LANES * (src + 1)))
                    part = lane_roll(part, j if side < 0 else j - (TB - 1))
                    acc = jnp.where(lane % TB == j, part, acc)
        ab_ref[t, pack.b_row + TL * col : pack.b_row + TL * (col + 1), :] = acc
    for side, ref in ((1, up_ref), (-1, dn_ref)):
        row = TL - 1 if side > 0 else 0
        for key in pack.lists[(0, side)]:
            j = pack.slot(0, side, key)
            for col in range(COLS):
                ref[t, j * COLS + col : j * COLS + col + 1, :] = get(
                    key, slice(row, row + 1), slice(LANES * col, LANES * (col + 1))
                )


def build_inverse(pos_ref, inv_ref, n_layers, group):
    layer = lax.axis_index("gx")
    for off in (-1, 0, 1):
        for w in range(group + 1):
            inv_ref[off + 1, w] = -1
        target = layer + off
        valid = (target >= 0) & (target < n_layers)
        first = jnp.clip(target, 0, n_layers - 1) * group
        for s in range(group):
            p = pos_ref[first + s]
            inv_ref[off + 1, jnp.where(valid & (p >= 0), p, group)] = s


class Neighbours:
    def __init__(self, pack, t, faces_ref, pos_ref, inv_ref, n_cross, count):
        self.pack = pack
        self.ref = faces_ref
        group = n_cross * count
        own = pos_ref[lax.axis_index("gx") * group + lax.axis_index("yz") * count + t]
        p = jnp.maximum(own, 0)
        a, b = p // count, p % count
        self.alive = own >= 0
        self.where = {}
        for d in [vel(i) for i in range(1, Q)]:
            ta, tb = a + d[1], b + d[2]
            ok = (ta >= 0) & (ta < n_cross) & (tb >= 0) & (tb < count)
            s = inv_ref[d[0] + 1, jnp.where(ok, ta * count + tb, group)]
            found = ok & (s >= 0)
            self.where[d] = (jnp.where(found, s, 0), found)
        self.planes = {}

    def a_face(self, d, side, key, fill):
        k, found = self.where[d]
        j = self.pack.slot(1, side, key)
        row = self.pack.a_row + TL * (j // 4)
        face = self.ref[k, row : row + TL, :]
        face = lane_roll(face, (LANES - TB if side > 0 else 0) - TB * (j % 4))
        return jnp.where(found, face, fill)

    def b_plane(self, d):
        if d not in self.planes:
            k, found = self.where[d]
            row = self.pack.b_row
            half = jnp.concatenate(
                [
                    self.ref[k, row + TL * c : row + TL * (c + 1), :]
                    for c in range(self.pack.b_cols)
                ],
                axis=1,
            )
            if self.pack.fold == 2:
                half = jnp.concatenate([half, lane_roll(half, -(TB // 2))], axis=1)
            self.planes[d] = half
        return self.planes[d], self.where[d][1]

    def l_row(self, d, side, key, fill):
        k, found = self.where[d]
        first = self.pack.up_row if side > 0 else self.pack.dn_row
        first = first + self.pack.slot(0, side, key) * COLS
        row = jnp.concatenate(
            [self.ref[k, first + c : first + c + 1, :] for c in range(COLS)], axis=1
        )
        return jnp.where(found, row, fill)

    def stream(self, own, c, key, fill):
        cl, ca, cb = c
        shape = (TL, CELLS)
        lane = lane_iota(shape)
        edge_b = lane % TB == (TB - 1 if cb > 0 else 0)
        edge_a = lane // TB == (TA - 1 if ca > 0 else 0)
        x = own
        if ca:
            face = self.a_face((0, -ca, 0), ca, key, fill)
            part = slice(CELLS - LANES, CELLS) if ca > 0 else slice(0, LANES)
            inner = lane_iota((TL, LANES))
            hit = inner >= LANES - TB if ca > 0 else inner < TB
            face = jnp.where(hit, face, x[:, part])
            x = jnp.concatenate(
                [x[:, : CELLS - LANES], face] if ca > 0 else [face, x[:, LANES:]], axis=1
            )
        if cb:
            j = self.pack.slot(2, cb, key)
            shift = -1 - j if cb > 0 else TB - j
            plane, found = self.b_plane((0, 0, -cb))
            face = jnp.where(found, lane_roll(plane, shift), fill)
            if ca:
                plane, found = self.b_plane((0, -ca, -cb))
                corner = jnp.where(found, lane_roll(plane, shift), fill)
                at = (TA - 1 if ca > 0 else 0) + (-1 if cb > 0 else 1)
                face = jnp.where(lane // TB == at % TA, corner, face)
            x = jnp.where(edge_b, face, x)
        if cl:
            row = self.l_row((-cl, 0, 0), cl, key, fill)
            lane_r = lane_iota((1, CELLS))
            if ca:
                corner = self.l_row((-cl, -ca, 0), cl, key, fill)
                row = jnp.where(lane_r // TB == (TA - 1 if ca > 0 else 0), corner, row)
            if cb:
                corner = self.l_row((-cl, 0, -cb), cl, key, fill)
                corner = lane_roll(corner, -TB if cb > 0 else TB)
                row = jnp.where(lane_r % TB == (TB - 1 if cb > 0 else 0), corner, row)
            at = TL - 1 if cl > 0 else 0
            x = jnp.where(row_iota(shape) == at, jnp.broadcast_to(row, shape), x)
        return row_roll(lane_roll(x, TB * ca + cb), cl)


def first_kernel(pops, mask, frac, probe, post, ab, up, dn):
    count = pops.shape[0]

    def run(t, r, c):
        f = [chunk(pops, t, i, r, c) for i in range(Q)]
        solid = plane_chunk(mask, t, r, c).astype(jnp.float32) * plane_chunk(frac, t, r, c)
        out = collide(f, solid, *flow(f))
        for i in range(Q):
            post[t, i, pl.ds(r, 8), pl.ds(c, LANES)] = out[i]

    for_chunks(count, run)

    def faces(t, carry):
        def get(key, rows, lanes):
            if key[0] == "probe":
                return probe[t, rows, lanes]
            return post[t, key[1], rows, lanes]

        write_faces(PACK1, t, get, ab, up, dn)
        return carry

    lax.fori_loop(0, count, faces, 0)


def second_kernel(
    dims, pos, post0, mask, frac, probe, around, post1, adj1, dsolid, ab, up, dn, state, pulled, inv
):
    n_layers, n_cross = dims
    count = post0.shape[0]
    build_inverse(pos, inv, n_layers, n_cross * count)

    def move(t, carry):
        near = Neighbours(PACK1, t, around, pos, inv, n_cross, count)
        for i in range(Q):
            state[t, i] = near.stream(post0[t, i], vel(i), ("post", i), WEIGHTS[i])
        for n, i in enumerate(AXIAL):
            back = tuple(-v for v in vel(i))
            moved = near.stream(probe[t], back, ("probe", 0), 0.0)
            pulled[t, n] = moved if vel(i)[0] > 0 else -moved
        return carry

    lax.fori_loop(0, count, move, 0)

    def run(t, r, c):
        f = [chunk(state, t, i, r, c) for i in range(Q)]
        solid = plane_chunk(mask, t, r, c).astype(jnp.float32) * plane_chunk(frac, t, r, c)
        rho, u, base = flow(f)
        out = collide(f, solid, rho, u, base)
        for i in range(Q):
            post1[t, i, pl.ds(r, 8), pl.ds(c, LANES)] = out[i]
        g = [None] * Q
        for n, i in enumerate(AXIAL):
            g[i] = chunk(pulled, t, n, r, c)
        back, ds = pullback(f, solid, rho, u, base, g)
        for i in range(Q):
            adj1[t, i, pl.ds(r, 8), pl.ds(c, LANES)] = back[i]
        dsolid[t, pl.ds(r, 8), pl.ds(c, LANES)] = ds

    for_chunks(count, run)

    def faces(t, carry):
        def get(key, rows, lanes):
            return (post1 if key[0] == "post" else adj1)[t, key[1], rows, lanes]

        write_faces(PACK2, t, get, ab, up, dn)
        return carry

    lax.fori_loop(0, count, faces, 0)


def third_kernel(
    dims, pos, post1, adj1, pops, mask, frac, patch, dsolid, around, final, start, sums, pulled, weighted, inv
):
    n_layers, n_cross = dims
    count = pops.shape[0]
    group = n_cross * count
    build_inverse(pos, inv, n_layers, group)

    def move(t, carry):
        near = Neighbours(PACK2, t, around, pos, inv, n_cross, count)
        for i in range(Q):
            moved = near.stream(post1[t, i], vel(i), ("post", i), WEIGHTS[i])
            final[t, i] = jnp.where(near.alive, moved, 0.0)
            back = tuple(-v for v in vel(i))
            pulled[t, i] = near.stream(adj1[t, i], back, ("adj", i), 0.0)
        return carry

    lax.fori_loop(0, count, move, 0)
    base_slot = lax.axis_index("gx") * group + lax.axis_index("yz") * count

    def run(t, r, c):
        alive = pos[base_slot + t] >= 0
        f = [chunk(pops, t, i, r, c) for i in range(Q)]
        g = [chunk(pulled, t, i, r, c) for i in range(Q)]
        wall = plane_chunk(mask, t, r, c).astype(jnp.float32)
        solid = wall * plane_chunk(frac, t, r, c)
        rho, u, base = flow(f)
        back, ds = pullback(f, solid, rho, u, base, g)
        for i in range(Q):
            start[t, i, pl.ds(r, 8), pl.ds(c, LANES)] = jnp.where(alive, back[i], 0.0)
        total = wall * (ds + plane_chunk(dsolid, t, r, c))
        weighted[t, pl.ds(r, 8), pl.ds(c, LANES)] = jnp.where(alive, total, 0.0)

    for_chunks(count, run)

    n_high = sums.shape[0]
    high_iota = lax.broadcasted_iota(jnp.int32, (n_high, CELLS), 0)
    low_iota = lax.broadcasted_iota(jnp.int32, (LANES, CELLS), 0)

    def add(k, acc):
        t = k // TL
        r = k % TL
        ids = patch[t, pl.ds(r, 1), :]
        w = weighted[t, pl.ds(r, 1), :]
        w1 = w.astype(jnp.bfloat16).astype(jnp.float32)
        w2 = (w - w1).astype(jnp.bfloat16).astype(jnp.float32)
        w3 = w - w1 - w2
        high = high_iota == ids // LANES
        left = jnp.concatenate(
            [jnp.where(high, part, 0.0).astype(jnp.bfloat16) for part in (w1, w2, w3)],
            axis=0,
        )
        right = jnp.where(low_iota == ids % LANES, 1.0, 0.0).astype(jnp.bfloat16)
        return acc + lax.dot_general(
            left, right, (((1,), (1,)), ((), ())), preferred_element_type=jnp.float32
        )

    acc = lax.fori_loop(
        0, count * TL, add, jnp.zeros((3 * n_high, LANES), jnp.float32)
    )
    sums[...] = acc[:n_high] + acc[n_high : 2 * n_high] + acc[2 * n_high :]


def call(kernel, outs, scratch, args, in_smem=()):
    vmem = pl.BlockSpec(memory_space=pltpu.VMEM)
    smem = pl.BlockSpec(memory_space=pltpu.SMEM)
    return pl.pallas_call(
        kernel,
        out_shape=[jax.ShapeDtypeStruct(s, jnp.float32) for s in outs],
        in_specs=[smem if n in in_smem else vmem for n in range(len(args))],
        out_specs=[vmem] * len(outs),
        scratch_shapes=scratch,
        compiler_params=pltpu.CompilerParams(vmem_limit_bytes=40 << 20),
    )(*args)


def exchange(pack, ab, up, dn):
    n = lax.axis_size("gx")
    forward = [(i, (i + 1) % n) for i in range(n)]
    backward = [(j, i) for i, j in forward]
    below = lax.ppermute(up, "gx", forward)
    above = lax.ppermute(dn, "gx", backward)
    block = jnp.concatenate([ab, below, above], axis=1)
    return lax.all_gather(block, "yz", axis=0, tiled=True)


def body(pops_start, tile_pos, wall_mask, wall_frac, patch_id, probe):
    count = pops_start.shape[0]
    n_layers = lax.axis_size("gx")
    n_cross = lax.axis_size("yz")
    parts = n_layers * n_cross
    dims = (n_layers, n_cross)
    field = pops_start.shape
    plane = wall_frac.shape
    patch_dev = 64
    n_high = patch_dev * parts // LANES
    inverse = pltpu.SMEM((3, n_cross * count + 1), jnp.int32)

    def packs(pack):
        return [
            (count, pack.ab_rows, LANES),
            (count, pack.l_rows, LANES),
            (count, pack.l_rows, LANES),
        ]

    post0, ab, up, dn = call(
        first_kernel,
        [field] + packs(PACK1),
        [],
        (pops_start, wall_mask, wall_frac, probe),
    )
    around = exchange(PACK1, ab, up, dn)
    post1, adj1, dsolid, ab, up, dn = call(
        functools.partial(second_kernel, dims),
        [field, field, plane] + packs(PACK2),
        [
            pltpu.VMEM(field, jnp.float32),
            pltpu.VMEM((count, len(AXIAL)) + plane[1:], jnp.float32),
            inverse,
        ],
        (tile_pos, post0, wall_mask, wall_frac, probe, around),
        in_smem=(0,),
    )
    around = exchange(PACK2, ab, up, dn)
    pops_final, adjoint_start, sums = call(
        functools.partial(third_kernel, dims),
        [field, field, (n_high, LANES)],
        [
            pltpu.VMEM(field, jnp.float32),
            pltpu.VMEM(plane, jnp.float32),
            inverse,
        ],
        (tile_pos, post1, adj1, pops_start, wall_mask, wall_frac, patch_id, dsolid, around),
        in_smem=(0,),
    )
    shares = lax.all_to_all(
        sums.reshape(parts, patch_dev), ("gx", "yz"), 0, 0, tiled=True
    )
    return (pops_final, adjoint_start, jnp.sum(shares, axis=0))


def solution(mesh):
    in_specs = (
        P(("gx", "yz"), None, None, None),
        P(),
        P(("gx", "yz"), None, None),
        P(("gx", "yz"), None, None),
        P(("gx", "yz"), None, None),
        P(("gx", "yz"), None, None),
    )
    out_specs = (
        P(("gx", "yz"), None, None, None),
        P(("gx", "yz"), None, None, None),
        P(("gx", "yz")),
    )
    return jax.shard_map(body, mesh=mesh, in_specs=in_specs, out_specs=out_specs, check_vma=False)
```

time: 1180 us -> 68.4 us (0.06); the launches traced: 1170 us -> 68.1 us
  local copies, waits for them, and re-layouts: 642 us -> 3.9 us
  other arithmetic: 334 us -> 0.59 us
  blocking collectives: 108 us -> 28.7 us
  matrix products: 51.6 us -> 0 us
  Pallas kernels: 0 us -> 19.6 us
  starting transfers between devices: 26 us -> 10.9 us
    unnamed x1005 -> x16, local copies, waits for them, and re-layouts: 276 us -> 3.83 us
    concatenate x17 -> x2, other arithmetic: 156 us -> 0.03 us  [exchange(): block = jnp.concatenate([ab, below, above], axis=1)]
    another operation x270 -> x0, local copies, waits for them, and re-layouts: 135 us -> none  [the longest x62 80.4 us: stream(): return jnp.stack(parts, axis=1)]
    slice x93 -> x0, local copies, waits for them, and re-layouts: 116 us -> none  [the longest x8 57.1 us: faces(): cube[:, :, :, :, 0]]
    scatter-add x1 -> x0, other arithmetic: 86.8 us -> none  [body(): jax.ops.segment_sum(weighted.reshape(-1), patch_id.reshape(-1), num_segme...]
    all_gather x12 -> x2, blocking collectives: 66.8 us -> 16.2 us  [exchange(): return lax.all_gather(block, 'yz', axis=0, tiled=True)]
    reshape x50 -> x0, local copies, waits for them, and re-layouts: 46.3 us -> none  [the longest x8 9.15 us: b_slab(): row_low = edge_line(0, -1, 2, side).reshape(count, 19, 1, TA, 1)]
    unnamed x1 -> x0, blocking collectives: 40.7 us -> none
  transfers between devices with their start and end apart: 8 -> 4, of which waited for: 0 -> 2; matrix products, arithmetic and copies ran while one was open for 28% -> 0% of each run, Pallas kernels for 0% -> 0%
where the time goes in v1:
time: 68.4 us; the launch traced here: 68.1 us
  blocking collectives  28.7 us (42%)
  Pallas kernels  19.6 us (29%)
  starting transfers between devices  10.9 us (16%)
  local copies, waits for them, and re-layouts  3.9 us (6%)
  waiting for transfers between devices  3.76 us (5%)
  between operations  0.69 us (1%)
    pallas_call x3, Pallas kernels, call(): pl.pallas_call(kernel, out_shape=[jax.ShapeDtypeStruct(s, jnp.float32) fo...  19.6 us
    all_gather x2, blocking collectives, exchange(): return lax.all_gather(block, 'yz', axis=0, tiled=True)  16.2 us
    all_to_all x1, blocking collectives, body(): lax.all_to_all(sums.reshape(parts, patch_dev), ('gx', 'yz'), 0, 0, tiled=...  12.4 us
    ppermute x2, starting transfers between devices, exchange(): above = lax.ppermute(dn, 'gx', backward)  6.65 us
    ppermute x2, starting transfers between devices, exchange(): below = lax.ppermute(up, 'gx', forward)  4.28 us
    unnamed x16, local copies, waits for them, and re-layouts  3.83 us
    ppermute x2, waiting for transfers between devices, exchange(): below = lax.ppermute(up, 'gx', forward)  3.75 us
  transfers between devices with their start and end apart: 4, of which 2 were waited for; matrix products, arithmetic and copies ran while one was open for 0% of the time, Pallas kernels for 0%

profile of v1, /device:TPU:0, one launch (start us, length us, event | category | flops | bytes accessed | tf_op | source)
XLA Modules:
  0.0 68.1 jit_solution(8675763468794975868)
XLA Ops:
  0.6 0.0 copy-start
  0.6 1.3 %copy-done = f32[2,19,16,512]{3,2,1,0:T(8,128)S(1)} copy-done((f32[2,19,16,512]{3,2,1,0:T(8,128)S(1)}, f32[2,19,16,512]{3,2,1,0:T(8,128)}, u32[]{:S(2)}) %copy-start) | copy-done | bytes 1245208
  1.9 0.0 copy-start.2
  1.9 0.8 %copy-done.2 = s32[2,16,512]{2,1,0:T(8,128)S(1)} copy-done((s32[2,16,512]{2,1,0:T(8,128)S(1)}, s32[2,16,512]{2,1,0:T(8,128)}, u32[]{:S(2)}) %copy-start.2) | copy-done | bytes 65560
  2.8 0.0 copy-start.3
  2.8 0.8 %copy-done.3 = f32[2,16,512]{2,1,0:T(8,128)S(1)} copy-done((f32[2,16,512]{2,1,0:T(8,128)S(1)}, f32[2,16,512]{2,1,0:T(8,128)}, u32[]{:S(2)}) %copy-start.3) | copy-done | bytes 65560
  3.6 0.0 copy-start.4
  3.6 0.8 %copy-done.4 = f32[2,16,512]{2,1,0:T(8,128)S(1)} copy-done((f32[2,16,512]{2,1,0:T(8,128)S(1)}, f32[2,16,512]{2,1,0:T(8,128)}, u32[]{:S(2)}) %copy-start.4) | copy-done | bytes 65560
  4.4 0.0 copy-start.5
  4.5 0.0 copy-start.7
  4.5 1.2 %shard_map.85 = (f32[2,19,16,512]{3,2,1,0:T(8,128)S(1)}, f32[2,80,128]{2,1,0:T(8,128)S(1)}, f32[2,24,128]{2,1,0:T(8,128)S(1)}, f32[2,24,128]{2,1,0:T(8,128)S(1)}) custom-call(f32[2,19,16,512]{3,2,1,0:T(8,128)S(1)} %copy-done, s32[2,16,512]{2,1,0:T(8,128)S(1)} %copy-done.2, f32[2,16,512]{2,1,0:T(8,128)S(1)} %copy-done.3, f32[2,16,512]{2,1,0:T(8,128)S(1)} %copy-done.4), custom_call_target="tpu_custom_call" | custom-call | tf_op jit(solution)/shard_map/pallas_call | solution.py:514
  5.7 3.0 %collective-permute-start = (f32[2,24,128]{2,1,0:T(8,128)S(1)}, f32[2,24,128]{2,1,0:T(8,128)S(1)}, u32[]{:S(2)}, u32[]{:S(2)}) collective-permute-start(f32[2,24,128]{2,1,0:T(8,128)S(1)} %get-tuple-element.18), channel_id=1, source_target_pairs={{0,4},{4,8},{8,12},{12,16},{16,20},{20,24},{24,28},{28,0},{1,5},{5... | collective-permute-start | bytes 73736 | tf_op jit(solution)/shard_map/ppermute | solution.py:528
  8.7 3.1 %collective-permute-start.1 = (f32[2,24,128]{2,1,0:T(8,128)S(1)}, f32[2,24,128]{2,1,0:T(8,128)S(1)}, u32[]{:S(2)}, u32[]{:S(2)}) collective-permute-start(f32[2,24,128]{2,1,0:T(8,128)S(1)} %get-tuple-element.19), channel_id=1, source_target_pairs={{4,0},{8,4},{12,8},{16,12},{20,16},{24,20},{28,24},{0,28},{5,1},{9... | collective-permute-start | bytes 73736 | tf_op jit(solution)/shard_map/ppermute | solution.py:529
  11.8 1.7 %collective-permute-done = f32[2,24,128]{2,1,0:T(8,128)S(1)} collective-permute-done((f32[2,24,128]{2,1,0:T(8,128)S(1)}, f32[2,24,128]{2,1,0:T(8,128)S(1)}, u32[]{:S(2)}, u32[]{:S(2)}) %collective-permute-start) | collective-permute-done | bytes 24608 | tf_op jit(solution)/shard_map/ppermute | solution.py:528
  13.5 0.0 collective-permute-done.1
  13.5 7.4 %all_gather.6.around = f32[8,128,128]{2,1,0:T(8,128)S(1)} all-gather(f32[2,128,128]{2,1,0:T(8,128)S(1)} %pad_maximum_fusion.1), channel_id=1, replica_groups=mesh['gx'=8,'yz'=4] {'yz'}, dimensions={0}, use_global_device_ids=true | all-gather | bytes 655360 | tf_op jit(solution)/shard_map/all_gather | solution.py:531
  20.9 0.0 copy-done.5
  20.9 0.0 copy-done.7
  20.9 5.4 %shard_map.86 = (f32[2,19,16,512]{3,2,1,0:T(8,128)S(1)}, f32[2,19,16,512]{3,2,1,0:T(8,128)S(1)}, f32[2,16,512]{2,1,0:T(8,128)S(1)}, f32[2,144,128]{2,1,0:T(8,128...) custom-call(s32[64]{0:T(128)S(1)} %copy-done.7, f32[2,19,16,512]{3,2,1,0:T(8,128)S(1)} %get-tuple-element.16.post0, ...), custom_call_target="tpu_custom_call" | custom-call | tf_op jit(solution)/shard_map/pallas_call | solution.py:514
  26.3 0.0 copy-start.1
  26.4 0.0 copy-start.6
  26.4 1.3 %collective-permute-start.2 = (f32[2,40,128]{2,1,0:T(8,128)S(1)}, f32[2,40,128]{2,1,0:T(8,128)S(1)}, u32[]{:S(2)}, u32[]{:S(2)}) collective-permute-start(f32[2,40,128]{2,1,0:T(8,128)S(1)} %get-tuple-element.24), channel_id=1, source_target_pairs={{0,4},{4,8},{8,12},{12,16},{16,20},{20,24},{24,28},{28,0},{1,5},{5... | collective-permute-start | bytes 122888 | tf_op jit(solution)/shard_map/ppermute | solution.py:528
  27.7 3.5 %collective-permute-start.3 = (f32[2,40,128]{2,1,0:T(8,128)S(1)}, f32[2,40,128]{2,1,0:T(8,128)S(1)}, u32[]{:S(2)}, u32[]{:S(2)}) collective-permute-start(f32[2,40,128]{2,1,0:T(8,128)S(1)} %get-tuple-element.25), channel_id=1, source_target_pairs={{4,0},{8,4},{12,8},{16,12},{20,16},{24,20},{28,24},{0,28},{5,1},{9... | collective-permute-start | bytes 122888 | tf_op jit(solution)/shard_map/ppermute | solution.py:529
  31.2 2.0 %collective-permute-done.2 = f32[2,40,128]{2,1,0:T(8,128)S(1)} collective-permute-done((f32[2,40,128]{2,1,0:T(8,128)S(1)}, f32[2,40,128]{2,1,0:T(8,128)S(1)}, u32[]{:S(2)}, u32[]{:S(2)}) %collective-permute-start.2) | collective-permute-done | bytes 40992 | tf_op jit(solution)/shard_map/ppermute | solution.py:528
  33.2 0.0 collective-permute-done.3
  33.2 8.9 %all_gather.7.around = f32[8,224,128]{2,1,0:T(8,128)S(1)} all-gather(f32[2,224,128]{2,1,0:T(8,128)S(1)} %pad_maximum_fusion), channel_id=1, replica_groups=mesh['gx'=8,'yz'=4] {'yz'}, dimensions={0}, use_global_device_ids=true | all-gather | bytes 1146880 | tf_op jit(solution)/shard_map/all_gather | solution.py:531
  42.1 0.0 copy-done.1
  42.1 0.0 copy-done.6
  42.1 12.9 %shard_map.87 = (f32[2,19,16,512]{3,2,1,0:T(8,128)}, f32[2,19,16,512]{3,2,1,0:T(8,128)}, f32[16,128]{1,0:T(8,128)S(1)}) custom-call(s32[64]{0:T(128)S(1)} %copy-done.7, f32[2,19,16,512]{3,2,1,0:T(8,128)S(1)} %get-tuple-element.20.post1, f32[2,19,16,512]{3,2,1,0:T(8,128)S(1)} %get-tuple-element.21.adj1, f32[2,19,16,512]{3,2,1,0:T(8,128)S(1)} %copy-done.1, ...), custom_call_target="tpu_custom_call" | custom-call | tf_op jit(solution)/shard_map/pallas_call | solution.py:514
  55.0 0.1 all_to_all.6
  55.1 12.4 %all_to_all.9 = f32[32,1,64]{2,1,0:T(1,128)S(1)} all-to-all(f32[32,1,64]{2,1,0:T(1,128)S(1)} %bitcast.1), channel_id=1, replica_groups=mesh['gx'=8,'yz'=4] {'gx','yz'}, dimensions={0} | all-to-all | bytes 16384 | tf_op jit(solution)/shard_map/all_to_all | solution.py:583
  67.5 0.6 reduce_sum.9
  (2 shorter events, 0.0 us)
Async XLA Ops:
  0.6 1.3 %copy-start = (f32[2,19,16,512]{3,2,1,0:T(8,128)S(1)}, f32[2,19,16,512]{3,2,1,0:T(8,128)}, u32[]{:S(2)}) copy-start(f32[2,19,16,512]{3,2,1,0:T(8,128)} %pops.3) | copy-start | bytes 3735556
  1.9 0.8 %copy-start.2 = (s32[2,16,512]{2,1,0:T(8,128)S(1)}, s32[2,16,512]{2,1,0:T(8,128)}, u32[]{:S(2)}) copy-start(s32[2,16,512]{2,1,0:T(8,128)} %mask.5) | copy-start | bytes 196612
  2.8 0.8 %copy-start.3 = (f32[2,16,512]{2,1,0:T(8,128)S(1)}, f32[2,16,512]{2,1,0:T(8,128)}, u32[]{:S(2)}) copy-start(f32[2,16,512]{2,1,0:T(8,128)} %frac.5) | copy-start | bytes 196612
  3.6 0.8 %copy-start.4 = (f32[2,16,512]{2,1,0:T(8,128)S(1)}, f32[2,16,512]{2,1,0:T(8,128)}, u32[]{:S(2)}) copy-start(f32[2,16,512]{2,1,0:T(8,128)} %probe.3) | copy-start | bytes 196612
  4.4 16.5 %copy-start.5 = (f32[2,16,512]{2,1,0:T(8,128)S(1)}, f32[2,16,512]{2,1,0:T(8,128)}, u32[]{:S(2)}) copy-start(f32[2,16,512]{2,1,0:T(8,128)} %probe.3) | copy-start | bytes 196612
  4.5 16.5 %copy-start.7 = (s32[64]{0:T(128)S(1)}, s32[64]{0:T(128)}, u32[]{:S(2)}) copy-start(s32[64]{0:T(128)} %pos.3) | copy-start | bytes 772
  5.7 7.8 %collective-permute-start = (f32[2,24,128]{2,1,0:T(8,128)S(1)}, f32[2,24,128]{2,1,0:T(8,128)S(1)}, u32[]{:S(2)}, u32[]{:S(2)}) collective-permute-start(f32[2,24,128]{2,1,0:T(8,128)S(1)} %get-tuple-element.18), channel_id=1, source_target_pairs={{0,4},{4,8},{8,12},{12,16},{16,20},{20,24},{24,28},{28,0},{1,5},{5... | collective-permute-start | bytes 73736 | tf_op jit(solution)/shard_map/ppermute | solution.py:528
  8.7 4.8 %collective-permute-start.1 = (f32[2,24,128]{2,1,0:T(8,128)S(1)}, f32[2,24,128]{2,1,0:T(8,128)S(1)}, u32[]{:S(2)}, u32[]{:S(2)}) collective-permute-start(f32[2,24,128]{2,1,0:T(8,128)S(1)} %get-tuple-element.19), channel_id=1, source_target_pairs={{4,0},{8,4},{12,8},{16,12},{20,16},{24,20},{28,24},{0,28},{5,1},{9... | collective-permute-start | bytes 73736 | tf_op jit(solution)/shard_map/ppermute | solution.py:529
  26.3 15.8 %copy-start.1 = (f32[2,19,16,512]{3,2,1,0:T(8,128)S(1)}, f32[2,19,16,512]{3,2,1,0:T(8,128)}, u32[]{:S(2)}) copy-start(f32[2,19,16,512]{3,2,1,0:T(8,128)} %pops.3) | copy-start | bytes 3735556
  26.4 15.7 %copy-start.6 = (s32[2,16,512]{2,1,0:T(8,128)S(1)}, s32[2,16,512]{2,1,0:T(8,128)}, u32[]{:S(2)}) copy-start(s32[2,16,512]{2,1,0:T(8,128)} %patch.1) | copy-start | bytes 196612
  26.4 6.9 %collective-permute-start.2 = (f32[2,40,128]{2,1,0:T(8,128)S(1)}, f32[2,40,128]{2,1,0:T(8,128)S(1)}, u32[]{:S(2)}, u32[]{:S(2)}) collective-permute-start(f32[2,40,128]{2,1,0:T(8,128)S(1)} %get-tuple-element.24), channel_id=1, source_target_pairs={{0,4},{4,8},{8,12},{12,16},{16,20},{20,24},{24,28},{28,0},{1,5},{5... | collective-permute-start | bytes 122888 | tf_op jit(solution)/shard_map/ppermute | solution.py:528
  27.7 5.6 %collective-permute-start.3 = (f32[2,40,128]{2,1,0:T(8,128)S(1)}, f32[2,40,128]{2,1,0:T(8,128)S(1)}, u32[]{:S(2)}, u32[]{:S(2)}) collective-permute-start(f32[2,40,128]{2,1,0:T(8,128)S(1)} %get-tuple-element.25), channel_id=1, source_target_pairs={{4,0},{8,4},{12,8},{16,12},{20,16},{24,20},{28,24},{0,28},{5,1},{9... | collective-permute-start | bytes 122888 | tf_op jit(solution)/shard_map/ppermute | solution.py:529

commit v2 on v1

--- a/solution.py
+++ b/solution.py
@@ -246,7 +246,7 @@
                         get(key, slice(None), slice(CELLS - LANES, CELLS)),
                         to - (LANES - TB),
                     )
-                acc = jnp.where(lane // TB == j % 4, part, acc)
+                acc = jnp.where((lane >> 5) == j % 4, part, acc)
         ab_ref[t, pack.a_row + TL * col : pack.a_row + TL * (col + 1), :] = acc
     for col in range(pack.b_cols):
         acc = jnp.zeros((TL, LANES), jnp.float32)
@@ -257,7 +257,7 @@
                     j = pack.slot(2, side, key) + half * (TB // 2)
                     part = get(key, slice(None), slice(LANES * src, LANES * (src + 1)))
                     part = lane_roll(part, j if side < 0 else j - (TB - 1))
-                    acc = jnp.where(lane % TB == j, part, acc)
+                    acc = jnp.where((lane & (TB - 1)) == j, part, acc)
         ab_ref[t, pack.b_row + TL * col : pack.b_row + TL * (col + 1), :] = acc
     for side, ref in ((1, up_ref), (-1, dn_ref)):
         row = TL - 1 if side > 0 else 0
@@ -337,8 +337,8 @@
         cl, ca, cb = c
         shape = (TL, CELLS)
         lane = lane_iota(shape)
-        edge_b = lane % TB == (TB - 1 if cb > 0 else 0)
-        edge_a = lane // TB == (TA - 1 if ca > 0 else 0)
+        edge_b = (lane & (TB - 1)) == (TB - 1 if cb > 0 else 0)
+        edge_a = (lane >> 5) == (TA - 1 if ca > 0 else 0)
         x = own
         if ca:
             face = self.a_face((0, -ca, 0), ca, key, fill)
@@ -358,34 +358,57 @@
                 plane, found = self.b_plane((0, -ca, -cb))
                 corner = jnp.where(found, lane_roll(plane, shift), fill)
                 at = (TA - 1 if ca > 0 else 0) + (-1 if cb > 0 else 1)
-                face = jnp.where(lane // TB == at % TA, corner, face)
+                face = jnp.where((lane >> 5) == at % TA, corner, face)
             x = jnp.where(edge_b, face, x)
         if cl:
             row = self.l_row((-cl, 0, 0), cl, key, fill)
             lane_r = lane_iota((1, CELLS))
             if ca:
                 corner = self.l_row((-cl, -ca, 0), cl, key, fill)
-                row = jnp.where(lane_r // TB == (TA - 1 if ca > 0 else 0), corner, row)
+                row = jnp.where((lane_r >> 5) == (TA - 1 if ca > 0 else 0), corner, row)
             if cb:
                 corner = self.l_row((-cl, 0, -cb), cl, key, fill)
                 corner = lane_roll(corner, -TB if cb > 0 else TB)
-                row = jnp.where(lane_r % TB == (TB - 1 if cb > 0 else 0), corner, row)
+                row = jnp.where((lane_r & (TB - 1)) == (TB - 1 if cb > 0 else 0), corner, row)
             at = TL - 1 if cl > 0 else 0
             x = jnp.where(row_iota(shape) == at, jnp.broadcast_to(row, shape), x)
         return row_roll(lane_roll(x, TB * ca + cb), cl)
 
 
-def first_kernel(pops, mask, frac, probe, post, ab, up, dn):
+def first_kernel(pops_in, mask_in, frac_in, probe_in, post, solid, probe, ab, up, dn, pops, mask, frac, sems):
     count = pops.shape[0]
-
-    def run(t, r, c):
-        f = [chunk(pops, t, i, r, c) for i in range(Q)]
-        solid = plane_chunk(mask, t, r, c).astype(jnp.float32) * plane_chunk(frac, t, r, c)
-        out = collide(f, solid, *flow(f))
-        for i in range(Q):
-            post[t, i, pl.ds(r, 8), pl.ds(c, LANES)] = out[i]
-
-    for_chunks(count, run)
+    small = [
+        pltpu.make_async_copy(src, dst, sems.at[n])
+        for n, (src, dst) in enumerate(((mask_in, mask), (frac_in, frac), (probe_in, probe)))
+    ]
+    halves = [(t, r) for t in range(count) for r in range(2)]
+    large = [
+        pltpu.make_async_copy(
+            pops_in.at[t, :, pl.ds(8 * r, 8), :],
+            pops.at[t, :, pl.ds(8 * r, 8), :],
+            sems.at[len(small) + n],
+        )
+        for n, (t, r) in enumerate(halves)
+    ]
+    for copy in small[:2] + large + small[2:]:
+        copy.start()
+    for copy in small[:2]:
+        copy.wait()
+    solid[...] = mask[...].astype(jnp.float32) * frac[...]
+
+    for n, (t, r) in enumerate(halves):
+        large[n].wait()
+
+        def run(k, carry, t=t, r=8 * r):
+            c = pl.multiple_of(k * LANES, LANES)
+            f = [chunk(pops, t, i, r, c) for i in range(Q)]
+            out = collide(f, plane_chunk(solid, t, r, c), *flow(f))
+            for i in range(Q):
+                post[t, i, pl.ds(r, 8), pl.ds(c, LANES)] = out[i]
+            return carry
+
+        lax.fori_loop(0, COLS, run, 0)
+    small[2].wait()
 
     def faces(t, carry):
         def get(key, rows, lanes):
@@ -400,7 +423,7 @@
 
 
 def second_kernel(
-    dims, pos, post0, mask, frac, probe, around, post1, adj1, dsolid, ab, up, dn, state, pulled, inv
+    dims, pos, post0, solid_in, probe, around, post1, adj1, dsolid, ab, up, dn, state, pulled, inv
 ):
     n_layers, n_cross = dims
     count = post0.shape[0]
@@ -420,7 +443,7 @@
 
     def run(t, r, c):
         f = [chunk(state, t, i, r, c) for i in range(Q)]
-        solid = plane_chunk(mask, t, r, c).astype(jnp.float32) * plane_chunk(frac, t, r, c)
+        solid = plane_chunk(solid_in, t, r, c)
         rho, u, base = flow(f)
         out = collide(f, solid, rho, u, base)
         for i in range(Q):
@@ -446,7 +469,7 @@
 
 
 def third_kernel(
-    dims, pos, post1, adj1, pops, mask, frac, patch, dsolid, around, final, start, sums, pulled, weighted, inv
+    dims, pos, post1, adj1, pops, mask, solid_in, patch, dsolid, around, final_out, start_out, sums, final, start, pulled, weighted, inv, sems
 ):
     n_layers, n_cross = dims
     count = pops.shape[0]
@@ -463,6 +486,8 @@
         return carry
 
     lax.fori_loop(0, count, move, 0)
+    out_final = pltpu.make_async_copy(final, final_out, sems.at[0])
+    out_final.start()
     base_slot = lax.axis_index("gx") * group + lax.axis_index("yz") * count
 
     def run(t, r, c):
@@ -470,7 +495,7 @@
         f = [chunk(pops, t, i, r, c) for i in range(Q)]
         g = [chunk(pulled, t, i, r, c) for i in range(Q)]
         wall = plane_chunk(mask, t, r, c).astype(jnp.float32)
-        solid = wall * plane_chunk(frac, t, r, c)
+        solid = plane_chunk(solid_in, t, r, c)
         rho, u, base = flow(f)
         back, ds = pullback(f, solid, rho, u, base, g)
         for i in range(Q):
@@ -479,43 +504,54 @@
         weighted[t, pl.ds(r, 8), pl.ds(c, LANES)] = jnp.where(alive, total, 0.0)
 
     for_chunks(count, run)
+    out_start = pltpu.make_async_copy(start, start_out, sems.at[1])
+    out_start.start()
 
     n_high = sums.shape[0]
     high_iota = lax.broadcasted_iota(jnp.int32, (n_high, CELLS), 0)
     low_iota = lax.broadcasted_iota(jnp.int32, (LANES, CELLS), 0)
 
     def add(k, acc):
-        t = k // TL
-        r = k % TL
-        ids = patch[t, pl.ds(r, 1), :]
-        w = weighted[t, pl.ds(r, 1), :]
-        w1 = w.astype(jnp.bfloat16).astype(jnp.float32)
-        w2 = (w - w1).astype(jnp.bfloat16).astype(jnp.float32)
-        w3 = w - w1 - w2
-        high = high_iota == ids // LANES
-        left = jnp.concatenate(
-            [jnp.where(high, part, 0.0).astype(jnp.bfloat16) for part in (w1, w2, w3)],
-            axis=0,
-        )
-        right = jnp.where(low_iota == ids % LANES, 1.0, 0.0).astype(jnp.bfloat16)
-        return acc + lax.dot_general(
-            left, right, (((1,), (1,)), ((), ())), preferred_element_type=jnp.float32
-        )
+        t = k // 2
+        r = pl.multiple_of((k % 2) * 8, 8)
+        ids8 = patch[t, pl.ds(r, 8), :]
+        w8 = weighted[t, pl.ds(r, 8), :]
+        for n in range(8):
+            ids = ids8[n : n + 1]
+            w = w8[n : n + 1]
+            w1 = w.astype(jnp.bfloat16).astype(jnp.float32)
+            w2 = (w - w1).astype(jnp.bfloat16).astype(jnp.float32)
+            w3 = w - w1 - w2
+            high = high_iota == (ids >> 7)
+            left = jnp.concatenate(
+                [jnp.where(high, part, 0.0).astype(jnp.bfloat16) for part in (w1, w2, w3)],
+                axis=0,
+            )
+            right = jnp.where(low_iota == (ids & (LANES - 1)), 1.0, 0.0).astype(jnp.bfloat16)
+            acc = acc + lax.dot_general(
+                left, right, (((1,), (1,)), ((), ())), preferred_element_type=jnp.float32
+            )
+        return acc
 
     acc = lax.fori_loop(
-        0, count * TL, add, jnp.zeros((3 * n_high, LANES), jnp.float32)
+        0, count * 2, add, jnp.zeros((3 * n_high, LANES), jnp.float32)
     )
+    out_final.wait()
+    out_start.wait()
     sums[...] = acc[:n_high] + acc[n_high : 2 * n_high] + acc[2 * n_high :]
 
 
-def call(kernel, outs, scratch, args, in_smem=()):
+def call(kernel, outs, scratch, args, in_smem=(), in_hbm=(), out_hbm=()):
     vmem = pl.BlockSpec(memory_space=pltpu.VMEM)
+    hbm = pl.BlockSpec(memory_space=pltpu.HBM)
     smem = pl.BlockSpec(memory_space=pltpu.SMEM)
     return pl.pallas_call(
         kernel,
         out_shape=[jax.ShapeDtypeStruct(s, jnp.float32) for s in outs],
-        in_specs=[smem if n in in_smem else vmem for n in range(len(args))],
-        out_specs=[vmem] * len(outs),
+        in_specs=[
+            smem if n in in_smem else hbm if n in in_hbm else vmem for n in range(len(args))
+        ],
+        out_specs=[hbm if n in out_hbm else vmem for n in range(len(outs))],
         scratch_shapes=scratch,
         compiler_params=pltpu.CompilerParams(vmem_limit_bytes=40 << 20),
     )(*args)
@@ -550,11 +586,20 @@
             (count, pack.l_rows, LANES),
         ]
 
-    post0, ab, up, dn = call(
+    post0, solid, probe_kept, ab, up, dn = call(
         first_kernel,
-        [field] + packs(PACK1),
-        [],
-        (pops_start, wall_mask, wall_frac, probe),
+        [field, plane, plane] + packs(PACK1),
+        [
+            pltpu.VMEM(field, jnp.float32),
+            pltpu.VMEM(plane, jnp.int32),
+            pltpu.VMEM(plane, jnp.float32),
+            pltpu.SemaphoreType.DMA((3 + 2 * count,)),
+        ],
+        tuple(
+            pltpu.with_memory_space_constraint(x, pltpu.HBM)
+            for x in (pops_start, wall_mask, wall_frac, probe)
+        ),
+        in_hbm=range(4),
     )
     around = exchange(PACK1, ab, up, dn)
     post1, adj1, dsolid, ab, up, dn = call(
@@ -565,7 +610,7 @@
             pltpu.VMEM((count, len(AXIAL)) + plane[1:], jnp.float32),
             inverse,
         ],
-        (tile_pos, post0, wall_mask, wall_frac, probe, around),
+        (tile_pos, post0, solid, probe_kept, around),
         in_smem=(0,),
     )
     around = exchange(PACK2, ab, up, dn)
@@ -574,11 +619,15 @@
         [field, field, (n_high, LANES)],
         [
             pltpu.VMEM(field, jnp.float32),
+            pltpu.VMEM(field, jnp.float32),
+            pltpu.VMEM(field, jnp.float32),
             pltpu.VMEM(plane, jnp.float32),
             inverse,
+            pltpu.SemaphoreType.DMA((2,)),
         ],
-        (tile_pos, post1, adj1, pops_start, wall_mask, wall_frac, patch_id, dsolid, around),
+        (tile_pos, post1, adj1, pops_start, wall_mask, solid, patch_id, dsolid, around),
         in_smem=(0,),
+        out_hbm=(0, 1),
     )
     shares = lax.all_to_all(
         sums.reshape(parts, patch_dev), ("gx", "yz"), 0, 0, tiled=True

time: 68.4 us -> 60.6 us (0.89)
  Pallas kernels: 19.6 us -> 15.7 us
  local copies, waits for them, and re-layouts: 3.9 us -> 0.09 us
    pallas_call x3, Pallas kernels: 19.6 us -> 15.7 us  [call(): pl.pallas_call(kernel, out_shape=[jax.ShapeDtypeStruct(s, jnp.float32) fo...]
    unnamed x16 -> x8, local copies, waits for them, and re-layouts: 3.83 us -> 0.02 us
where the time goes in v2:
time: 60.6 us; the launch traced here: 60.4 us
  blocking collectives  28.7 us (47%)
  Pallas kernels  15.7 us (26%)
  starting transfers between devices  10.9 us (18%)
  waiting for transfers between devices  3.76 us (6%)
  between operations  0.7 us (1%)
    all_gather x2, blocking collectives, exchange(): return lax.all_gather(block, 'yz', axis=0, tiled=True)  16.2 us
    pallas_call x3, Pallas kernels, call(): pl.pallas_call(kernel, out_shape=[jax.ShapeDtypeStruct(s, jnp.float32) fo...  15.7 us
    all_to_all x1, blocking collectives, body(): lax.all_to_all(sums.reshape(parts, patch_dev), ('gx', 'yz'), 0, 0, tiled=...  12.4 us
    ppermute x2, starting transfers between devices, exchange(): above = lax.ppermute(dn, 'gx', backward)  6.65 us
    ppermute x2, starting transfers between devices, exchange(): below = lax.ppermute(up, 'gx', forward)  4.28 us
    ppermute x2, waiting for transfers between devices, exchange(): below = lax.ppermute(up, 'gx', forward)  3.75 us
  transfers between devices with their start and end apart: 4, of which 2 were waited for; matrix products, arithmetic and copies ran while one was open for 0% of the time, Pallas kernels for 0%

profile of v2, /device:TPU:0, one launch (start us, length us, event | category | flops | bytes accessed | tf_op | source)
XLA Modules:
  0.0 60.4 jit_solution(2805974374286919507)
XLA Ops:
  0.6 0.0 copy-start.3
  0.6 2.1 %shard_map.85 = (f32[2,19,16,512]{3,2,1,0:T(8,128)S(1)}, f32[2,16,512]{2,1,0:T(8,128)S(1)}, f32[2,16,512]{2,1,0:T(8,128)S(1)}, f32[2,80,128]{2,1,0:T(8,128)S(1)}...) custom-call(f32[2,19,16,512]{3,2,1,0:T(8,128)} %pops.1, s32[2,16,512]{2,1,0:T(8,128)} %mask.1, ...), custom_call_target="tpu_custom_call" | custom-call | tf_op jit(solution)/shard_map/pallas_call | solution.py:548
  2.8 3.0 %collective-permute-start = (f32[2,24,128]{2,1,0:T(8,128)S(1)}, f32[2,24,128]{2,1,0:T(8,128)S(1)}, u32[]{:S(2)}, u32[]{:S(2)}) collective-permute-start(f32[2,24,128]{2,1,0:T(8,128)S(1)} %get-tuple-element.22), channel_id=1, source_target_pairs={{0,4},{4,8},{8,12},{12,16},{16,20},{20,24},{24,28},{28,0},{1,5},{5... | collective-permute-start | bytes 73736 | tf_op jit(solution)/shard_map/ppermute | solution.py:564
  5.8 3.1 %collective-permute-start.1 = (f32[2,24,128]{2,1,0:T(8,128)S(1)}, f32[2,24,128]{2,1,0:T(8,128)S(1)}, u32[]{:S(2)}, u32[]{:S(2)}) collective-permute-start(f32[2,24,128]{2,1,0:T(8,128)S(1)} %get-tuple-element.23), channel_id=1, source_target_pairs={{4,0},{8,4},{12,8},{16,12},{20,16},{24,20},{28,24},{0,28},{5,1},{9... | collective-permute-start | bytes 73736 | tf_op jit(solution)/shard_map/ppermute | solution.py:565
  8.9 1.7 %collective-permute-done = f32[2,24,128]{2,1,0:T(8,128)S(1)} collective-permute-done((f32[2,24,128]{2,1,0:T(8,128)S(1)}, f32[2,24,128]{2,1,0:T(8,128)S(1)}, u32[]{:S(2)}, u32[]{:S(2)}) %collective-permute-start) | collective-permute-done | bytes 24608 | tf_op jit(solution)/shard_map/ppermute | solution.py:564
  10.6 0.0 collective-permute-done.1
  10.6 7.4 %all_gather.6.around = f32[8,128,128]{2,1,0:T(8,128)S(1)} all-gather(f32[2,128,128]{2,1,0:T(8,128)S(1)} %pad_maximum_fusion.1), channel_id=1, replica_groups=mesh['gx'=8,'yz'=4] {'yz'}, dimensions={0}, use_global_device_ids=true | all-gather | bytes 655360 | tf_op jit(solution)/shard_map/all_gather | solution.py:567
  18.0 0.0 copy-done.3
  18.0 5.4 %shard_map.86 = (f32[2,19,16,512]{3,2,1,0:T(8,128)S(1)}, f32[2,19,16,512]{3,2,1,0:T(8,128)S(1)}, f32[2,16,512]{2,1,0:T(8,128)S(1)}, f32[2,144,128]{2,1,0:T(8,128...) custom-call(s32[64]{0:T(128)S(1)} %copy-done.3, f32[2,19,16,512]{3,2,1,0:T(8,128)S(1)} %get-tuple-element.18.post0, ...), custom_call_target="tpu_custom_call" | custom-call | tf_op jit(solution)/shard_map/pallas_call | solution.py:548
  23.5 0.0 copy-start
  23.5 0.0 copy-start.1
  23.5 0.0 copy-start.2
  23.5 1.3 %collective-permute-start.2 = (f32[2,40,128]{2,1,0:T(8,128)S(1)}, f32[2,40,128]{2,1,0:T(8,128)S(1)}, u32[]{:S(2)}, u32[]{:S(2)}) collective-permute-start(f32[2,40,128]{2,1,0:T(8,128)S(1)} %get-tuple-element.28), channel_id=1, source_target_pairs={{0,4},{4,8},{8,12},{12,16},{16,20},{20,24},{24,28},{28,0},{1,5},{5... | collective-permute-start | bytes 122888 | tf_op jit(solution)/shard_map/ppermute | solution.py:564
  24.8 3.5 %collective-permute-start.3 = (f32[2,40,128]{2,1,0:T(8,128)S(1)}, f32[2,40,128]{2,1,0:T(8,128)S(1)}, u32[]{:S(2)}, u32[]{:S(2)}) collective-permute-start(f32[2,40,128]{2,1,0:T(8,128)S(1)} %get-tuple-element.29), channel_id=1, source_target_pairs={{4,0},{8,4},{12,8},{16,12},{20,16},{24,20},{28,24},{0,28},{5,1},{9... | collective-permute-start | bytes 122888 | tf_op jit(solution)/shard_map/ppermute | solution.py:565
  28.3 2.0 %collective-permute-done.2 = f32[2,40,128]{2,1,0:T(8,128)S(1)} collective-permute-done((f32[2,40,128]{2,1,0:T(8,128)S(1)}, f32[2,40,128]{2,1,0:T(8,128)S(1)}, u32[]{:S(2)}, u32[]{:S(2)}) %collective-permute-start.2) | collective-permute-done | bytes 40992 | tf_op jit(solution)/shard_map/ppermute | solution.py:564
  30.3 0.0 collective-permute-done.3
  30.4 8.9 %all_gather.7.around = f32[8,224,128]{2,1,0:T(8,128)S(1)} all-gather(f32[2,224,128]{2,1,0:T(8,128)S(1)} %pad_maximum_fusion), channel_id=1, replica_groups=mesh['gx'=8,'yz'=4] {'yz'}, dimensions={0}, use_global_device_ids=true | all-gather | bytes 1146880 | tf_op jit(solution)/shard_map/all_gather | solution.py:567
  39.2 0.0 copy-done
  39.2 0.0 copy-done.1
  39.2 0.0 copy-done.2
  39.2 8.1 %shard_map.87 = (f32[2,19,16,512]{3,2,1,0:T(8,128)}, f32[2,19,16,512]{3,2,1,0:T(8,128)}, f32[16,128]{1,0:T(8,128)S(1)}) custom-call(s32[64]{0:T(128)S(1)} %copy-done.3, f32[2,19,16,512]{3,2,1,0:T(8,128)S(1)} %get-tuple-element.24.post1, f32[2,19,16,512]{3,2,1,0:T(8,128)S(1)} %get-tuple-element.25.adj1, f32[2,19,16,512]{3,2,1,0:T(8,128)S(1)} %copy-done, ...), custom_call_target="tpu_custom_call" | custom-call | tf_op jit(solution)/shard_map/pallas_call | solution.py:548
  47.3 0.1 all_to_all.6
  47.4 12.4 %all_to_all.9 = f32[32,1,64]{2,1,0:T(1,128)S(1)} all-to-all(f32[32,1,64]{2,1,0:T(1,128)S(1)} %bitcast.1), channel_id=1, replica_groups=mesh['gx'=8,'yz'=4] {'gx','yz'}, dimensions={0} | all-to-all | bytes 16384 | tf_op jit(solution)/shard_map/all_to_all | solution.py:632
  59.8 0.6 reduce_sum.9
  (2 shorter events, 0.0 us)
Async XLA Ops:
  0.6 17.4 %copy-start.3 = (s32[64]{0:T(128)S(1)}, s32[64]{0:T(128)}, u32[]{:S(2)}) copy-start(s32[64]{0:T(128)} %pos.3) | copy-start | bytes 772
  2.8 7.8 %collective-permute-start = (f32[2,24,128]{2,1,0:T(8,128)S(1)}, f32[2,24,128]{2,1,0:T(8,128)S(1)}, u32[]{:S(2)}, u32[]{:S(2)}) collective-permute-start(f32[2,24,128]{2,1,0:T(8,128)S(1)} %get-tuple-element.22), channel_id=1, source_target_pairs={{0,4},{4,8},{8,12},{12,16},{16,20},{20,24},{24,28},{28,0},{1,5},{5... | collective-permute-start | bytes 73736 | tf_op jit(solution)/shard_map/ppermute | solution.py:564
  5.8 4.8 %collective-permute-start.1 = (f32[2,24,128]{2,1,0:T(8,128)S(1)}, f32[2,24,128]{2,1,0:T(8,128)S(1)}, u32[]{:S(2)}, u32[]{:S(2)}) collective-permute-start(f32[2,24,128]{2,1,0:T(8,128)S(1)} %get-tuple-element.23), channel_id=1, source_target_pairs={{4,0},{8,4},{12,8},{16,12},{20,16},{24,20},{28,24},{0,28},{5,1},{9... | collective-permute-start | bytes 73736 | tf_op jit(solution)/shard_map/ppermute | solution.py:565
  23.5 15.8 %copy-start = (f32[2,19,16,512]{3,2,1,0:T(8,128)S(1)}, f32[2,19,16,512]{3,2,1,0:T(8,128)}, u32[]{:S(2)}) copy-start(f32[2,19,16,512]{3,2,1,0:T(8,128)} %pops.1) | copy-start | bytes 3735556
  23.5 15.8 %copy-start.1 = (s32[2,16,512]{2,1,0:T(8,128)S(1)}, s32[2,16,512]{2,1,0:T(8,128)}, u32[]{:S(2)}) copy-start(s32[2,16,512]{2,1,0:T(8,128)} %mask.1) | copy-start | bytes 196612
  23.5 15.7 %copy-start.2 = (s32[2,16,512]{2,1,0:T(8,128)S(1)}, s32[2,16,512]{2,1,0:T(8,128)}, u32[]{:S(2)}) copy-start(s32[2,16,512]{2,1,0:T(8,128)} %patch.1) | copy-start | bytes 196612
  23.5 6.9 %collective-permute-start.2 = (f32[2,40,128]{2,1,0:T(8,128)S(1)}, f32[2,40,128]{2,1,0:T(8,128)S(1)}, u32[]{:S(2)}, u32[]{:S(2)}) collective-permute-start(f32[2,40,128]{2,1,0:T(8,128)S(1)} %get-tuple-element.28), channel_id=1, source_target_pairs={{0,4},{4,8},{8,12},{12,16},{16,20},{20,24},{24,28},{28,0},{1,5},{5... | collective-permute-start | bytes 122888 | tf_op jit(solution)/shard_map/ppermute | solution.py:564
  24.8 5.6 %collective-permute-start.3 = (f32[2,40,128]{2,1,0:T(8,128)S(1)}, f32[2,40,128]{2,1,0:T(8,128)S(1)}, u32[]{:S(2)}, u32[]{:S(2)}) collective-permute-start(f32[2,40,128]{2,1,0:T(8,128)S(1)} %get-tuple-element.29), channel_id=1, source_target_pairs={{4,0},{8,4},{12,8},{16,12},{20,16},{24,20},{28,24},{0,28},{5,1},{9... | collective-permute-start | bytes 122888 | tf_op jit(solution)/shard_map/ppermute | solution.py:565

commit v3 on v2

--- a/solution.py
+++ b/solution.py
@@ -559,10 +559,17 @@
 
 def exchange(pack, ab, up, dn):
     n = lax.axis_size("gx")
-    forward = [(i, (i + 1) % n) for i in range(n)]
-    backward = [(j, i) for i, j in forward]
-    below = lax.ppermute(up, "gx", forward)
-    above = lax.ppermute(dn, "gx", backward)
+    m = lax.axis_size("yz")
+    hop = []
+    for q in range(m):
+        for g in range(n):
+            to = g + 1 if q % 2 == 0 else g - 1
+            hop.append((g * m + q, to * m + q if 0 <= to < n else g * m + (q ^ 1)))
+    is_even = lax.axis_index("yz") % 2 == 0
+    one = lax.ppermute(jnp.where(is_even, up, dn), ("gx", "yz"), hop)
+    two = lax.ppermute(jnp.where(is_even, dn, up), ("gx", "yz"), [(j, i) for i, j in hop])
+    below = jnp.where(is_even, one, two)
+    above = jnp.where(is_even, two, one)
     block = jnp.concatenate([ab, below, above], axis=1)
     return lax.all_gather(block, "yz", axis=0, tiled=True)
 

time: 60.6 us -> 58 us (0.957)
  starting transfers between devices: 10.9 us -> 5.51 us
  waiting for transfers between devices: 3.76 us -> 7.82 us
  blocking collectives: 28.7 us -> 27.3 us
    ppermute x4, starting transfers between devices: 10.9 us -> 5.51 us  [the longest x2 5.5 us: exchange(): one = lax.ppermute(jnp.where(is_even, up, dn), ('gx', 'yz'), hop)]
    ppermute x4, waiting for transfers between devices: 3.76 us -> 7.82 us  [the longest x2 4.63 us: exchange(): lax.ppermute(jnp.where(is_even, dn, up), ('gx', 'yz'), [(j, i) for i, j i...]
    all_to_all x1, blocking collectives: 12.4 us -> 11.5 us  [body(): lax.all_to_all(sums.reshape(parts, patch_dev), ('gx', 'yz'), 0, 0, tiled=...]
  transfers between devices with their start and end apart: 4 -> 4, of which waited for: 2 -> 4; matrix products, arithmetic and copies ran while one was open for 0% -> 0% of each run, Pallas kernels for 0% -> 0%
where the time goes in v3:
time: 58 us; the launch traced here: 57.8 us
  blocking collectives  27.3 us (47%)
  Pallas kernels  15.7 us (27%)
  waiting for transfers between devices  7.82 us (13%)
  starting transfers between devices  5.51 us (10%)
  between operations  0.74 us (1%)
  other arithmetic  0.62 us (1%)
    all_gather x2, blocking collectives, exchange(): return lax.all_gather(block, 'yz', axis=0, tiled=True)  15.8 us
    pallas_call x3, Pallas kernels, call(): pl.pallas_call(kernel, out_shape=[jax.ShapeDtypeStruct(s, jnp.float32) fo...  15.7 us
    all_to_all x1, blocking collectives, body(): lax.all_to_all(sums.reshape(parts, patch_dev), ('gx', 'yz'), 0, 0, tiled=...  11.5 us
    ppermute x2, starting transfers between devices, exchange(): one = lax.ppermute(jnp.where(is_even, up, dn), ('gx', 'yz'), hop)  5.5 us
    ppermute x2, waiting for transfers between devices, exchange(): lax.ppermute(jnp.where(is_even, dn, up), ('gx', 'yz'), [(j, i) for i, j i...  4.63 us
    ppermute x2, waiting for transfers between devices, exchange(): one = lax.ppermute(jnp.where(is_even, up, dn), ('gx', 'yz'), hop)  3.19 us
  transfers between devices with their start and end apart: 4, of which 4 were waited for; matrix products, arithmetic and copies ran while one was open for 0% of the time, Pallas kernels for 0%

profile of v3, /device:TPU:0, one launch (start us, length us, event | category | flops | bytes accessed | tf_op | source)
XLA Modules:
  0.0 57.8 jit_solution(9109724259147771596)
XLA Ops:
  0.6 0.0 copy-start.3
  0.7 2.1 %shard_map.85 = (f32[2,19,16,512]{3,2,1,0:T(8,128)S(1)}, f32[2,16,512]{2,1,0:T(8,128)S(1)}, f32[2,16,512]{2,1,0:T(8,128)S(1)}, f32[2,80,128]{2,1,0:T(8,128)S(1)}...) custom-call(f32[2,19,16,512]{3,2,1,0:T(8,128)} %pops.1, s32[2,16,512]{2,1,0:T(8,128)} %mask.1, ...), custom_call_target="tpu_custom_call" | custom-call | tf_op jit(solution)/shard_map/pallas_call | solution.py:548
  2.8 3.0 %collective-permute-start = (f32[2,24,128]{2,1,0:T(8,128)S(1)}, f32[2,24,128]{2,1,0:T(8,128)S(1)}, u32[]{:S(2)}, u32[]{:S(2)}) collective-permute-start(f32[2,24,128]{2,1,0:T(8,128)S(1)} %get-tuple-element.39), channel_id=1, source_target_pairs={{0,4},{4,8},{8,12},{12,16},{16,20},{20,24},{24,28},{28,29},{1,0},{... | collective-permute-start | bytes 73736 | tf_op jit(solution)/shard_map/ppermute | solution.py:569
  5.8 0.0 collective-permute-start.1
  5.8 1.5 %collective-permute-done = f32[2,24,128]{2,1,0:T(8,128)S(1)} collective-permute-done((f32[2,24,128]{2,1,0:T(8,128)S(1)}, f32[2,24,128]{2,1,0:T(8,128)S(1)}, u32[]{:S(2)}, u32[]{:S(2)}) %collective-permute-start) | collective-permute-done | bytes 24608 | tf_op jit(solution)/shard_map/ppermute | solution.py:569
  7.3 2.3 %collective-permute-done.1 = f32[2,24,128]{2,1,0:T(8,128)S(1)} collective-permute-done((f32[2,24,128]{2,1,0:T(8,128)S(1)}, f32[2,24,128]{2,1,0:T(8,128)S(1)}, u32[]{:S(2)}, u32[]{:S(2)}) %collective-permute-start.1) | collective-permute-done | bytes 24608 | tf_op jit(solution)/shard_map/ppermute | solution.py:570
  9.7 7.2 %all_gather.6.around = f32[8,128,128]{2,1,0:T(8,128)S(1)} all-gather(f32[2,128,128]{2,1,0:T(8,128)S(1)} %pad_maximum_fusion.1), channel_id=1, replica_groups=mesh['gx'=8,'yz'=4] {'yz'}, dimensions={0}, use_global_device_ids=true | all-gather | bytes 655360 | tf_op jit(solution)/shard_map/all_gather | solution.py:574
  16.9 0.0 copy-done.3
  16.9 5.4 %shard_map.86 = (f32[2,19,16,512]{3,2,1,0:T(8,128)S(1)}, f32[2,19,16,512]{3,2,1,0:T(8,128)S(1)}, f32[2,16,512]{2,1,0:T(8,128)S(1)}, f32[2,144,128]{2,1,0:T(8,128...) custom-call(s32[64]{0:T(128)S(1)} %copy-done.3, f32[2,19,16,512]{3,2,1,0:T(8,128)S(1)} %get-tuple-element.18.post0, ...), custom_call_target="tpu_custom_call" | custom-call | tf_op jit(solution)/shard_map/pallas_call | solution.py:548
  22.3 0.0 copy-start
  22.3 0.0 copy-start.1
  22.3 0.0 copy-start.2
  22.3 2.5 %collective-permute-start.2 = (f32[2,40,128]{2,1,0:T(8,128)S(1)}, f32[2,40,128]{2,1,0:T(8,128)S(1)}, u32[]{:S(2)}, u32[]{:S(2)}) collective-permute-start(f32[2,40,128]{2,1,0:T(8,128)S(1)} %get-tuple-element.35), channel_id=1, source_target_pairs={{0,4},{4,8},{8,12},{12,16},{16,20},{20,24},{24,28},{28,29},{1,0},{... | collective-permute-start | bytes 122888 | tf_op jit(solution)/shard_map/ppermute | solution.py:569
  24.8 0.0 collective-permute-start.3
  24.9 1.7 %collective-permute-done.2 = f32[2,40,128]{2,1,0:T(8,128)S(1)} collective-permute-done((f32[2,40,128]{2,1,0:T(8,128)S(1)}, f32[2,40,128]{2,1,0:T(8,128)S(1)}, u32[]{:S(2)}, u32[]{:S(2)}) %collective-permute-start.2) | collective-permute-done | bytes 40992 | tf_op jit(solution)/shard_map/ppermute | solution.py:569
  26.5 2.3 %collective-permute-done.3 = f32[2,40,128]{2,1,0:T(8,128)S(1)} collective-permute-done((f32[2,40,128]{2,1,0:T(8,128)S(1)}, f32[2,40,128]{2,1,0:T(8,128)S(1)}, u32[]{:S(2)}, u32[]{:S(2)}) %collective-permute-start.3) | collective-permute-done | bytes 40992 | tf_op jit(solution)/shard_map/ppermute | solution.py:570
  28.9 8.6 %all_gather.7.around = f32[8,224,128]{2,1,0:T(8,128)S(1)} all-gather(f32[2,224,128]{2,1,0:T(8,128)S(1)} %pad_maximum_fusion), channel_id=1, replica_groups=mesh['gx'=8,'yz'=4] {'yz'}, dimensions={0}, use_global_device_ids=true | all-gather | bytes 1146880 | tf_op jit(solution)/shard_map/all_gather | solution.py:574
  37.5 0.0 copy-done
  37.5 0.0 copy-done.1
  37.5 0.0 copy-done.2
  37.5 8.1 %shard_map.87 = (f32[2,19,16,512]{3,2,1,0:T(8,128)}, f32[2,19,16,512]{3,2,1,0:T(8,128)}, f32[16,128]{1,0:T(8,128)S(1)}) custom-call(s32[64]{0:T(128)S(1)} %copy-done.3, f32[2,19,16,512]{3,2,1,0:T(8,128)S(1)} %get-tuple-element.24.post1, f32[2,19,16,512]{3,2,1,0:T(8,128)S(1)} %get-tuple-element.25.adj1, f32[2,19,16,512]{3,2,1,0:T(8,128)S(1)} %copy-done, ...), custom_call_target="tpu_custom_call" | custom-call | tf_op jit(solution)/shard_map/pallas_call | solution.py:548
  45.7 0.1 all_to_all.6
  45.7 11.5 %all_to_all.9 = f32[32,1,64]{2,1,0:T(1,128)S(1)} all-to-all(f32[32,1,64]{2,1,0:T(1,128)S(1)} %bitcast.1), channel_id=1, replica_groups=mesh['gx'=8,'yz'=4] {'gx','yz'}, dimensions={0} | all-to-all | bytes 16384 | tf_op jit(solution)/shard_map/all_to_all | solution.py:639
  57.2 0.6 reduce_sum.9
  (6 shorter events, 0.1 us)
Async XLA Ops:
  0.6 16.2 %copy-start.3 = (s32[64]{0:T(128)S(1)}, s32[64]{0:T(128)}, u32[]{:S(2)}) copy-start(s32[64]{0:T(128)} %pos.3) | copy-start | bytes 772
  2.8 4.5 %collective-permute-start = (f32[2,24,128]{2,1,0:T(8,128)S(1)}, f32[2,24,128]{2,1,0:T(8,128)S(1)}, u32[]{:S(2)}, u32[]{:S(2)}) collective-permute-start(f32[2,24,128]{2,1,0:T(8,128)S(1)} %get-tuple-element.39), channel_id=1, source_target_pairs={{0,4},{4,8},{8,12},{12,16},{16,20},{20,24},{24,28},{28,29},{1,0},{... | collective-permute-start | bytes 73736 | tf_op jit(solution)/shard_map/ppermute | solution.py:569
  5.8 3.8 %collective-permute-start.1 = (f32[2,24,128]{2,1,0:T(8,128)S(1)}, f32[2,24,128]{2,1,0:T(8,128)S(1)}, u32[]{:S(2)}, u32[]{:S(2)}) collective-permute-start(f32[2,24,128]{2,1,0:T(8,128)S(1)} %get-tuple-element.40), channel_id=1, source_target_pairs={{4,0},{8,4},{12,8},{16,12},{20,16},{24,20},{28,24},{29,28},{0,1},{... | collective-permute-start | bytes 73736 | tf_op jit(solution)/shard_map/ppermute | solution.py:570
  22.3 15.3 %copy-start = (f32[2,19,16,512]{3,2,1,0:T(8,128)S(1)}, f32[2,19,16,512]{3,2,1,0:T(8,128)}, u32[]{:S(2)}) copy-start(f32[2,19,16,512]{3,2,1,0:T(8,128)} %pops.1) | copy-start | bytes 3735556
  22.3 15.2 %copy-start.1 = (s32[2,16,512]{2,1,0:T(8,128)S(1)}, s32[2,16,512]{2,1,0:T(8,128)}, u32[]{:S(2)}) copy-start(s32[2,16,512]{2,1,0:T(8,128)} %mask.1) | copy-start | bytes 196612
  22.3 15.2 %copy-start.2 = (s32[2,16,512]{2,1,0:T(8,128)S(1)}, s32[2,16,512]{2,1,0:T(8,128)}, u32[]{:S(2)}) copy-start(s32[2,16,512]{2,1,0:T(8,128)} %patch.1) | copy-start | bytes 196612
  22.3 4.2 %collective-permute-start.2 = (f32[2,40,128]{2,1,0:T(8,128)S(1)}, f32[2,40,128]{2,1,0:T(8,128)S(1)}, u32[]{:S(2)}, u32[]{:S(2)}) collective-permute-start(f32[2,40,128]{2,1,0:T(8,128)S(1)} %get-tuple-element.35), channel_id=1, source_target_pairs={{0,4},{4,8},{8,12},{12,16},{16,20},{20,24},{24,28},{28,29},{1,0},{... | collective-permute-start | bytes 122888 | tf_op jit(solution)/shard_map/ppermute | solution.py:569
  24.8 4.0 %collective-permute-start.3 = (f32[2,40,128]{2,1,0:T(8,128)S(1)}, f32[2,40,128]{2,1,0:T(8,128)S(1)}, u32[]{:S(2)}, u32[]{:S(2)}) collective-permute-start(f32[2,40,128]{2,1,0:T(8,128)S(1)} %get-tuple-element.36), channel_id=1, source_target_pairs={{4,0},{8,4},{12,8},{16,12},{20,16},{24,20},{28,24},{29,28},{0,1},{... | collective-permute-start | bytes 122888 | tf_op jit(solution)/shard_map/ppermute | solution.py:570

commit v4 on v3

--- a/solution.py
+++ b/solution.py
@@ -206,32 +206,10 @@
     return out, dsolid
 
 
-def load_chunk(ref, t, i, r, c):
-    return ref[t, i, pl.ds(8 * r, 8), pl.ds(c, LANES)]
-
-
-def for_chunks(count, run):
-    def step(k, carry):
-        t = k // (2 * COLS)
-        r = (k // COLS) % 2
-        c = pl.multiple_of((k % COLS) * LANES, LANES)
-        run(t, pl.multiple_of(r * 8, 8), c)
-        return carry
-
-    lax.fori_loop(0, count * 2 * COLS, step, 0)
-
-
-def chunk(ref, t, i, r, c):
-    return ref[t, i, pl.ds(r, 8), pl.ds(c, LANES)]
-
-
-def plane_chunk(ref, t, r, c):
-    return ref[t, pl.ds(r, 8), pl.ds(c, LANES)]
-
-
-def write_faces(pack, t, get, ab_ref, up_ref, dn_ref):
+def face_jobs(pack, t, get, ab_ref, up_ref, dn_ref):
     lane = lane_iota((TL, LANES))
-    for col in range(pack.a_cols):
+
+    def a_col(col):
         acc = jnp.zeros((TL, LANES), jnp.float32)
         for side in (-1, 1):
             for key in pack.lists[(1, side)]:
@@ -248,7 +226,8 @@
                     )
                 acc = jnp.where((lane >> 5) == j % 4, part, acc)
         ab_ref[t, pack.a_row + TL * col : pack.a_row + TL * (col + 1), :] = acc
-    for col in range(pack.b_cols):
+
+    def b_col(col):
         acc = jnp.zeros((TL, LANES), jnp.float32)
         for half in range(pack.fold):
             src = col + half * pack.b_cols
@@ -259,14 +238,43 @@
                     part = lane_roll(part, j if side < 0 else j - (TB - 1))
                     acc = jnp.where((lane & (TB - 1)) == j, part, acc)
         ab_ref[t, pack.b_row + TL * col : pack.b_row + TL * (col + 1), :] = acc
-    for side, ref in ((1, up_ref), (-1, dn_ref)):
+
+    def l_rows(side, ref, key):
         row = TL - 1 if side > 0 else 0
-        for key in pack.lists[(0, side)]:
-            j = pack.slot(0, side, key)
-            for col in range(COLS):
-                ref[t, j * COLS + col : j * COLS + col + 1, :] = get(
-                    key, slice(row, row + 1), slice(LANES * col, LANES * (col + 1))
-                )
+        j = pack.slot(0, side, key)
+        for col in range(COLS):
+            ref[t, j * COLS + col : j * COLS + col + 1, :] = get(
+                key, slice(row, row + 1), slice(LANES * col, LANES * (col + 1))
+            )
+
+    return (
+        [functools.partial(a_col, c) for c in range(pack.a_cols)]
+        + [functools.partial(b_col, c) for c in range(pack.b_cols)]
+        + [
+            functools.partial(l_rows, side, ref, key)
+            for side, ref in ((1, up_ref), (-1, dn_ref))
+            for key in pack.lists[(0, side)]
+        ]
+    )
+
+
+def weave(lists):
+    jobs = [
+        ((n + 0.5) / len(items), k, job)
+        for k, items in enumerate(lists)
+        for n, job in enumerate(items)
+    ]
+    for _, _, job in sorted(jobs, key=lambda job: job[:2]):
+        job()
+
+
+def staged(count, stages, after=None):
+    for step in range(count + len(stages) - 1):
+        live = [(k, step - k) for k in range(len(stages)) if 0 <= step - k < count]
+        weave([stages[k](t) for k, t in live])
+        if after is not None:
+            for k, t in live:
+                after(k, t)
 
 
 def build_inverse(pos_ref, inv_ref, n_layers, group):
@@ -297,7 +305,11 @@
             ok = (ta >= 0) & (ta < n_cross) & (tb >= 0) & (tb < count)
             s = inv_ref[d[0] + 1, jnp.where(ok, ta * count + tb, group)]
             found = ok & (s >= 0)
-            self.where[d] = (jnp.where(found, s, 0), found)
+            s = jnp.where(found, s, 0)
+            owner, slot = s // count, s % count
+            half = ((owner ^ lax.axis_index("yz")) >> 1) & 1
+            block = ((owner & 1) * 2 + half) * count + slot
+            self.where[d] = (block, found)
         self.planes = {}
 
     def a_face(self, d, side, key, fill):
@@ -353,12 +365,17 @@
             j = self.pack.slot(2, cb, key)
             shift = -1 - j if cb > 0 else TB - j
             plane, found = self.b_plane((0, 0, -cb))
-            face = jnp.where(found, lane_roll(plane, shift), fill)
+            plane = jnp.where(found, plane, fill)
             if ca:
-                plane, found = self.b_plane((0, -ca, -cb))
-                corner = jnp.where(found, lane_roll(plane, shift), fill)
-                at = (TA - 1 if ca > 0 else 0) + (-1 if cb > 0 else 1)
-                face = jnp.where((lane >> 5) == at % TA, corner, face)
+                corner, found = self.b_plane((0, -ca, -cb))
+                part = slice(CELLS - LANES, CELLS) if ca > 0 else slice(0, LANES)
+                corner = jnp.where(found, corner[:, part], fill)
+                corner = jnp.where(hit, corner, plane[:, part])
+                plane = jnp.concatenate(
+                    [plane[:, : CELLS - LANES], corner] if ca > 0 else [corner, plane[:, LANES:]],
+                    axis=1,
+                )
+            face = lane_roll(plane, shift)
             x = jnp.where(edge_b, face, x)
         if cl:
             row = self.l_row((-cl, 0, 0), cl, key, fill)
@@ -370,8 +387,14 @@
                 corner = self.l_row((-cl, 0, -cb), cl, key, fill)
                 corner = lane_roll(corner, -TB if cb > 0 else TB)
                 row = jnp.where((lane_r & (TB - 1)) == (TB - 1 if cb > 0 else 0), corner, row)
-            at = TL - 1 if cl > 0 else 0
-            x = jnp.where(row_iota(shape) == at, jnp.broadcast_to(row, shape), x)
+            half = (TL // 2, CELLS)
+            if cl > 0:
+                low, edge = x[: TL // 2], x[TL // 2 :]
+            else:
+                edge, low = x[: TL // 2], x[TL // 2 :]
+            hit = row_iota(half) == (TL // 2 - 1 if cl > 0 else 0)
+            edge = jnp.where(hit, jnp.broadcast_to(row, half), edge)
+            x = jnp.concatenate([low, edge] if cl > 0 else [edge, low], axis=0)
         return row_roll(lane_roll(x, TB * ca + cb), cl)
 
 
@@ -396,30 +419,29 @@
         copy.wait()
     solid[...] = mask[...].astype(jnp.float32) * frac[...]
 
-    for n, (t, r) in enumerate(halves):
-        large[n].wait()
-
-        def run(k, carry, t=t, r=8 * r):
-            c = pl.multiple_of(k * LANES, LANES)
-            f = [chunk(pops, t, i, r, c) for i in range(Q)]
-            out = collide(f, plane_chunk(solid, t, r, c), *flow(f))
+    def collides(t):
+        def run(r, c):
+            if c == 0:
+                large[halves.index((t, r))].wait()
+            rows = slice(8 * r, 8 * r + 8)
+            lanes = slice(LANES * c, LANES * (c + 1))
+            f = [pops[t, i, rows, lanes] for i in range(Q)]
+            out = collide(f, solid[t, rows, lanes], *flow(f))
             for i in range(Q):
-                post[t, i, pl.ds(r, 8), pl.ds(c, LANES)] = out[i]
-            return carry
-
-        lax.fori_loop(0, COLS, run, 0)
-    small[2].wait()
-
-    def faces(t, carry):
+                post[t, i, rows, lanes] = out[i]
+
+        return [functools.partial(run, r, c) for r in range(2) for c in range(COLS)]
+
+    def faces(t):
         def get(key, rows, lanes):
             if key[0] == "probe":
                 return probe[t, rows, lanes]
             return post[t, key[1], rows, lanes]
 
-        write_faces(PACK1, t, get, ab, up, dn)
-        return carry
-
-    lax.fori_loop(0, count, faces, 0)
+        return face_jobs(PACK1, t, get, ab, up, dn)
+
+    small[2].wait()
+    staged(count, [collides, faces])
 
 
 def second_kernel(
@@ -429,43 +451,48 @@
     count = post0.shape[0]
     build_inverse(pos, inv, n_layers, n_cross * count)
 
-    def move(t, carry):
+    def moves(t):
         near = Neighbours(PACK1, t, around, pos, inv, n_cross, count)
-        for i in range(Q):
+
+        def forward(i):
             state[t, i] = near.stream(post0[t, i], vel(i), ("post", i), WEIGHTS[i])
-        for n, i in enumerate(AXIAL):
+
+        def backward(n, i):
             back = tuple(-v for v in vel(i))
             moved = near.stream(probe[t], back, ("probe", 0), 0.0)
             pulled[t, n] = moved if vel(i)[0] > 0 else -moved
-        return carry
-
-    lax.fori_loop(0, count, move, 0)
-
-    def run(t, r, c):
-        f = [chunk(state, t, i, r, c) for i in range(Q)]
-        solid = plane_chunk(solid_in, t, r, c)
-        rho, u, base = flow(f)
-        out = collide(f, solid, rho, u, base)
-        for i in range(Q):
-            post1[t, i, pl.ds(r, 8), pl.ds(c, LANES)] = out[i]
-        g = [None] * Q
-        for n, i in enumerate(AXIAL):
-            g[i] = chunk(pulled, t, n, r, c)
-        back, ds = pullback(f, solid, rho, u, base, g)
-        for i in range(Q):
-            adj1[t, i, pl.ds(r, 8), pl.ds(c, LANES)] = back[i]
-        dsolid[t, pl.ds(r, 8), pl.ds(c, LANES)] = ds
-
-    for_chunks(count, run)
-
-    def faces(t, carry):
+
+        return [functools.partial(forward, i) for i in range(Q)] + [
+            functools.partial(backward, n, i) for n, i in enumerate(AXIAL)
+        ]
+
+    def runs(t):
+        def run(r, c):
+            rows = slice(8 * r, 8 * r + 8)
+            lanes = slice(LANES * c, LANES * (c + 1))
+            f = [state[t, i, rows, lanes] for i in range(Q)]
+            solid = solid_in[t, rows, lanes]
+            rho, u, base = flow(f)
+            out = collide(f, solid, rho, u, base)
+            for i in range(Q):
+                post1[t, i, rows, lanes] = out[i]
+            g = [None] * Q
+            for n, i in enumerate(AXIAL):
+                g[i] = pulled[t, n, rows, lanes]
+            back, ds = pullback(f, solid, rho, u, base, g)
+            for i in range(Q):
+                adj1[t, i, rows, lanes] = back[i]
+            dsolid[t, rows, lanes] = ds
+
+        return [functools.partial(run, r, c) for r in range(2) for c in range(COLS)]
+
+    def faces(t):
         def get(key, rows, lanes):
             return (post1 if key[0] == "post" else adj1)[t, key[1], rows, lanes]
 
-        write_faces(PACK2, t, get, ab, up, dn)
-        return carry
-
-    lax.fori_loop(0, count, faces, 0)
+        return face_jobs(PACK2, t, get, ab, up, dn)
+
+    staged(count, [moves, runs, faces])
 
 
 def third_kernel(
@@ -476,68 +503,76 @@
     group = n_cross * count
     build_inverse(pos, inv, n_layers, group)
 
-    def move(t, carry):
-        near = Neighbours(PACK2, t, around, pos, inv, n_cross, count)
-        for i in range(Q):
-            moved = near.stream(post1[t, i], vel(i), ("post", i), WEIGHTS[i])
-            final[t, i] = jnp.where(near.alive, moved, 0.0)
-            back = tuple(-v for v in vel(i))
-            pulled[t, i] = near.stream(adj1[t, i], back, ("adj", i), 0.0)
-        return carry
-
-    lax.fori_loop(0, count, move, 0)
-    out_final = pltpu.make_async_copy(final, final_out, sems.at[0])
-    out_final.start()
     base_slot = lax.axis_index("gx") * group + lax.axis_index("yz") * count
-
-    def run(t, r, c):
-        alive = pos[base_slot + t] >= 0
-        f = [chunk(pops, t, i, r, c) for i in range(Q)]
-        g = [chunk(pulled, t, i, r, c) for i in range(Q)]
-        wall = plane_chunk(mask, t, r, c).astype(jnp.float32)
-        solid = plane_chunk(solid_in, t, r, c)
-        rho, u, base = flow(f)
-        back, ds = pullback(f, solid, rho, u, base, g)
-        for i in range(Q):
-            start[t, i, pl.ds(r, 8), pl.ds(c, LANES)] = jnp.where(alive, back[i], 0.0)
-        total = wall * (ds + plane_chunk(dsolid, t, r, c))
-        weighted[t, pl.ds(r, 8), pl.ds(c, LANES)] = jnp.where(alive, total, 0.0)
-
-    for_chunks(count, run)
-    out_start = pltpu.make_async_copy(start, start_out, sems.at[1])
-    out_start.start()
-
     n_high = sums.shape[0]
     high_iota = lax.broadcasted_iota(jnp.int32, (n_high, CELLS), 0)
     low_iota = lax.broadcasted_iota(jnp.int32, (LANES, CELLS), 0)
-
-    def add(k, acc):
-        t = k // 2
-        r = pl.multiple_of((k % 2) * 8, 8)
-        ids8 = patch[t, pl.ds(r, 8), :]
-        w8 = weighted[t, pl.ds(r, 8), :]
-        for n in range(8):
-            ids = ids8[n : n + 1]
-            w = w8[n : n + 1]
-            w1 = w.astype(jnp.bfloat16).astype(jnp.float32)
-            w2 = (w - w1).astype(jnp.bfloat16).astype(jnp.float32)
-            w3 = w - w1 - w2
-            high = high_iota == (ids >> 7)
-            left = jnp.concatenate(
-                [jnp.where(high, part, 0.0).astype(jnp.bfloat16) for part in (w1, w2, w3)],
-                axis=0,
-            )
-            right = jnp.where(low_iota == (ids & (LANES - 1)), 1.0, 0.0).astype(jnp.bfloat16)
-            acc = acc + lax.dot_general(
-                left, right, (((1,), (1,)), ((), ())), preferred_element_type=jnp.float32
-            )
-        return acc
-
-    acc = lax.fori_loop(
-        0, count * 2, add, jnp.zeros((3 * n_high, LANES), jnp.float32)
-    )
-    out_final.wait()
-    out_start.wait()
+    total = [jnp.zeros((3 * n_high, LANES), jnp.float32)]
+
+    def moves(t):
+        near = Neighbours(PACK2, t, around, pos, inv, n_cross, count)
+
+        def forward(i):
+            moved = near.stream(post1[t, i], vel(i), ("post", i), WEIGHTS[i])
+            final[t, i] = jnp.where(near.alive, moved, 0.0)
+
+        def backward(i):
+            back = tuple(-v for v in vel(i))
+            pulled[t, i] = near.stream(adj1[t, i], back, ("adj", i), 0.0)
+
+        order = [functools.partial(backward, i) for i in range(Q)]
+        return order + [functools.partial(forward, i) for i in range(Q)]
+
+    def runs(t):
+        alive = pos[base_slot + t] >= 0
+
+        def run(r, c):
+            rows = slice(8 * r, 8 * r + 8)
+            lanes = slice(LANES * c, LANES * (c + 1))
+            f = [pops[t, i, rows, lanes] for i in range(Q)]
+            g = [pulled[t, i, rows, lanes] for i in range(Q)]
+            wall = mask[t, rows, lanes].astype(jnp.float32)
+            solid = solid_in[t, rows, lanes]
+            rho, u, base = flow(f)
+            back, ds = pullback(f, solid, rho, u, base, g)
+            for i in range(Q):
+                start[t, i, rows, lanes] = jnp.where(alive, back[i], 0.0)
+            part = wall * (ds + dsolid[t, rows, lanes])
+            weighted[t, rows, lanes] = jnp.where(alive, part, 0.0)
+
+        return [functools.partial(run, r, c) for r in range(2) for c in range(COLS)]
+
+    def add(t, r):
+        ids = patch[t, r : r + 1, :]
+        w = weighted[t, r : r + 1, :]
+        w1 = w.astype(jnp.bfloat16).astype(jnp.float32)
+        w2 = (w - w1).astype(jnp.bfloat16).astype(jnp.float32)
+        w3 = w - w1 - w2
+        high = high_iota == (ids >> 7)
+        left = jnp.concatenate(
+            [jnp.where(high, part, 0.0).astype(jnp.bfloat16) for part in (w1, w2, w3)],
+            axis=0,
+        )
+        right = jnp.where(low_iota == (ids & (LANES - 1)), 1.0, 0.0).astype(jnp.bfloat16)
+        total[0] = total[0] + lax.dot_general(
+            left, right, (((1,), (1,)), ((), ())), preferred_element_type=jnp.float32
+        )
+
+    def adds(t):
+        return [functools.partial(add, t, r) for r in range(TL)]
+
+    copies = []
+
+    def send(k, t):
+        if k < 2:
+            src, dst = ((final, final_out), (start, start_out))[k]
+            copies.append(pltpu.make_async_copy(src.at[t], dst.at[t], sems.at[len(copies)]))
+            copies[-1].start()
+
+    staged(count, [moves, runs, adds], send)
+    for copy in copies:
+        copy.wait()
+    acc = total[0]
     sums[...] = acc[:n_high] + acc[n_high : 2 * n_high] + acc[2 * n_high :]
 
 
@@ -557,9 +592,10 @@
     )(*args)
 
 
-def exchange(pack, ab, up, dn):
+def exchange(ab, up, dn):
     n = lax.axis_size("gx")
     m = lax.axis_size("yz")
+    assert m == 4
     hop = []
     for q in range(m):
         for g in range(n):
@@ -568,10 +604,18 @@
     is_even = lax.axis_index("yz") % 2 == 0
     one = lax.ppermute(jnp.where(is_even, up, dn), ("gx", "yz"), hop)
     two = lax.ppermute(jnp.where(is_even, dn, up), ("gx", "yz"), [(j, i) for i, j in hop])
-    below = jnp.where(is_even, one, two)
-    above = jnp.where(is_even, two, one)
-    block = jnp.concatenate([ab, below, above], axis=1)
-    return lax.all_gather(block, "yz", axis=0, tiled=True)
+    across = [(q, q ^ 2) for q in range(m)]
+    ab_far = lax.ppermute(ab, "yz", across)
+    l_near = jnp.concatenate(
+        [jnp.where(is_even, one, two), jnp.where(is_even, two, one)], axis=1
+    )
+    l_far = lax.ppermute(l_near, "yz", across)
+    both = jnp.concatenate(
+        [jnp.concatenate([ab, l_near], axis=1), jnp.concatenate([ab_far, l_far], axis=1)],
+        axis=0,
+    )
+    pairs = [[0, 1], [2, 3]]
+    return lax.all_gather(both, "yz", axis=0, tiled=True, axis_index_groups=pairs)
 
 
 def body(pops_start, tile_pos, wall_mask, wall_frac, patch_id, probe):
@@ -608,7 +652,7 @@
         ),
         in_hbm=range(4),
     )
-    around = exchange(PACK1, ab, up, dn)
+    around = exchange(ab, up, dn)
     post1, adj1, dsolid, ab, up, dn = call(
         functools.partial(second_kernel, dims),
         [field, field, plane] + packs(PACK2),
@@ -620,7 +664,7 @@
         (tile_pos, post0, solid, probe_kept, around),
         in_smem=(0,),
     )
-    around = exchange(PACK2, ab, up, dn)
+    around = exchange(ab, up, dn)
     pops_final, adjoint_start, sums = call(
         functools.partial(third_kernel, dims),
         [field, field, (n_high, LANES)],
@@ -630,7 +674,7 @@
             pltpu.VMEM(field, jnp.float32),
             pltpu.VMEM(plane, jnp.float32),
             inverse,
-            pltpu.SemaphoreType.DMA((2,)),
+            pltpu.SemaphoreType.DMA((2 * count,)),
         ],
         (tile_pos, post1, adj1, pops_start, wall_mask, solid, patch_id, dsolid, around),
         in_smem=(0,),

time: 58 us -> 53.1 us (0.916)
  blocking collectives: 27.3 us -> 16.4 us
  starting transfers between devices: 5.51 us -> 11.7 us
  Pallas kernels: 15.7 us -> 13 us
  waiting for transfers between devices: 7.82 us -> 10.3 us
    all_gather x2, blocking collectives: 15.8 us -> 4.64 us  [exchange(): lax.all_gather(both, 'yz', axis=0, tiled=True, axis_index_groups=pairs)]
    ppermute x0 -> x4, starting transfers between devices: none -> 6.21 us  [the longest x2 3.17 us: exchange(): l_far = lax.ppermute(l_near, 'yz', across)]
    ppermute x0 -> x4, waiting for transfers between devices: none -> 5.5 us  [the longest x2 5.49 us: exchange(): l_far = lax.ppermute(l_near, 'yz', across)]
    ppermute x2, waiting for transfers between devices: 3.19 us -> 0.47 us  [exchange(): one = lax.ppermute(jnp.where(is_even, up, dn), ('gx', 'yz'), hop)]
    pallas_call x3, Pallas kernels: 15.7 us -> 13 us  [call(): pl.pallas_call(kernel, out_shape=[jax.ShapeDtypeStruct(s, jnp.float32) fo...]
  transfers between devices with their start and end apart: 4 -> 8, of which waited for: 4 -> 5; matrix products, arithmetic and copies ran while one was open for 0% -> 0% of each run, Pallas kernels for 0% -> 0%
where the time goes in v4:
time: 53.1 us; the launch traced here: 52.9 us
  blocking collectives  16.4 us (31%)
  Pallas kernels  13 us (24%)
  starting transfers between devices  11.7 us (22%)
  waiting for transfers between devices  10.3 us (19%)
  between operations  0.74 us (1%)
  other arithmetic  0.67 us (1%)
    pallas_call x3, Pallas kernels, call(): pl.pallas_call(kernel, out_shape=[jax.ShapeDtypeStruct(s, jnp.float32) fo...  13 us
    all_to_all x1, blocking collectives, body(): lax.all_to_all(sums.reshape(parts, patch_dev), ('gx', 'yz'), 0, 0, tiled=...  11.8 us
    ppermute x2, starting transfers between devices, exchange(): one = lax.ppermute(jnp.where(is_even, up, dn), ('gx', 'yz'), hop)  5.5 us
    ppermute x2, waiting for transfers between devices, exchange(): l_far = lax.ppermute(l_near, 'yz', across)  5.49 us
    all_gather x2, blocking collectives, exchange(): lax.all_gather(both, 'yz', axis=0, tiled=True, axis_index_groups=pairs)  4.64 us
    ppermute x2, waiting for transfers between devices, exchange(): lax.ppermute(jnp.where(is_even, dn, up), ('gx', 'yz'), [(j, i) for i, j i...  4.31 us
    ppermute x2, starting transfers between devices, exchange(): l_far = lax.ppermute(l_near, 'yz', across)  3.17 us
    ppermute x2, starting transfers between devices, exchange(): ab_far = lax.ppermute(ab, 'yz', across)  3.04 us
  transfers between devices with their start and end apart: 8, of which 5 were waited for; matrix products, arithmetic and copies ran while one was open for 0% of the time, Pallas kernels for 0%

profile of v4, /device:TPU:0, one launch (start us, length us, event | category | flops | bytes accessed | tf_op | source)
XLA Modules:
  0.0 52.9 jit_solution(12003702834219588180)
XLA Ops:
  0.6 0.0 copy-start.3
  0.7 2.1 %shard_map.85 = (f32[2,19,16,512]{3,2,1,0:T(8,128)S(1)}, f32[2,16,512]{2,1,0:T(8,128)S(1)}, f32[2,16,512]{2,1,0:T(8,128)S(1)}, f32[2,80,128]{2,1,0:T(8,128)S(1)}...) custom-call(f32[2,19,16,512]{3,2,1,0:T(8,128)} %pops.1, s32[2,16,512]{2,1,0:T(8,128)} %mask.1, ...), custom_call_target="tpu_custom_call" | custom-call | tf_op jit(solution)/shard_map/pallas_call | solution.py:583
  2.8 3.0 %collective-permute-start = (f32[2,24,128]{2,1,0:T(8,128)S(1)}, f32[2,24,128]{2,1,0:T(8,128)S(1)}, u32[]{:S(2)}, u32[]{:S(2)}) collective-permute-start(f32[2,24,128]{2,1,0:T(8,128)S(1)} %get-tuple-element.39), channel_id=1, source_target_pairs={{0,4},{4,8},{8,12},{12,16},{16,20},{20,24},{24,28},{28,29},{1,0},{... | collective-permute-start | bytes 73736 | tf_op jit(solution)/shard_map/ppermute | solution.py:605
  5.8 0.0 collective-permute-start.1
  5.8 1.5 %collective-permute-start.2 = (f32[2,80,128]{2,1,0:T(8,128)S(1)}, f32[2,80,128]{2,1,0:T(8,128)S(1)}, u32[]{:S(2)}, u32[]{:S(2)}) collective-permute-start(f32[2,80,128]{2,1,0:T(8,128)S(1)} %get-tuple-element.21), channel_id=1, source_target_pairs={{0,2},{1,3},{2,0},{3,1},{4,6},{5,7},{6,4},{7,5},{8,10},{9,11},{10,... | collective-permute-start | bytes 245768 | tf_op jit(solution)/shard_map/ppermute | solution.py:608
  7.3 0.0 collective-permute-done
  7.3 2.3 %collective-permute-done.1 = f32[2,24,128]{2,1,0:T(8,128)S(1)} collective-permute-done((f32[2,24,128]{2,1,0:T(8,128)S(1)}, f32[2,24,128]{2,1,0:T(8,128)S(1)}, u32[]{:S(2)}, u32[]{:S(2)}) %collective-permute-start.1) | collective-permute-done | bytes 24608 | tf_op jit(solution)/shard_map/ppermute | solution.py:606
  9.6 1.6 %collective-permute-start.3 = (f32[2,48,128]{2,1,0:T(8,128)S(1)}, f32[2,48,128]{2,1,0:T(8,128)S(1)}, u32[]{:S(2)}, u32[]{:S(2)}) collective-permute-start(f32[2,48,128]{2,1,0:T(8,128)S(1)} %pad_maximum_fusion.1), channel_id=1, source_target_pairs={{0,2},{1,3},{2,0},{3,1},{4,6},{5,7},{6,4},{7,5},{8,10},{9,11},{10,... | collective-permute-start | bytes 147464 | tf_op jit(solution)/shard_map/ppermute | solution.py:612
  11.2 2.6 %collective-permute-done.3 = f32[2,48,128]{2,1,0:T(8,128)S(1)} collective-permute-done((f32[2,48,128]{2,1,0:T(8,128)S(1)}, f32[2,48,128]{2,1,0:T(8,128)S(1)}, u32[]{:S(2)}, u32[]{:S(2)}) %collective-permute-start.3) | collective-permute-done | bytes 49184 | tf_op jit(solution)/shard_map/ppermute | solution.py:612
  13.8 0.0 collective-permute-done.2
  13.8 2.2 %all_gather.6.around = f32[8,128,128]{2,1,0:T(8,128)S(1)} all-gather(f32[4,128,128]{2,1,0:T(8,128)S(1)} %maximum_maximum_fusion.1), channel_id=1, replica_groups={{0,1},{2,3},{4,5},{6,7},{8,9},{10,11},{12,13},{14,15},{16,17},{18,19},{..., dimensions={0}, use_global_device_ids=true | all-gather | bytes 786432 | tf_op jit(solution)/shard_map/all_gather | solution.py:618
  16.0 0.0 copy-done.3
  16.0 4.9 %shard_map.86 = (f32[2,19,16,512]{3,2,1,0:T(8,128)S(1)}, f32[2,19,16,512]{3,2,1,0:T(8,128)S(1)}, f32[2,16,512]{2,1,0:T(8,128)S(1)}, f32[2,144,128]{2,1,0:T(8,128...) custom-call(s32[64]{0:T(128)S(1)} %copy-done.3, f32[2,19,16,512]{3,2,1,0:T(8,128)S(1)} %get-tuple-element.18.post0, ...), custom_call_target="tpu_custom_call" | custom-call | tf_op jit(solution)/shard_map/pallas_call | solution.py:583
  20.9 2.5 %collective-permute-start.4 = (f32[2,40,128]{2,1,0:T(8,128)S(1)}, f32[2,40,128]{2,1,0:T(8,128)S(1)}, u32[]{:S(2)}, u32[]{:S(2)}) collective-permute-start(f32[2,40,128]{2,1,0:T(8,128)S(1)} %get-tuple-element.35), channel_id=1, source_target_pairs={{0,4},{4,8},{8,12},{12,16},{16,20},{20,24},{24,28},{28,29},{1,0},{... | collective-permute-start | bytes 122888 | tf_op jit(solution)/shard_map/ppermute | solution.py:605
  23.4 0.0 collective-permute-start.5
  23.4 1.5 %collective-permute-start.6 = (f32[2,144,128]{2,1,0:T(8,128)S(1)}, f32[2,144,128]{2,1,0:T(8,128)S(1)}, u32[]{:S(2)}, u32[]{:S(2)}) collective-permute-start(f32[2,144,128]{2,1,0:T(8,128)S(1)} %get-tuple-element.27), channel_id=1, source_target_pairs={{0,2},{1,3},{2,0},{3,1},{4,6},{5,7},{6,4},{7,5},{8,10},{9,11},{10,... | collective-permute-start | bytes 442376 | tf_op jit(solution)/shard_map/ppermute | solution.py:608
  24.9 0.5 collective-permute-done.4
  25.4 2.0 %collective-permute-done.5 = f32[2,40,128]{2,1,0:T(8,128)S(1)} collective-permute-done((f32[2,40,128]{2,1,0:T(8,128)S(1)}, f32[2,40,128]{2,1,0:T(8,128)S(1)}, u32[]{:S(2)}, u32[]{:S(2)}) %collective-permute-start.5) | collective-permute-done | bytes 40992 | tf_op jit(solution)/shard_map/ppermute | solution.py:606
  27.4 0.0 copy-start
  27.4 0.0 copy-start.1
  27.4 0.0 copy-start.2
  27.5 1.6 %collective-permute-start.7 = (f32[2,80,128]{2,1,0:T(8,128)S(1)}, f32[2,80,128]{2,1,0:T(8,128)S(1)}, u32[]{:S(2)}, u32[]{:S(2)}) collective-permute-start(f32[2,80,128]{2,1,0:T(8,128)S(1)} %pad_maximum_fusion), channel_id=1, source_target_pairs={{0,2},{1,3},{2,0},{3,1},{4,6},{5,7},{6,4},{7,5},{8,10},{9,11},{10,... | collective-permute-start | bytes 245768 | tf_op jit(solution)/shard_map/ppermute | solution.py:612
  29.1 2.9 %collective-permute-done.7 = f32[2,80,128]{2,1,0:T(8,128)S(1)} collective-permute-done((f32[2,80,128]{2,1,0:T(8,128)S(1)}, f32[2,80,128]{2,1,0:T(8,128)S(1)}, u32[]{:S(2)}, u32[]{:S(2)}) %collective-permute-start.7) | collective-permute-done | bytes 81952 | tf_op jit(solution)/shard_map/ppermute | solution.py:612
  32.0 0.0 collective-permute-done.6
  32.0 2.5 %all_gather.7.around = f32[8,224,128]{2,1,0:T(8,128)S(1)} all-gather(f32[4,224,128]{2,1,0:T(8,128)S(1)} %maximum_maximum_fusion), channel_id=1, replica_groups={{0,1},{2,3},{4,5},{6,7},{8,9},{10,11},{12,13},{14,15},{16,17},{18,19},{..., dimensions={0}, use_global_device_ids=true | all-gather | bytes 1376256 | tf_op jit(solution)/shard_map/all_gather | solution.py:618
  34.5 0.0 copy-done
  34.5 0.0 copy-done.1
  34.5 0.0 copy-done.2
  34.5 6.0 %shard_map.87 = (f32[2,19,16,512]{3,2,1,0:T(8,128)}, f32[2,19,16,512]{3,2,1,0:T(8,128)}, f32[16,128]{1,0:T(8,128)S(1)}) custom-call(s32[64]{0:T(128)S(1)} %copy-done.3, f32[2,19,16,512]{3,2,1,0:T(8,128)S(1)} %get-tuple-element.24.post1, f32[2,19,16,512]{3,2,1,0:T(8,128)S(1)} %get-tuple-element.25.adj1, f32[2,19,16,512]{3,2,1,0:T(8,128)S(1)} %copy-done, ...), custom_call_target="tpu_custom_call" | custom-call | tf_op jit(solution)/shard_map/pallas_call | solution.py:583
  40.5 0.1 all_to_all.6
  40.5 11.8 %all_to_all.9 = f32[32,1,64]{2,1,0:T(1,128)S(1)} all-to-all(f32[32,1,64]{2,1,0:T(1,128)S(1)} %bitcast.1), channel_id=1, replica_groups=mesh['gx'=8,'yz'=4] {'gx','yz'}, dimensions={0} | all-to-all | bytes 16384 | tf_op jit(solution)/shard_map/all_to_all | solution.py:683
  52.3 0.6 %reduce_sum.9 = f32[64]{0:T(128)} reduce(f32[32,1,64]{2,1,0:T(1,128)S(1)} %all_to_all.9, f32[]{:T(128)} %constant.21.clone.1), dimensions={0,1}, to_apply=%region_0.1 | reduce | flops 1984 | bytes 8452 | tf_op jit(solution)/shard_map/reduce_sum | solution.py:686
  (8 shorter events, 0.1 us)
Async XLA Ops:
  0.6 15.3 %copy-start.3 = (s32[64]{0:T(128)S(1)}, s32[64]{0:T(128)}, u32[]{:S(2)}) copy-start(s32[64]{0:T(128)} %pos.3) | copy-start | bytes 772
  2.8 4.5 %collective-permute-start = (f32[2,24,128]{2,1,0:T(8,128)S(1)}, f32[2,24,128]{2,1,0:T(8,128)S(1)}, u32[]{:S(2)}, u32[]{:S(2)}) collective-permute-start(f32[2,24,128]{2,1,0:T(8,128)S(1)} %get-tuple-element.39), channel_id=1, source_target_pairs={{0,4},{4,8},{8,12},{12,16},{16,20},{20,24},{24,28},{28,29},{1,0},{... | collective-permute-start | bytes 73736 | tf_op jit(solution)/shard_map/ppermute | solution.py:605
  5.8 3.8 %collective-permute-start.1 = (f32[2,24,128]{2,1,0:T(8,128)S(1)}, f32[2,24,128]{2,1,0:T(8,128)S(1)}, u32[]{:S(2)}, u32[]{:S(2)}) collective-permute-start(f32[2,24,128]{2,1,0:T(8,128)S(1)} %get-tuple-element.40), channel_id=1, source_target_pairs={{4,0},{8,4},{12,8},{16,12},{20,16},{24,20},{28,24},{29,28},{0,1},{... | collective-permute-start | bytes 73736 | tf_op jit(solution)/shard_map/ppermute | solution.py:606
  5.8 8.0 %collective-permute-start.2 = (f32[2,80,128]{2,1,0:T(8,128)S(1)}, f32[2,80,128]{2,1,0:T(8,128)S(1)}, u32[]{:S(2)}, u32[]{:S(2)}) collective-permute-start(f32[2,80,128]{2,1,0:T(8,128)S(1)} %get-tuple-element.21), channel_id=1, source_target_pairs={{0,2},{1,3},{2,0},{3,1},{4,6},{5,7},{6,4},{7,5},{8,10},{9,11},{10,... | collective-permute-start | bytes 245768 | tf_op jit(solution)/shard_map/ppermute | solution.py:608
  9.6 4.2 %collective-permute-start.3 = (f32[2,48,128]{2,1,0:T(8,128)S(1)}, f32[2,48,128]{2,1,0:T(8,128)S(1)}, u32[]{:S(2)}, u32[]{:S(2)}) collective-permute-start(f32[2,48,128]{2,1,0:T(8,128)S(1)} %pad_maximum_fusion.1), channel_id=1, source_target_pairs={{0,2},{1,3},{2,0},{3,1},{4,6},{5,7},{6,4},{7,5},{8,10},{9,11},{10,... | collective-permute-start | bytes 147464 | tf_op jit(solution)/shard_map/ppermute | solution.py:612
  20.9 4.5 %collective-permute-start.4 = (f32[2,40,128]{2,1,0:T(8,128)S(1)}, f32[2,40,128]{2,1,0:T(8,128)S(1)}, u32[]{:S(2)}, u32[]{:S(2)}) collective-permute-start(f32[2,40,128]{2,1,0:T(8,128)S(1)} %get-tuple-element.35), channel_id=1, source_target_pairs={{0,4},{4,8},{8,12},{12,16},{16,20},{20,24},{24,28},{28,29},{1,0},{... | collective-permute-start | bytes 122888 | tf_op jit(solution)/shard_map/ppermute | solution.py:605
  23.4 4.0 %collective-permute-start.5 = (f32[2,40,128]{2,1,0:T(8,128)S(1)}, f32[2,40,128]{2,1,0:T(8,128)S(1)}, u32[]{:S(2)}, u32[]{:S(2)}) collective-permute-start(f32[2,40,128]{2,1,0:T(8,128)S(1)} %get-tuple-element.36), channel_id=1, source_target_pairs={{4,0},{8,4},{12,8},{16,12},{20,16},{24,20},{28,24},{29,28},{0,1},{... | collective-permute-start | bytes 122888 | tf_op jit(solution)/shard_map/ppermute | solution.py:606
  23.4 8.6 %collective-permute-start.6 = (f32[2,144,128]{2,1,0:T(8,128)S(1)}, f32[2,144,128]{2,1,0:T(8,128)S(1)}, u32[]{:S(2)}, u32[]{:S(2)}) collective-permute-start(f32[2,144,128]{2,1,0:T(8,128)S(1)} %get-tuple-element.27), channel_id=1, source_target_pairs={{0,2},{1,3},{2,0},{3,1},{4,6},{5,7},{6,4},{7,5},{8,10},{9,11},{10,... | collective-permute-start | bytes 442376 | tf_op jit(solution)/shard_map/ppermute | solution.py:608
  27.4 7.1 %copy-start = (f32[2,19,16,512]{3,2,1,0:T(8,128)S(1)}, f32[2,19,16,512]{3,2,1,0:T(8,128)}, u32[]{:S(2)}) copy-start(f32[2,19,16,512]{3,2,1,0:T(8,128)} %pops.1) | copy-start | bytes 3735556
  27.4 7.1 %copy-start.1 = (s32[2,16,512]{2,1,0:T(8,128)S(1)}, s32[2,16,512]{2,1,0:T(8,128)}, u32[]{:S(2)}) copy-start(s32[2,16,512]{2,1,0:T(8,128)} %mask.1) | copy-start | bytes 196612
  27.4 7.1 %copy-start.2 = (s32[2,16,512]{2,1,0:T(8,128)S(1)}, s32[2,16,512]{2,1,0:T(8,128)}, u32[]{:S(2)}) copy-start(s32[2,16,512]{2,1,0:T(8,128)} %patch.1) | copy-start | bytes 196612
  27.5 4.5 %collective-permute-start.7 = (f32[2,80,128]{2,1,0:T(8,128)S(1)}, f32[2,80,128]{2,1,0:T(8,128)S(1)}, u32[]{:S(2)}, u32[]{:S(2)}) collective-permute-start(f32[2,80,128]{2,1,0:T(8,128)S(1)} %pad_maximum_fusion), channel_id=1, source_target_pairs={{0,2},{1,3},{2,0},{3,1},{4,6},{5,7},{6,4},{7,5},{8,10},{9,11},{10,... | collective-permute-start | bytes 245768 | tf_op jit(solution)/shard_map/ppermute | solution.py:612

commit v5 on v4

--- a/solution.py
+++ b/solution.py
@@ -206,7 +206,7 @@
     return out, dsolid
 
 
-def face_jobs(pack, t, get, ab_ref, up_ref, dn_ref):
+def side_jobs(pack, t, get, ab_ref):
     lane = lane_iota((TL, LANES))
 
     def a_col(col):
@@ -239,6 +239,12 @@
                     acc = jnp.where((lane & (TB - 1)) == j, part, acc)
         ab_ref[t, pack.b_row + TL * col : pack.b_row + TL * (col + 1), :] = acc
 
+    return [functools.partial(a_col, c) for c in range(pack.a_cols)] + [
+        functools.partial(b_col, c) for c in range(pack.b_cols)
+    ]
+
+
+def end_jobs(pack, t, get, up_ref, dn_ref):
     def l_rows(side, ref, key):
         row = TL - 1 if side > 0 else 0
         j = pack.slot(0, side, key)
@@ -247,15 +253,33 @@
                 key, slice(row, row + 1), slice(LANES * col, LANES * (col + 1))
             )
 
-    return (
-        [functools.partial(a_col, c) for c in range(pack.a_cols)]
-        + [functools.partial(b_col, c) for c in range(pack.b_cols)]
-        + [
-            functools.partial(l_rows, side, ref, key)
-            for side, ref in ((1, up_ref), (-1, dn_ref))
-            for key in pack.lists[(0, side)]
-        ]
-    )
+    return [
+        functools.partial(l_rows, side, ref, key)
+        for side, ref in ((1, up_ref), (-1, dn_ref))
+        for key in pack.lists[(0, side)]
+    ]
+
+
+def first_sides(post, probe, ab):
+    def sides(t):
+        def get(key, rows, lanes):
+            if key[0] == "probe":
+                return probe[t, rows, lanes]
+            return post[t, key[1], rows, lanes]
+
+        return side_jobs(PACK1, t, get, ab)
+
+    staged(post.shape[0], [sides])
+
+
+def second_sides(post1, adj1, ab):
+    def sides(t):
+        def get(key, rows, lanes):
+            return (post1 if key[0] == "post" else adj1)[t, key[1], rows, lanes]
+
+        return side_jobs(PACK2, t, get, ab)
+
+    staged(post1.shape[0], [sides])
 
 
 def weave(lists):
@@ -312,12 +336,12 @@
             self.where[d] = (block, found)
         self.planes = {}
 
-    def a_face(self, d, side, key, fill):
+    def a_face(self, d, side, key, fill, to):
         k, found = self.where[d]
         j = self.pack.slot(1, side, key)
         row = self.pack.a_row + TL * (j // 4)
         face = self.ref[k, row : row + TL, :]
-        face = lane_roll(face, (LANES - TB if side > 0 else 0) - TB * (j % 4))
+        face = lane_roll(face, to - TB * (j % 4))
         return jnp.where(found, face, fill)
 
     def b_plane(self, d):
@@ -345,60 +369,88 @@
         )
         return jnp.where(found, row, fill)
 
-    def stream(self, own, c, key, fill):
+    def enter(self, x, c, key, fill):
         cl, ca, cb = c
         shape = (TL, CELLS)
-        lane = lane_iota(shape)
-        edge_b = (lane & (TB - 1)) == (TB - 1 if cb > 0 else 0)
-        edge_a = (lane >> 5) == (TA - 1 if ca > 0 else 0)
-        x = own
         if ca:
-            face = self.a_face((0, -ca, 0), ca, key, fill)
-            part = slice(CELLS - LANES, CELLS) if ca > 0 else slice(0, LANES)
+            to = 0 if ca > 0 else LANES - TB
+            face = row_roll(self.a_face((0, -ca, 0), ca, key, fill, to + cb), cl)
             inner = lane_iota((TL, LANES))
-            hit = inner >= LANES - TB if ca > 0 else inner < TB
+            hit = inner < TB if ca > 0 else inner >= LANES - TB
+            part = slice(0, LANES) if ca > 0 else slice(CELLS - LANES, CELLS)
             face = jnp.where(hit, face, x[:, part])
             x = jnp.concatenate(
-                [x[:, : CELLS - LANES], face] if ca > 0 else [face, x[:, LANES:]], axis=1
+                [face, x[:, LANES:]] if ca > 0 else [x[:, : CELLS - LANES], face], axis=1
             )
         if cb:
-            j = self.pack.slot(2, cb, key)
-            shift = -1 - j if cb > 0 else TB - j
             plane, found = self.b_plane((0, 0, -cb))
             plane = jnp.where(found, plane, fill)
             if ca:
                 corner, found = self.b_plane((0, -ca, -cb))
                 part = slice(CELLS - LANES, CELLS) if ca > 0 else slice(0, LANES)
+                inner = lane_iota((TL, LANES))
+                hit = inner >= LANES - TB if ca > 0 else inner < TB
                 corner = jnp.where(found, corner[:, part], fill)
                 corner = jnp.where(hit, corner, plane[:, part])
                 plane = jnp.concatenate(
                     [plane[:, : CELLS - LANES], corner] if ca > 0 else [corner, plane[:, LANES:]],
                     axis=1,
                 )
-            face = lane_roll(plane, shift)
-            x = jnp.where(edge_b, face, x)
+            at = 0 if cb > 0 else TB - 1
+            face = lane_roll(plane, TB * ca + at - self.pack.slot(2, cb, key))
+            x = jnp.where((lane_iota(shape) & (TB - 1)) == at, row_roll(face, cl), x)
         if cl:
             row = self.l_row((-cl, 0, 0), cl, key, fill)
-            lane_r = lane_iota((1, CELLS))
+            lane = lane_iota((1, CELLS))
             if ca:
                 corner = self.l_row((-cl, -ca, 0), cl, key, fill)
-                row = jnp.where((lane_r >> 5) == (TA - 1 if ca > 0 else 0), corner, row)
+                row = jnp.where((lane >> 5) == (TA - 1 if ca > 0 else 0), corner, row)
+            row = lane_roll(row, TB * ca + cb)
             if cb:
                 corner = self.l_row((-cl, 0, -cb), cl, key, fill)
-                corner = lane_roll(corner, -TB if cb > 0 else TB)
-                row = jnp.where((lane_r & (TB - 1)) == (TB - 1 if cb > 0 else 0), corner, row)
+                corner = lane_roll(corner, -cb * (TB - 1))
+                row = jnp.where((lane & (TB - 1)) == (0 if cb > 0 else TB - 1), corner, row)
             half = (TL // 2, CELLS)
+            low, high = x[: TL // 2], x[TL // 2 :]
+            row = jnp.broadcast_to(row, half)
             if cl > 0:
-                low, edge = x[: TL // 2], x[TL // 2 :]
+                low = jnp.where(row_iota(half) == 0, row, low)
             else:
-                edge, low = x[: TL // 2], x[TL // 2 :]
-            hit = row_iota(half) == (TL // 2 - 1 if cl > 0 else 0)
-            edge = jnp.where(hit, jnp.broadcast_to(row, half), edge)
-            x = jnp.concatenate([low, edge] if cl > 0 else [edge, low], axis=0)
-        return row_roll(lane_roll(x, TB * ca + cb), cl)
-
-
-def first_kernel(pops_in, mask_in, frac_in, probe_in, post, solid, probe, ab, up, dn, pops, mask, frac, sems):
+                high = jnp.where(row_iota(half) == TL // 2 - 1, row, high)
+            x = jnp.concatenate([low, high], axis=0)
+        return x
+
+
+def shifted(x, c):
+    return row_roll(lane_roll(x, TB * c[1] + c[2]), c[0])
+
+
+def against(i):
+    return tuple(-v for v in vel(i))
+
+
+def first_own(post, probe, after, moved, back):
+    del after
+    for t in range(post.shape[0]):
+        for i in range(Q):
+            moved[t, i] = shifted(post[t, i], vel(i))
+        for n, i in enumerate(AXIAL):
+            back[t, n] = shifted(probe[t], against(i))
+
+
+def second_own(post1, adj1, patch, after, moved, back, onehot):
+    del after
+    low_iota = lax.broadcasted_iota(jnp.int32, (LANES, CELLS), 0)
+    for t in range(post1.shape[0]):
+        for i in range(Q):
+            moved[t, i] = shifted(post1[t, i], vel(i))
+            back[t, i] = shifted(adj1[t, i], against(i))
+            if i < TL:
+                low = patch[t, i : i + 1, :] & (LANES - 1)
+                onehot[t, i] = jnp.where(low_iota == low, 1.0, 0.0).astype(jnp.bfloat16)
+
+
+def first_kernel(pops_in, mask_in, frac_in, probe_in, post, solid, probe, up, dn, pops, mask, frac, sems):
     count = pops.shape[0]
     small = [
         pltpu.make_async_copy(src, dst, sems.at[n])
@@ -438,29 +490,28 @@
                 return probe[t, rows, lanes]
             return post[t, key[1], rows, lanes]
 
-        return face_jobs(PACK1, t, get, ab, up, dn)
+        return end_jobs(PACK1, t, get, up, dn)
 
     small[2].wait()
     staged(count, [collides, faces])
 
 
 def second_kernel(
-    dims, pos, post0, solid_in, probe, around, post1, adj1, dsolid, ab, up, dn, state, pulled, inv
+    dims, pos, moved, back, solid_in, around, post1, adj1, dsolid, up, dn, state, pulled, inv
 ):
     n_layers, n_cross = dims
-    count = post0.shape[0]
+    count = solid_in.shape[0]
     build_inverse(pos, inv, n_layers, n_cross * count)
 
     def moves(t):
         near = Neighbours(PACK1, t, around, pos, inv, n_cross, count)
 
         def forward(i):
-            state[t, i] = near.stream(post0[t, i], vel(i), ("post", i), WEIGHTS[i])
+            state[t, i] = near.enter(moved[t, i], vel(i), ("post", i), WEIGHTS[i])
 
         def backward(n, i):
-            back = tuple(-v for v in vel(i))
-            moved = near.stream(probe[t], back, ("probe", 0), 0.0)
-            pulled[t, n] = moved if vel(i)[0] > 0 else -moved
+            x = near.enter(back[t, n], against(i), ("probe", 0), 0.0)
+            pulled[t, n] = x if vel(i)[0] > 0 else -x
 
         return [functools.partial(forward, i) for i in range(Q)] + [
             functools.partial(backward, n, i) for n, i in enumerate(AXIAL)
@@ -479,9 +530,9 @@
             g = [None] * Q
             for n, i in enumerate(AXIAL):
                 g[i] = pulled[t, n, rows, lanes]
-            back, ds = pullback(f, solid, rho, u, base, g)
+            df, ds = pullback(f, solid, rho, u, base, g)
             for i in range(Q):
-                adj1[t, i, rows, lanes] = back[i]
+                adj1[t, i, rows, lanes] = df[i]
             dsolid[t, rows, lanes] = ds
 
         return [functools.partial(run, r, c) for r in range(2) for c in range(COLS)]
@@ -490,13 +541,13 @@
         def get(key, rows, lanes):
             return (post1 if key[0] == "post" else adj1)[t, key[1], rows, lanes]
 
-        return face_jobs(PACK2, t, get, ab, up, dn)
+        return end_jobs(PACK2, t, get, up, dn)
 
     staged(count, [moves, runs, faces])
 
 
 def third_kernel(
-    dims, pos, post1, adj1, pops, mask, solid_in, patch, dsolid, around, final_out, start_out, sums, final, start, pulled, weighted, inv, sems
+    dims, pos, moved, back, onehot, pops, mask, solid_in, patch, dsolid, around, final_out, start_out, sums, final, start, pulled, weighted, inv, sems
 ):
     n_layers, n_cross = dims
     count = pops.shape[0]
@@ -506,19 +557,17 @@
     base_slot = lax.axis_index("gx") * group + lax.axis_index("yz") * count
     n_high = sums.shape[0]
     high_iota = lax.broadcasted_iota(jnp.int32, (n_high, CELLS), 0)
-    low_iota = lax.broadcasted_iota(jnp.int32, (LANES, CELLS), 0)
     total = [jnp.zeros((3 * n_high, LANES), jnp.float32)]
 
     def moves(t):
         near = Neighbours(PACK2, t, around, pos, inv, n_cross, count)
 
         def forward(i):
-            moved = near.stream(post1[t, i], vel(i), ("post", i), WEIGHTS[i])
-            final[t, i] = jnp.where(near.alive, moved, 0.0)
+            x = near.enter(moved[t, i], vel(i), ("post", i), WEIGHTS[i])
+            final[t, i] = jnp.where(near.alive, x, 0.0)
 
         def backward(i):
-            back = tuple(-v for v in vel(i))
-            pulled[t, i] = near.stream(adj1[t, i], back, ("adj", i), 0.0)
+            pulled[t, i] = near.enter(back[t, i], against(i), ("adj", i), 0.0)
 
         order = [functools.partial(backward, i) for i in range(Q)]
         return order + [functools.partial(forward, i) for i in range(Q)]
@@ -534,9 +583,9 @@
             wall = mask[t, rows, lanes].astype(jnp.float32)
             solid = solid_in[t, rows, lanes]
             rho, u, base = flow(f)
-            back, ds = pullback(f, solid, rho, u, base, g)
+            df, ds = pullback(f, solid, rho, u, base, g)
             for i in range(Q):
-                start[t, i, rows, lanes] = jnp.where(alive, back[i], 0.0)
+                start[t, i, rows, lanes] = jnp.where(alive, df[i], 0.0)
             part = wall * (ds + dsolid[t, rows, lanes])
             weighted[t, rows, lanes] = jnp.where(alive, part, 0.0)
 
@@ -553,9 +602,8 @@
             [jnp.where(high, part, 0.0).astype(jnp.bfloat16) for part in (w1, w2, w3)],
             axis=0,
         )
-        right = jnp.where(low_iota == (ids & (LANES - 1)), 1.0, 0.0).astype(jnp.bfloat16)
         total[0] = total[0] + lax.dot_general(
-            left, right, (((1,), (1,)), ((), ())), preferred_element_type=jnp.float32
+            left, onehot[t, r], (((1,), (1,)), ((), ())), preferred_element_type=jnp.float32
         )
 
     def adds(t):
@@ -576,15 +624,19 @@
     sums[...] = acc[:n_high] + acc[n_high : 2 * n_high] + acc[2 * n_high :]
 
 
-def call(kernel, outs, scratch, args, in_smem=(), in_hbm=(), out_hbm=()):
+def call(kernel, outs, scratch, args, in_smem=(), in_hbm=(), in_any=(), out_hbm=(), types={}):
     vmem = pl.BlockSpec(memory_space=pltpu.VMEM)
     hbm = pl.BlockSpec(memory_space=pltpu.HBM)
+    free = pl.BlockSpec(memory_space=pl.ANY)
     smem = pl.BlockSpec(memory_space=pltpu.SMEM)
     return pl.pallas_call(
         kernel,
-        out_shape=[jax.ShapeDtypeStruct(s, jnp.float32) for s in outs],
+        out_shape=[
+            jax.ShapeDtypeStruct(s, types.get(n, jnp.float32)) for n, s in enumerate(outs)
+        ],
         in_specs=[
-            smem if n in in_smem else hbm if n in in_hbm else vmem for n in range(len(args))
+            smem if n in in_smem else hbm if n in in_hbm else free if n in in_any else vmem
+            for n in range(len(args))
         ],
         out_specs=[hbm if n in out_hbm else vmem for n in range(len(outs))],
         scratch_shapes=scratch,
@@ -606,16 +658,20 @@
     two = lax.ppermute(jnp.where(is_even, dn, up), ("gx", "yz"), [(j, i) for i, j in hop])
     across = [(q, q ^ 2) for q in range(m)]
     ab_far = lax.ppermute(ab, "yz", across)
+    one_far = lax.ppermute(one, "yz", across)
+    two_far = lax.ppermute(two, "yz", across)
     l_near = jnp.concatenate(
         [jnp.where(is_even, one, two), jnp.where(is_even, two, one)], axis=1
     )
-    l_far = lax.ppermute(l_near, "yz", across)
+    l_far = jnp.concatenate(
+        [jnp.where(is_even, one_far, two_far), jnp.where(is_even, two_far, one_far)], axis=1
+    )
     both = jnp.concatenate(
         [jnp.concatenate([ab, l_near], axis=1), jnp.concatenate([ab_far, l_far], axis=1)],
         axis=0,
     )
     pairs = [[0, 1], [2, 3]]
-    return lax.all_gather(both, "yz", axis=0, tiled=True, axis_index_groups=pairs)
+    return two, lax.all_gather(both, "yz", axis=0, tiled=True, axis_index_groups=pairs)
 
 
 def body(pops_start, tile_pos, wall_mask, wall_frac, patch_id, probe):
@@ -630,16 +686,15 @@
     n_high = patch_dev * parts // LANES
     inverse = pltpu.SMEM((3, n_cross * count + 1), jnp.int32)
 
-    def packs(pack):
-        return [
-            (count, pack.ab_rows, LANES),
-            (count, pack.l_rows, LANES),
-            (count, pack.l_rows, LANES),
-        ]
-
-    post0, solid, probe_kept, ab, up, dn = call(
+    def ends(pack):
+        return [(count, pack.l_rows, LANES)] * 2
+
+    def sides(pack):
+        return [(count, pack.ab_rows, LANES)]
+
+    post0, solid, probe_kept, up, dn = call(
         first_kernel,
-        [field, plane, plane] + packs(PACK1),
+        [field, plane, plane] + ends(PACK1),
         [
             pltpu.VMEM(field, jnp.float32),
             pltpu.VMEM(plane, jnp.int32),
@@ -652,19 +707,31 @@
         ),
         in_hbm=range(4),
     )
-    around = exchange(ab, up, dn)
-    post1, adj1, dsolid, ab, up, dn = call(
+    (ab,) = call(first_sides, sides(PACK1), [], (post0, probe_kept))
+    token, around = exchange(ab, up, dn)
+    axial = (count, len(AXIAL)) + plane[1:]
+    moved, back = call(first_own, [field, axial], [], (post0, probe_kept, token), in_any=(2,))
+    post1, adj1, dsolid, up, dn = call(
         functools.partial(second_kernel, dims),
-        [field, field, plane] + packs(PACK2),
+        [field, field, plane] + ends(PACK2),
         [
             pltpu.VMEM(field, jnp.float32),
             pltpu.VMEM((count, len(AXIAL)) + plane[1:], jnp.float32),
             inverse,
         ],
-        (tile_pos, post0, solid, probe_kept, around),
+        (tile_pos, moved, back, solid, around),
         in_smem=(0,),
     )
-    around = exchange(ab, up, dn)
+    (ab,) = call(second_sides, sides(PACK2), [], (post1, adj1))
+    token, around = exchange(ab, up, dn)
+    moved, back, onehot = call(
+        second_own,
+        [field, field, (count, TL, LANES, CELLS)],
+        [],
+        (post1, adj1, patch_id, token),
+        in_any=(3,),
+        types={2: jnp.bfloat16},
+    )
     pops_final, adjoint_start, sums = call(
         functools.partial(third_kernel, dims),
         [field, field, (n_high, LANES)],
@@ -676,7 +743,7 @@
             inverse,
             pltpu.SemaphoreType.DMA((2 * count,)),
         ],
-        (tile_pos, post1, adj1, pops_start, wall_mask, solid, patch_id, dsolid, around),
+        (tile_pos, moved, back, onehot, pops_start, wall_mask, solid, patch_id, dsolid, around),
         in_smem=(0,),
         out_hbm=(0, 1),
     )

time: 53.1 us -> 48.9 us (0.921)
  waiting for transfers between devices: 10.3 us -> 3.39 us
  starting transfers between devices: 11.7 us -> 14.3 us
  blocking collectives: 16.4 us -> 17.5 us
  Pallas kernels: 13 us -> 12 us
    ppermute x2 -> x4, waiting for transfers between devices: 5.49 us -> 2.11 us  [the longest x2 2.1 us: exchange(): two_far = lax.ppermute(two, 'yz', across)]
    ppermute x2, waiting for transfers between devices: 4.31 us -> 1.27 us  [exchange(): lax.ppermute(jnp.where(is_even, dn, up), ('gx', 'yz'), [(j, i) for i, j i...]
    ppermute x2 -> x4, starting transfers between devices: 3.17 us -> 5.66 us  [the longest x2 3.04 us: exchange(): two_far = lax.ppermute(two, 'yz', across)]
    all_to_all x1, blocking collectives: 11.8 us -> 12.8 us  [body(): lax.all_to_all(sums.reshape(parts, patch_dev), ('gx', 'yz'), 0, 0, tiled=...]
    pallas_call x3 -> x7, Pallas kernels: 13 us -> 12 us  [call(): pl.pallas_call(kernel, out_shape=[jax.ShapeDtypeStruct(s, types.get(n, jn...]
  transfers between devices with their start and end apart: 8 -> 10, of which waited for: 5 -> 4; matrix products, arithmetic and copies ran while one was open for 0% -> 0% of each run, Pallas kernels for 0% -> 7%
where the time goes in v5:
time: 48.9 us; the launch traced here: 48.7 us
  blocking collectives  17.5 us (36%)
  starting transfers between devices  14.3 us (29%)
  Pallas kernels  12 us (25%)
  waiting for transfers between devices  3.39 us (7%)
  between operations  0.79 us (2%)
  other arithmetic  0.67 us (1%)
    all_to_all x1, blocking collectives, body(): lax.all_to_all(sums.reshape(parts, patch_dev), ('gx', 'yz'), 0, 0, tiled=...  12.8 us
    pallas_call x7, Pallas kernels, call(): pl.pallas_call(kernel, out_shape=[jax.ShapeDtypeStruct(s, types.get(n, jn...  12 us
    ppermute x2, starting transfers between devices, exchange(): one = lax.ppermute(jnp.where(is_even, up, dn), ('gx', 'yz'), hop)  5.5 us
    all_gather x2, blocking collectives, exchange(): lax.all_gather(both, 'yz', axis=0, tiled=True, axis_index_groups=pairs)  4.64 us
    ppermute x2, starting transfers between devices, exchange(): ab_far = lax.ppermute(ab, 'yz', across)  3.17 us
    ppermute x2, starting transfers between devices, exchange(): two_far = lax.ppermute(two, 'yz', across)  3.04 us
    ppermute x2, starting transfers between devices, exchange(): one_far = lax.ppermute(one, 'yz', across)  2.62 us
    ppermute x2, waiting for transfers between devices, exchange(): two_far = lax.ppermute(two, 'yz', across)  2.1 us
  transfers between devices with their start and end apart: 10, of which 4 were waited for; matrix products, arithmetic and copies ran while one was open for 0% of the time, Pallas kernels for 7%

profile of v5, /device:TPU:0, one launch (start us, length us, event | category | flops | bytes accessed | tf_op | source)
XLA Modules:
  0.0 48.7 jit_solution(9867769519358716271)
XLA Ops:
  0.6 1.9 %shard_map.85 = (f32[2,19,16,512]{3,2,1,0:T(8,128)S(1)}, f32[2,16,512]{2,1,0:T(8,128)S(1)}, f32[2,16,512]{2,1,0:T(8,128)S(1)}, f32[2,24,128]{2,1,0:T(8,128)S(1)}, f32[2,24,128]{2,1,0:T(8,128)S(1)}) custom-call(f32[2,19,16,512]{3,2,1,0:T(8,128)} %pops.1, s32[2,16,512]{2,1,0:T(8,128)} %mask.1, f32[2,16,512]{2,1,0:T(8,128)} %frac_in.1, f32[2,16,512]{2,1,0:T(8,128)} %probe_in.1), custom_call_target="tpu_custom_call" | custom-call | tf_op jit(solution)/shard_map/pallas_call | solution.py:632
  2.6 3.0 %collective-permute-start.1 = (f32[2,24,128]{2,1,0:T(8,128)S(1)}, f32[2,24,128]{2,1,0:T(8,128)S(1)}, u32[]{:S(2)}, u32[]{:S(2)}) collective-permute-start(f32[2,24,128]{2,1,0:T(8,128)S(1)} %get-tuple-element.49), channel_id=1, source_target_pairs={{0,4},{4,8},{8,12},{12,16},{16,20},{20,24},{24,28},{28,29},{1,0},{... | collective-permute-start | bytes 73736 | tf_op jit(solution)/shard_map/ppermute | solution.py:657
  5.6 0.0 collective-permute-start
  5.6 0.3 shard_map.87
  5.9 1.6 %collective-permute-start.2 = (f32[2,80,128]{2,1,0:T(8,128)S(1)}, f32[2,80,128]{2,1,0:T(8,128)S(1)}, u32[]{:S(2)}, u32[]{:S(2)}) collective-permute-start(f32[2,80,128]{2,1,0:T(8,128)S(1)} %shard_map.87), channel_id=1, source_target_pairs={{0,2},{1,3},{2,0},{3,1},{4,6},{5,7},{6,4},{7,5},{8,10},{9,11},{10,... | collective-permute-start | bytes 245768 | tf_op jit(solution)/shard_map/ppermute | solution.py:660
  7.5 0.0 collective-permute-done.1
  7.5 1.2 %collective-permute-start.3 = (f32[2,24,128]{2,1,0:T(8,128)S(1)}, f32[2,24,128]{2,1,0:T(8,128)S(1)}, u32[]{:S(2)}, u32[]{:S(2)}) collective-permute-start(f32[2,24,128]{2,1,0:T(8,128)S(1)} %collective-permute-done.1), channel_id=1, source_target_pairs={{0,2},{1,3},{2,0},{3,1},{4,6},{5,7},{6,4},{7,5},{8,10},{9,11},{10,... | collective-permute-start | bytes 73736 | tf_op jit(solution)/shard_map/ppermute | solution.py:661
  8.6 0.8 %collective-permute-done.after = f32[2,24,128]{2,1,0:T(8,128)S(1)} collective-permute-done((f32[2,24,128]{2,1,0:T(8,128)S(1)}, f32[2,24,128]{2,1,0:T(8,128)S(1)}, u32[]{:S(2)}, u32[]{:S(2)}) %collective-permute-start) | collective-permute-done | bytes 24608 | tf_op jit(solution)/shard_map/ppermute | solution.py:658
  9.4 1.5 %collective-permute-start.4 = (f32[2,24,128]{2,1,0:T(8,128)S(1)}, f32[2,24,128]{2,1,0:T(8,128)S(1)}, u32[]{:S(2)}, u32[]{:S(2)}) collective-permute-start(f32[2,24,128]{2,1,0:T(8,128)S(1)} %collective-permute-done.after), channel_id=1, source_target_pairs={{0,2},{1,3},{2,0},{3,1},{4,6},{5,7},{6,4},{7,5},{8,10},{9,11},{10,... | collective-permute-start | bytes 73736 | tf_op jit(solution)/shard_map/ppermute | solution.py:662
  10.9 0.5 shard_map.86
  11.4 0.0 collective-permute-done.3
  11.4 1.8 %collective-permute-done.4 = f32[2,24,128]{2,1,0:T(8,128)S(1)} collective-permute-done((f32[2,24,128]{2,1,0:T(8,128)S(1)}, f32[2,24,128]{2,1,0:T(8,128)S(1)}, u32[]{:S(2)}, u32[]{:S(2)}) %collective-permute-start.4) | collective-permute-done | bytes 24608 | tf_op jit(solution)/shard_map/ppermute | solution.py:662
  13.2 0.0 collective-permute-done.2
  13.3 2.2 %all_gather.6.around = f32[8,128,128]{2,1,0:T(8,128)S(1)} all-gather(f32[4,128,128]{2,1,0:T(8,128)S(1)} %maximum_maximum_fusion.1), channel_id=1, replica_groups={{0,1},{2,3},{4,5},{6,7},{8,9},{10,11},{12,13},{14,15},{16,17},{18,19},{..., dimensions={0}, use_global_device_ids=true | all-gather | bytes 786432 | tf_op jit(solution)/shard_map/all_gather | solution.py:674
  15.4 2.7 %shard_map.88 = (f32[2,19,16,512]{3,2,1,0:T(8,128)S(1)}, f32[2,19,16,512]{3,2,1,0:T(8,128)S(1)}, f32[2,16,512]{2,1,0:T(8,128)S(1)}, f32[2,40,128]{2,1,0:T(8,128)S(1)}, f32[2,40,128]{2,1,0:T(8,128)S(1)}) custom-call(s32[64]{0:T(128)S(1)} %copy-done.3, f32[2,19,16,512]{3,2,1,0:T(8,128)S(1)} %get-tuple-element.25.moved, ...), custom_call_target="tpu_custom_call" | custom-call | tf_op jit(solution)/shard_map/pallas_call | solution.py:632
  18.2 2.5 %collective-permute-start.6 = (f32[2,40,128]{2,1,0:T(8,128)S(1)}, f32[2,40,128]{2,1,0:T(8,128)S(1)}, u32[]{:S(2)}, u32[]{:S(2)}) collective-permute-start(f32[2,40,128]{2,1,0:T(8,128)S(1)} %get-tuple-element.43), channel_id=1, source_target_pairs={{0,4},{4,8},{8,12},{12,16},{16,20},{20,24},{24,28},{28,29},{1,0},{... | collective-permute-start | bytes 122888 | tf_op jit(solution)/shard_map/ppermute | solution.py:657
  20.7 0.4 shard_map.90
  21.1 1.6 %collective-permute-start.7 = (f32[2,144,128]{2,1,0:T(8,128)S(1)}, f32[2,144,128]{2,1,0:T(8,128)S(1)}, u32[]{:S(2)}, u32[]{:S(2)}) collective-permute-start(f32[2,144,128]{2,1,0:T(8,128)S(1)} %shard_map.90), channel_id=1, source_target_pairs={{0,2},{1,3},{2,0},{3,1},{4,6},{5,7},{6,4},{7,5},{8,10},{9,11},{10,... | collective-permute-start | bytes 442376 | tf_op jit(solution)/shard_map/ppermute | solution.py:660
  22.7 0.0 collective-permute-done.6
  22.7 1.5 %collective-permute-start.8 = (f32[2,40,128]{2,1,0:T(8,128)S(1)}, f32[2,40,128]{2,1,0:T(8,128)S(1)}, u32[]{:S(2)}, u32[]{:S(2)}) collective-permute-start(f32[2,40,128]{2,1,0:T(8,128)S(1)} %collective-permute-done.6), channel_id=1, source_target_pairs={{0,2},{1,3},{2,0},{3,1},{4,6},{5,7},{6,4},{7,5},{8,10},{9,11},{10,... | collective-permute-start | bytes 122888 | tf_op jit(solution)/shard_map/ppermute | solution.py:661
  24.2 0.5 %collective-permute-done.5.after = f32[2,40,128]{2,1,0:T(8,128)S(1)} collective-permute-done((f32[2,40,128]{2,1,0:T(8,128)S(1)}, f32[2,40,128]{2,1,0:T(8,128)S(1)}, u32[]{:S(2)}, u32[]{:S(2)}) %collective-permute-start.5) | collective-permute-done | bytes 40992 | tf_op jit(solution)/shard_map/ppermute | solution.py:658
  24.7 1.5 %collective-permute-start.9 = (f32[2,40,128]{2,1,0:T(8,128)S(1)}, f32[2,40,128]{2,1,0:T(8,128)S(1)}, u32[]{:S(2)}, u32[]{:S(2)}) collective-permute-start(f32[2,40,128]{2,1,0:T(8,128)S(1)} %collective-permute-done.5.after), channel_id=1, source_target_pairs={{0,2},{1,3},{2,0},{3,1},{4,6},{5,7},{6,4},{7,5},{8,10},{9,11},{10,... | collective-permute-start | bytes 122888 | tf_op jit(solution)/shard_map/ppermute | solution.py:662
  26.2 2.1 %shard_map.89 = (f32[2,19,16,512]{3,2,1,0:T(8,128)S(1)}, f32[2,19,16,512]{3,2,1,0:T(8,128)S(1)}, bf16[2,16,128,512]{3,2,1,0:T(8,128)(2,1)S(1)}) custom-call(f32[2,19,16,512]{3,2,1,0:T(8,128)S(1)} %get-tuple-element.28.post1, f32[2,19,16,512]{3,2,1,0:T(8,128)S(1)} %get-tuple-element.29.adj1, s32[2,16,512]{2,1,0:T(8,128)S(1)} %copy-done.2, ...), custom_call_target="tpu_custom_call" | custom-call | tf_op jit(solution)/shard_map/pallas_call | solution.py:632
  28.4 0.0 copy-start
  28.4 0.0 copy-start.1
  28.4 0.3 collective-permute-done.9
  28.7 0.0 collective-permute-done.7
  28.8 2.5 %all_gather.7.around = f32[8,224,128]{2,1,0:T(8,128)S(1)} all-gather(f32[4,224,128]{2,1,0:T(8,128)S(1)} %maximum_maximum_fusion), channel_id=1, replica_groups={{0,1},{2,3},{4,5},{6,7},{8,9},{10,11},{12,13},{14,15},{16,17},{18,19},{..., dimensions={0}, use_global_device_ids=true | all-gather | bytes 1376256 | tf_op jit(solution)/shard_map/all_gather | solution.py:674
  31.2 4.0 %shard_map.91 = (f32[2,19,16,512]{3,2,1,0:T(8,128)}, f32[2,19,16,512]{3,2,1,0:T(8,128)}, f32[16,128]{1,0:T(8,128)S(1)}) custom-call(s32[64]{0:T(128)S(1)} %copy-done.3, f32[2,19,16,512]{3,2,1,0:T(8,128)S(1)} %get-tuple-element.32.moved, f32[2,19,16,512]{3,2,1,0:T(8,128)S(1)} %get-tuple-element.33.back, ...), custom_call_target="tpu_custom_call" | custom-call | tf_op jit(solution)/shard_map/pallas_call | solution.py:632
  35.3 0.1 all_to_all.6
  35.3 12.8 %all_to_all.9 = f32[32,1,64]{2,1,0:T(1,128)S(1)} all-to-all(f32[32,1,64]{2,1,0:T(1,128)S(1)} %bitcast.1), channel_id=1, replica_groups=mesh['gx'=8,'yz'=4] {'gx','yz'}, dimensions={0} | all-to-all | bytes 16384 | tf_op jit(solution)/shard_map/all_to_all | solution.py:750
  48.1 0.6 %reduce_sum.9 = f32[64]{0:T(128)} reduce(f32[32,1,64]{2,1,0:T(1,128)S(1)} %all_to_all.9, f32[]{:T(128)} %constant.21.clone.1), dimensions={0,1}, to_apply=%region_0.1 | reduce | flops 1984 | bytes 8452 | tf_op jit(solution)/shard_map/reduce_sum | solution.py:753
  (16 shorter events, 0.1 us)
Async XLA Ops:
  2.6 4.9 %collective-permute-start.1 = (f32[2,24,128]{2,1,0:T(8,128)S(1)}, f32[2,24,128]{2,1,0:T(8,128)S(1)}, u32[]{:S(2)}, u32[]{:S(2)}) collective-permute-start(f32[2,24,128]{2,1,0:T(8,128)S(1)} %get-tuple-element.49), channel_id=1, source_target_pairs={{0,4},{4,8},{8,12},{12,16},{16,20},{20,24},{24,28},{28,29},{1,0},{... | collective-permute-start | bytes 73736 | tf_op jit(solution)/shard_map/ppermute | solution.py:657
  5.6 3.8 %collective-permute-start = (f32[2,24,128]{2,1,0:T(8,128)S(1)}, f32[2,24,128]{2,1,0:T(8,128)S(1)}, u32[]{:S(2)}, u32[]{:S(2)}) collective-permute-start(f32[2,24,128]{2,1,0:T(8,128)S(1)} %get-tuple-element.50), channel_id=1, source_target_pairs={{4,0},{8,4},{12,8},{16,12},{20,16},{24,20},{28,24},{29,28},{0,1},{... | collective-permute-start | bytes 73736 | tf_op jit(solution)/shard_map/ppermute | solution.py:658
  5.9 7.4 %collective-permute-start.2 = (f32[2,80,128]{2,1,0:T(8,128)S(1)}, f32[2,80,128]{2,1,0:T(8,128)S(1)}, u32[]{:S(2)}, u32[]{:S(2)}) collective-permute-start(f32[2,80,128]{2,1,0:T(8,128)S(1)} %shard_map.87), channel_id=1, source_target_pairs={{0,2},{1,3},{2,0},{3,1},{4,6},{5,7},{6,4},{7,5},{8,10},{9,11},{10,... | collective-permute-start | bytes 245768 | tf_op jit(solution)/shard_map/ppermute | solution.py:660
  7.5 4.0 %collective-permute-start.3 = (f32[2,24,128]{2,1,0:T(8,128)S(1)}, f32[2,24,128]{2,1,0:T(8,128)S(1)}, u32[]{:S(2)}, u32[]{:S(2)}) collective-permute-start(f32[2,24,128]{2,1,0:T(8,128)S(1)} %collective-permute-done.1), channel_id=1, source_target_pairs={{0,2},{1,3},{2,0},{3,1},{4,6},{5,7},{6,4},{7,5},{8,10},{9,11},{10,... | collective-permute-start | bytes 73736 | tf_op jit(solution)/shard_map/ppermute | solution.py:661
  9.4 3.8 %collective-permute-start.4 = (f32[2,24,128]{2,1,0:T(8,128)S(1)}, f32[2,24,128]{2,1,0:T(8,128)S(1)}, u32[]{:S(2)}, u32[]{:S(2)}) collective-permute-start(f32[2,24,128]{2,1,0:T(8,128)S(1)} %collective-permute-done.after), channel_id=1, source_target_pairs={{0,2},{1,3},{2,0},{3,1},{4,6},{5,7},{6,4},{7,5},{8,10},{9,11},{10,... | collective-permute-start | bytes 73736 | tf_op jit(solution)/shard_map/ppermute | solution.py:662
  10.9 4.5 %copy-start.3 = (s32[64]{0:T(128)S(1)}, s32[64]{0:T(128)}, u32[]{:S(2)}) copy-start(s32[64]{0:T(128)} %pos.3) | copy-start | bytes 772
  18.2 4.5 %collective-permute-start.6 = (f32[2,40,128]{2,1,0:T(8,128)S(1)}, f32[2,40,128]{2,1,0:T(8,128)S(1)}, u32[]{:S(2)}, u32[]{:S(2)}) collective-permute-start(f32[2,40,128]{2,1,0:T(8,128)S(1)} %get-tuple-element.43), channel_id=1, source_target_pairs={{0,4},{4,8},{8,12},{12,16},{16,20},{20,24},{24,28},{28,29},{1,0},{... | collective-permute-start | bytes 122888 | tf_op jit(solution)/shard_map/ppermute | solution.py:657
  20.7 4.0 %collective-permute-start.5 = (f32[2,40,128]{2,1,0:T(8,128)S(1)}, f32[2,40,128]{2,1,0:T(8,128)S(1)}, u32[]{:S(2)}, u32[]{:S(2)}) collective-permute-start(f32[2,40,128]{2,1,0:T(8,128)S(1)} %get-tuple-element.44), channel_id=1, source_target_pairs={{4,0},{8,4},{12,8},{16,12},{20,16},{24,20},{28,24},{29,28},{0,1},{... | collective-permute-start | bytes 122888 | tf_op jit(solution)/shard_map/ppermute | solution.py:658
  20.7 5.5 %copy-start.2 = (s32[2,16,512]{2,1,0:T(8,128)S(1)}, s32[2,16,512]{2,1,0:T(8,128)}, u32[]{:S(2)}) copy-start(s32[2,16,512]{2,1,0:T(8,128)} %patch.3) | copy-start | bytes 196612
  21.1 7.6 %collective-permute-start.7 = (f32[2,144,128]{2,1,0:T(8,128)S(1)}, f32[2,144,128]{2,1,0:T(8,128)S(1)}, u32[]{:S(2)}, u32[]{:S(2)}) collective-permute-start(f32[2,144,128]{2,1,0:T(8,128)S(1)} %shard_map.90), channel_id=1, source_target_pairs={{0,2},{1,3},{2,0},{3,1},{4,6},{5,7},{6,4},{7,5},{8,10},{9,11},{10,... | collective-permute-start | bytes 442376 | tf_op jit(solution)/shard_map/ppermute | solution.py:660
  22.7 5.7 %collective-permute-start.8 = (f32[2,40,128]{2,1,0:T(8,128)S(1)}, f32[2,40,128]{2,1,0:T(8,128)S(1)}, u32[]{:S(2)}, u32[]{:S(2)}) collective-permute-start(f32[2,40,128]{2,1,0:T(8,128)S(1)} %collective-permute-done.6), channel_id=1, source_target_pairs={{0,2},{1,3},{2,0},{3,1},{4,6},{5,7},{6,4},{7,5},{8,10},{9,11},{10,... | collective-permute-start | bytes 122888 | tf_op jit(solution)/shard_map/ppermute | solution.py:661
  24.7 4.0 %collective-permute-start.9 = (f32[2,40,128]{2,1,0:T(8,128)S(1)}, f32[2,40,128]{2,1,0:T(8,128)S(1)}, u32[]{:S(2)}, u32[]{:S(2)}) collective-permute-start(f32[2,40,128]{2,1,0:T(8,128)S(1)} %collective-permute-done.5.after), channel_id=1, source_target_pairs={{0,2},{1,3},{2,0},{3,1},{4,6},{5,7},{6,4},{7,5},{8,10},{9,11},{10,... | collective-permute-start | bytes 122888 | tf_op jit(solution)/shard_map/ppermute | solution.py:662
  28.4 2.9 %copy-start = (f32[2,19,16,512]{3,2,1,0:T(8,128)S(1)}, f32[2,19,16,512]{3,2,1,0:T(8,128)}, u32[]{:S(2)}) copy-start(f32[2,19,16,512]{3,2,1,0:T(8,128)} %pops.1) | copy-start | bytes 3735556
  28.4 2.9 %copy-start.1 = (s32[2,16,512]{2,1,0:T(8,128)S(1)}, s32[2,16,512]{2,1,0:T(8,128)}, u32[]{:S(2)}) copy-start(s32[2,16,512]{2,1,0:T(8,128)} %mask.1) | copy-start | bytes 196612

commit v6 on v5

--- a/solution.py
+++ b/solution.py
@@ -332,7 +332,10 @@
             s = jnp.where(found, s, 0)
             owner, slot = s // count, s % count
             half = ((owner ^ lax.axis_index("yz")) >> 1) & 1
-            block = ((owner & 1) * 2 + half) * count + slot
+            side = owner & 1
+            if pack is PACK1:
+                side = side ^ (lax.axis_index("yz") & 1)
+            block = (side * 2 + half) * count + slot
             self.where[d] = (block, found)
         self.planes = {}
 
@@ -513,9 +516,9 @@
             x = near.enter(back[t, n], against(i), ("probe", 0), 0.0)
             pulled[t, n] = x if vel(i)[0] > 0 else -x
 
-        return [functools.partial(forward, i) for i in range(Q)] + [
-            functools.partial(backward, n, i) for n, i in enumerate(AXIAL)
-        ]
+        jobs = [(vel(i), functools.partial(forward, i)) for i in range(Q)]
+        jobs += [(against(i), functools.partial(backward, n, i)) for n, i in enumerate(AXIAL)]
+        return [job for _, job in sorted(jobs, key=lambda item: (item[0][2], item[0][1]))]
 
     def runs(t):
         def run(r, c):
@@ -644,32 +647,35 @@
     )(*args)
 
 
-def exchange(ab, up, dn):
+def exchange(ab, up, dn, first):
     n = lax.axis_size("gx")
     m = lax.axis_size("yz")
     assert m == 4
     hop = []
     for q in range(m):
         for g in range(n):
-            to = g + 1 if q % 2 == 0 else g - 1
-            hop.append((g * m + q, to * m + q if 0 <= to < n else g * m + (q ^ 1)))
-    is_even = lax.axis_index("yz") % 2 == 0
-    one = lax.ppermute(jnp.where(is_even, up, dn), ("gx", "yz"), hop)
-    two = lax.ppermute(jnp.where(is_even, dn, up), ("gx", "yz"), [(j, i) for i, j in hop])
+            to = g + 1 if q < 2 else g - 1
+            hop.append((g * m + q, to * m + q if 0 <= to < n else g * m + (q ^ 2)))
+    is_low = lax.axis_index("yz") < 2
+    one = lax.ppermute(jnp.where(is_low, up, dn), ("gx", "yz"), hop)
+    two = lax.ppermute(jnp.where(is_low, dn, up), ("gx", "yz"), [(j, i) for i, j in hop])
     across = [(q, q ^ 2) for q in range(m)]
     ab_far = lax.ppermute(ab, "yz", across)
     one_far = lax.ppermute(one, "yz", across)
     two_far = lax.ppermute(two, "yz", across)
     l_near = jnp.concatenate(
-        [jnp.where(is_even, one, two), jnp.where(is_even, two, one)], axis=1
+        [jnp.where(is_low, one, two), jnp.where(is_low, two, one)], axis=1
     )
     l_far = jnp.concatenate(
-        [jnp.where(is_even, one_far, two_far), jnp.where(is_even, two_far, one_far)], axis=1
+        [jnp.where(is_low, two_far, one_far), jnp.where(is_low, one_far, two_far)], axis=1
     )
     both = jnp.concatenate(
         [jnp.concatenate([ab, l_near], axis=1), jnp.concatenate([ab_far, l_far], axis=1)],
         axis=0,
     )
+    if first:
+        other = lax.ppermute(both, "yz", [(q, q ^ 1) for q in range(m)])
+        return two, jnp.concatenate([both, other], axis=0)
     pairs = [[0, 1], [2, 3]]
     return two, lax.all_gather(both, "yz", axis=0, tiled=True, axis_index_groups=pairs)
 
@@ -708,7 +714,7 @@
         in_hbm=range(4),
     )
     (ab,) = call(first_sides, sides(PACK1), [], (post0, probe_kept))
-    token, around = exchange(ab, up, dn)
+    token, around = exchange(ab, up, dn, True)
     axial = (count, len(AXIAL)) + plane[1:]
     moved, back = call(first_own, [field, axial], [], (post0, probe_kept, token), in_any=(2,))
     post1, adj1, dsolid, up, dn = call(
@@ -723,7 +729,7 @@
         in_smem=(0,),
     )
     (ab,) = call(second_sides, sides(PACK2), [], (post1, adj1))
-    token, around = exchange(ab, up, dn)
+    token, around = exchange(ab, up, dn, False)
     moved, back, onehot = call(
         second_own,
         [field, field, (count, TL, LANES, CELLS)],

time: 48.9 us -> 47.3 us (0.967)
  blocking collectives: 17.5 us -> 14.3 us
  waiting for transfers between devices: 3.39 us -> 4.52 us
  starting transfers between devices: 14.3 us -> 14.9 us
    all_gather x2 -> x1, blocking collectives: 4.64 us -> 2.46 us  [exchange(): lax.all_gather(both, 'yz', axis=0, tiled=True, axis_index_groups=pairs)]
    ppermute x2, waiting for transfers between devices: 0.01 us -> 1.83 us  [exchange(): one_far = lax.ppermute(one, 'yz', across)]
    ppermute x2, waiting for transfers between devices: 2.1 us -> 0.9 us  [exchange(): two_far = lax.ppermute(two, 'yz', across)]
    all_to_all x1, blocking collectives: 12.8 us -> 11.9 us  [body(): lax.all_to_all(sums.reshape(parts, patch_dev), ('gx', 'yz'), 0, 0, tiled=...]
    ppermute x2, starting transfers between devices: 3.17 us -> 4.03 us  [exchange(): ab_far = lax.ppermute(ab, 'yz', across)]
    ppermute x4 -> x5, waiting for transfers between devices: 1.28 us -> 1.79 us  [the longest x1 1.04 us: exchange(): other = lax.ppermute(both, 'yz', [(q, q ^ 1) for q in range(m)])]
    ppermute x4 -> x5, starting transfers between devices: 5.51 us -> 5.2 us  [the longest x2 4.56 us: exchange(): lax.ppermute(jnp.where(is_low, dn, up), ('gx', 'yz'), [(j, i) for i, j in...]
  transfers between devices with their start and end apart: 10 -> 11, of which waited for: 4 -> 5; matrix products, arithmetic and copies ran while one was open for 0% -> 0% of each run, Pallas kernels for 7% -> 7%
where the time goes in v6:
time: 47.3 us; the launch traced here: 47.2 us
  starting transfers between devices  14.9 us (32%)
  blocking collectives  14.3 us (30%)
  Pallas kernels  11.8 us (25%)
  waiting for transfers between devices  4.52 us (10%)
  between operations  0.8 us (2%)
  other arithmetic  0.72 us (2%)
    all_to_all x1, blocking collectives, body(): lax.all_to_all(sums.reshape(parts, patch_dev), ('gx', 'yz'), 0, 0, tiled=...  11.9 us
    pallas_call x7, Pallas kernels, call(): pl.pallas_call(kernel, out_shape=[jax.ShapeDtypeStruct(s, types.get(n, jn...  11.8 us
    ppermute x2, starting transfers between devices, exchange(): lax.ppermute(jnp.where(is_low, dn, up), ('gx', 'yz'), [(j, i) for i, j in...  4.56 us
    ppermute x2, starting transfers between devices, exchange(): ab_far = lax.ppermute(ab, 'yz', across)  4.03 us
    ppermute x2, starting transfers between devices, exchange(): one_far = lax.ppermute(one, 'yz', across)  3.08 us
    ppermute x2, starting transfers between devices, exchange(): two_far = lax.ppermute(two, 'yz', across)  2.59 us
    all_gather x1, blocking collectives, exchange(): lax.all_gather(both, 'yz', axis=0, tiled=True, axis_index_groups=pairs)  2.46 us
    ppermute x2, waiting for transfers between devices, exchange(): one_far = lax.ppermute(one, 'yz', across)  1.83 us
  transfers between devices with their start and end apart: 11, of which 5 were waited for; matrix products, arithmetic and copies ran while one was open for 0% of the time, Pallas kernels for 7%

profile of v6, /device:TPU:0, one launch (start us, length us, event | category | flops | bytes accessed | tf_op | source)
XLA Modules:
  0.0 47.2 jit_solution(4344570997785305659)
XLA Ops:
  0.6 1.9 %shard_map.85 = (f32[2,19,16,512]{3,2,1,0:T(8,128)S(1)}, f32[2,16,512]{2,1,0:T(8,128)S(1)}, f32[2,16,512]{2,1,0:T(8,128)S(1)}, f32[2,24,128]{2,1,0:T(8,128)S(1)}, f32[2,24,128]{2,1,0:T(8,128)S(1)}) custom-call(f32[2,19,16,512]{3,2,1,0:T(8,128)} %pops.1, s32[2,16,512]{2,1,0:T(8,128)} %mask.1, f32[2,16,512]{2,1,0:T(8,128)} %frac_in.1, f32[2,16,512]{2,1,0:T(8,128)} %probe_in.1), custom_call_target="tpu_custom_call" | custom-call | tf_op jit(solution)/shard_map/pallas_call | solution.py:635
  2.6 3.0 %collective-permute-start = (f32[2,24,128]{2,1,0:T(8,128)S(1)}, f32[2,24,128]{2,1,0:T(8,128)S(1)}, u32[]{:S(2)}, u32[]{:S(2)}) collective-permute-start(f32[2,24,128]{2,1,0:T(8,128)S(1)} %get-tuple-element.50), channel_id=1, source_target_pairs={{4,0},{8,4},{12,8},{16,12},{20,16},{24,20},{28,24},{30,28},{5,1},{... | collective-permute-start | bytes 73736 | tf_op jit(solution)/shard_map/ppermute | solution.py:661
  5.6 0.0 collective-permute-start.1
  5.6 0.3 shard_map.87
  5.9 2.1 %collective-permute-start.2 = (f32[2,80,128]{2,1,0:T(8,128)S(1)}, f32[2,80,128]{2,1,0:T(8,128)S(1)}, u32[]{:S(2)}, u32[]{:S(2)}) collective-permute-start(f32[2,80,128]{2,1,0:T(8,128)S(1)} %shard_map.87), channel_id=1, source_target_pairs={{0,2},{1,3},{2,0},{3,1},{4,6},{5,7},{6,4},{7,5},{8,10},{9,11},{10,... | collective-permute-start | bytes 245768 | tf_op jit(solution)/shard_map/ppermute | solution.py:663
  8.0 0.0 collective-permute-done.after
  8.0 1.4 %collective-permute-start.3 = (f32[2,24,128]{2,1,0:T(8,128)S(1)}, f32[2,24,128]{2,1,0:T(8,128)S(1)}, u32[]{:S(2)}, u32[]{:S(2)}) collective-permute-start(f32[2,24,128]{2,1,0:T(8,128)S(1)} %collective-permute-done.after), channel_id=1, source_target_pairs={{0,2},{1,3},{2,0},{3,1},{4,6},{5,7},{6,4},{7,5},{8,10},{9,11},{10,... | collective-permute-start | bytes 73736 | tf_op jit(solution)/shard_map/ppermute | solution.py:665
  9.4 1.5 %collective-permute-start.4 = (f32[2,24,128]{2,1,0:T(8,128)S(1)}, f32[2,24,128]{2,1,0:T(8,128)S(1)}, u32[]{:S(2)}, u32[]{:S(2)}) collective-permute-start(f32[2,24,128]{2,1,0:T(8,128)S(1)} %collective-permute-done.1), channel_id=1, source_target_pairs={{0,2},{1,3},{2,0},{3,1},{4,6},{5,7},{6,4},{7,5},{8,10},{9,11},{10,... | collective-permute-start | bytes 73736 | tf_op jit(solution)/shard_map/ppermute | solution.py:664
  10.9 0.9 %collective-permute-done.3 = f32[2,24,128]{2,1,0:T(8,128)S(1)} collective-permute-done((f32[2,24,128]{2,1,0:T(8,128)S(1)}, f32[2,24,128]{2,1,0:T(8,128)S(1)}, u32[]{:S(2)}, u32[]{:S(2)}) %collective-permute-start.3) | collective-permute-done | bytes 24608 | tf_op jit(solution)/shard_map/ppermute | solution.py:665
  11.8 1.4 %collective-permute-done.4 = f32[2,24,128]{2,1,0:T(8,128)S(1)} collective-permute-done((f32[2,24,128]{2,1,0:T(8,128)S(1)}, f32[2,24,128]{2,1,0:T(8,128)S(1)}, u32[]{:S(2)}, u32[]{:S(2)}) %collective-permute-start.4) | collective-permute-done | bytes 24608 | tf_op jit(solution)/shard_map/ppermute | solution.py:664
  13.2 0.0 collective-permute-done.2
  13.3 0.0 copy-start.3
  13.3 0.1 collective-permute-start.5
  13.4 0.5 %shard_map.86 = (f32[2,19,16,512]{3,2,1,0:T(8,128)S(1)}, f32[2,10,16,512]{3,2,1,0:T(8,128)S(1)}) custom-call(f32[2,19,16,512]{3,2,1,0:T(8,128)S(1)} %get-tuple-element.21.post, f32[2,16,512]{2,1,0:T(8,128)S(1)} %get-tuple-element.22.probe, f32[2,24,128]{2,1,0:T(8,128)S(1)} %collective-permute-done.after), custom_call_target="tpu_custom_call" | custom-call | tf_op jit(solution)/shard_map/pallas_call | solution.py:635
  13.9 1.0 %collective-permute-done.5 = f32[4,128,128]{2,1,0:T(8,128)S(1)} collective-permute-done((f32[4,128,128]{2,1,0:T(8,128)S(1)}, f32[4,128,128]{2,1,0:T(8,128)S(1)}, u32[]{:S(2)}, u32[]{:S(2)}) %collective-permute-start.5) | collective-permute-done | bytes 262176 | tf_op jit(solution)/shard_map/ppermute | solution.py:677
  15.0 2.6 %shard_map.88 = (f32[2,19,16,512]{3,2,1,0:T(8,128)S(1)}, f32[2,19,16,512]{3,2,1,0:T(8,128)S(1)}, f32[2,16,512]{2,1,0:T(8,128)S(1)}, f32[2,40,128]{2,1,0:T(8,128)S(1)}, f32[2,40,128]{2,1,0:T(8,128)S(1)}) custom-call(s32[64]{0:T(128)S(1)} %copy-done.3, f32[2,19,16,512]{3,2,1,0:T(8,128)S(1)} %get-tuple-element.25.moved, ...), custom_call_target="tpu_custom_call" | custom-call | tf_op jit(solution)/shard_map/pallas_call | solution.py:635
  17.5 1.5 %collective-permute-start.6 = (f32[2,40,128]{2,1,0:T(8,128)S(1)}, f32[2,40,128]{2,1,0:T(8,128)S(1)}, u32[]{:S(2)}, u32[]{:S(2)}) collective-permute-start(f32[2,40,128]{2,1,0:T(8,128)S(1)} %get-tuple-element.44), channel_id=1, source_target_pairs={{4,0},{8,4},{12,8},{16,12},{20,16},{24,20},{28,24},{30,28},{5,1},{... | collective-permute-start | bytes 122888 | tf_op jit(solution)/shard_map/ppermute | solution.py:661
  19.1 0.5 %collective-permute-start.7 = (f32[2,40,128]{2,1,0:T(8,128)S(1)}, f32[2,40,128]{2,1,0:T(8,128)S(1)}, u32[]{:S(2)}, u32[]{:S(2)}) collective-permute-start(f32[2,40,128]{2,1,0:T(8,128)S(1)} %get-tuple-element.43), channel_id=1, source_target_pairs={{0,4},{4,8},{8,12},{12,16},{16,20},{20,24},{24,28},{28,30},{1,5},{... | collective-permute-start | bytes 122888 | tf_op jit(solution)/shard_map/ppermute | solution.py:660
  19.6 0.4 shard_map.90
  20.1 2.0 %collective-permute-start.8 = (f32[2,144,128]{2,1,0:T(8,128)S(1)}, f32[2,144,128]{2,1,0:T(8,128)S(1)}, u32[]{:S(2)}, u32[]{:S(2)}) collective-permute-start(f32[2,144,128]{2,1,0:T(8,128)S(1)} %shard_map.90), channel_id=1, source_target_pairs={{0,2},{1,3},{2,0},{3,1},{4,6},{5,7},{6,4},{7,5},{8,10},{9,11},{10,... | collective-permute-start | bytes 442376 | tf_op jit(solution)/shard_map/ppermute | solution.py:663
  22.1 1.2 %collective-permute-start.9 = (f32[2,40,128]{2,1,0:T(8,128)S(1)}, f32[2,40,128]{2,1,0:T(8,128)S(1)}, u32[]{:S(2)}, u32[]{:S(2)}) collective-permute-start(f32[2,40,128]{2,1,0:T(8,128)S(1)} %collective-permute-done.6.after), channel_id=1, source_target_pairs={{0,2},{1,3},{2,0},{3,1},{4,6},{5,7},{6,4},{7,5},{8,10},{9,11},{10,... | collective-permute-start | bytes 122888 | tf_op jit(solution)/shard_map/ppermute | solution.py:665
  23.2 0.7 %collective-permute-done.7 = f32[2,40,128]{2,1,0:T(8,128)S(1)} collective-permute-done((f32[2,40,128]{2,1,0:T(8,128)S(1)}, f32[2,40,128]{2,1,0:T(8,128)S(1)}, u32[]{:S(2)}, u32[]{:S(2)}) %collective-permute-start.7) | collective-permute-done | bytes 40992 | tf_op jit(solution)/shard_map/ppermute | solution.py:660
  23.9 1.6 %collective-permute-start.10 = (f32[2,40,128]{2,1,0:T(8,128)S(1)}, f32[2,40,128]{2,1,0:T(8,128)S(1)}, u32[]{:S(2)}, u32[]{:S(2)}) collective-permute-start(f32[2,40,128]{2,1,0:T(8,128)S(1)} %collective-permute-done.7), channel_id=1, source_target_pairs={{0,2},{1,3},{2,0},{3,1},{4,6},{5,7},{6,4},{7,5},{8,10},{9,11},{10,... | collective-permute-start | bytes 122888 | tf_op jit(solution)/shard_map/ppermute | solution.py:664
  25.6 2.1 %shard_map.89 = (f32[2,19,16,512]{3,2,1,0:T(8,128)S(1)}, f32[2,19,16,512]{3,2,1,0:T(8,128)S(1)}, bf16[2,16,128,512]{3,2,1,0:T(8,128)(2,1)S(1)}) custom-call(f32[2,19,16,512]{3,2,1,0:T(8,128)S(1)} %get-tuple-element.28.post1, f32[2,19,16,512]{3,2,1,0:T(8,128)S(1)} %get-tuple-element.29.adj1, s32[2,16,512]{2,1,0:T(8,128)S(1)} %copy-done.2, ...), custom_call_target="tpu_custom_call" | custom-call | tf_op jit(solution)/shard_map/pallas_call | solution.py:635
  27.7 0.0 copy-start
  27.7 0.0 copy-start.1
  27.7 0.4 collective-permute-done.10
  28.2 2.5 %all_gather.3.around = f32[8,224,128]{2,1,0:T(8,128)S(1)} all-gather(f32[4,224,128]{2,1,0:T(8,128)S(1)} %maximum_maximum_fusion), channel_id=1, replica_groups={{0,1},{2,3},{4,5},{6,7},{8,9},{10,11},{12,13},{14,15},{16,17},{18,19},{..., dimensions={0}, use_global_device_ids=true | all-gather | bytes 1376256 | tf_op jit(solution)/shard_map/all_gather | solution.py:680
  30.7 4.0 %shard_map.91 = (f32[2,19,16,512]{3,2,1,0:T(8,128)}, f32[2,19,16,512]{3,2,1,0:T(8,128)}, f32[16,128]{1,0:T(8,128)S(1)}) custom-call(s32[64]{0:T(128)S(1)} %copy-done.3, f32[2,19,16,512]{3,2,1,0:T(8,128)S(1)} %get-tuple-element.32.moved, f32[2,19,16,512]{3,2,1,0:T(8,128)S(1)} %get-tuple-element.33.back, ...), custom_call_target="tpu_custom_call" | custom-call | tf_op jit(solution)/shard_map/pallas_call | solution.py:635
  34.7 0.1 all_to_all.6
  34.7 11.9 %all_to_all.9 = f32[32,1,64]{2,1,0:T(1,128)S(1)} all-to-all(f32[32,1,64]{2,1,0:T(1,128)S(1)} %bitcast.1), channel_id=1, replica_groups=mesh['gx'=8,'yz'=4] {'gx','yz'}, dimensions={0} | all-to-all | bytes 16384 | tf_op jit(solution)/shard_map/all_to_all | solution.py:756
  46.6 0.6 %reduce_sum.9 = f32[64]{0:T(128)} reduce(f32[32,1,64]{2,1,0:T(1,128)S(1)} %all_to_all.9, f32[]{:T(128)} %constant.2.clone.1), dimensions={0,1}, to_apply=%region_0.1 | reduce | flops 1984 | bytes 8452 | tf_op jit(solution)/shard_map/reduce_sum | solution.py:759
  (18 shorter events, 0.2 us)
Async XLA Ops:
  2.6 5.4 %collective-permute-start = (f32[2,24,128]{2,1,0:T(8,128)S(1)}, f32[2,24,128]{2,1,0:T(8,128)S(1)}, u32[]{:S(2)}, u32[]{:S(2)}) collective-permute-start(f32[2,24,128]{2,1,0:T(8,128)S(1)} %get-tuple-element.50), channel_id=1, source_target_pairs={{4,0},{8,4},{12,8},{16,12},{20,16},{24,20},{28,24},{30,28},{5,1},{... | collective-permute-start | bytes 73736 | tf_op jit(solution)/shard_map/ppermute | solution.py:661
  5.6 3.8 %collective-permute-start.1 = (f32[2,24,128]{2,1,0:T(8,128)S(1)}, f32[2,24,128]{2,1,0:T(8,128)S(1)}, u32[]{:S(2)}, u32[]{:S(2)}) collective-permute-start(f32[2,24,128]{2,1,0:T(8,128)S(1)} %get-tuple-element.49), channel_id=1, source_target_pairs={{0,4},{4,8},{8,12},{12,16},{16,20},{20,24},{24,28},{28,30},{1,5},{... | collective-permute-start | bytes 73736 | tf_op jit(solution)/shard_map/ppermute | solution.py:660
  5.9 7.3 %collective-permute-start.2 = (f32[2,80,128]{2,1,0:T(8,128)S(1)}, f32[2,80,128]{2,1,0:T(8,128)S(1)}, u32[]{:S(2)}, u32[]{:S(2)}) collective-permute-start(f32[2,80,128]{2,1,0:T(8,128)S(1)} %shard_map.87), channel_id=1, source_target_pairs={{0,2},{1,3},{2,0},{3,1},{4,6},{5,7},{6,4},{7,5},{8,10},{9,11},{10,... | collective-permute-start | bytes 245768 | tf_op jit(solution)/shard_map/ppermute | solution.py:663
  8.0 3.8 %collective-permute-start.3 = (f32[2,24,128]{2,1,0:T(8,128)S(1)}, f32[2,24,128]{2,1,0:T(8,128)S(1)}, u32[]{:S(2)}, u32[]{:S(2)}) collective-permute-start(f32[2,24,128]{2,1,0:T(8,128)S(1)} %collective-permute-done.after), channel_id=1, source_target_pairs={{0,2},{1,3},{2,0},{3,1},{4,6},{5,7},{6,4},{7,5},{8,10},{9,11},{10,... | collective-permute-start | bytes 73736 | tf_op jit(solution)/shard_map/ppermute | solution.py:665
  9.4 3.8 %collective-permute-start.4 = (f32[2,24,128]{2,1,0:T(8,128)S(1)}, f32[2,24,128]{2,1,0:T(8,128)S(1)}, u32[]{:S(2)}, u32[]{:S(2)}) collective-permute-start(f32[2,24,128]{2,1,0:T(8,128)S(1)} %collective-permute-done.1), channel_id=1, source_target_pairs={{0,2},{1,3},{2,0},{3,1},{4,6},{5,7},{6,4},{7,5},{8,10},{9,11},{10,... | collective-permute-start | bytes 73736 | tf_op jit(solution)/shard_map/ppermute | solution.py:664
  13.3 1.7 %copy-start.3 = (s32[64]{0:T(128)S(1)}, s32[64]{0:T(128)}, u32[]{:S(2)}) copy-start(s32[64]{0:T(128)} %pos.3) | copy-start | bytes 772
  13.3 1.6 %collective-permute-start.5 = (f32[4,128,128]{2,1,0:T(8,128)S(1)}, f32[4,128,128]{2,1,0:T(8,128)S(1)}, u32[]{:S(2)}, u32[]{:S(2)}) collective-permute-start(f32[4,128,128]{2,1,0:T(8,128)S(1)} %maximum_maximum_fusion.1), channel_id=1, source_target_pairs={{0,1},{1,0},{2,3},{3,2},{4,5},{5,4},{6,7},{7,6},{8,9},{9,8},{10,11... | collective-permute-start | bytes 786440 | tf_op jit(solution)/shard_map/ppermute | solution.py:677
  17.5 4.5 %collective-permute-start.6 = (f32[2,40,128]{2,1,0:T(8,128)S(1)}, f32[2,40,128]{2,1,0:T(8,128)S(1)}, u32[]{:S(2)}, u32[]{:S(2)}) collective-permute-start(f32[2,40,128]{2,1,0:T(8,128)S(1)} %get-tuple-element.44), channel_id=1, source_target_pairs={{4,0},{8,4},{12,8},{16,12},{20,16},{24,20},{28,24},{30,28},{5,1},{... | collective-permute-start | bytes 122888 | tf_op jit(solution)/shard_map/ppermute | solution.py:661
  19.1 4.9 %collective-permute-start.7 = (f32[2,40,128]{2,1,0:T(8,128)S(1)}, f32[2,40,128]{2,1,0:T(8,128)S(1)}, u32[]{:S(2)}, u32[]{:S(2)}) collective-permute-start(f32[2,40,128]{2,1,0:T(8,128)S(1)} %get-tuple-element.43), channel_id=1, source_target_pairs={{0,4},{4,8},{8,12},{12,16},{16,20},{20,24},{24,28},{28,30},{1,5},{... | collective-permute-start | bytes 122888 | tf_op jit(solution)/shard_map/ppermute | solution.py:660
  19.6 5.9 %copy-start.2 = (s32[2,16,512]{2,1,0:T(8,128)S(1)}, s32[2,16,512]{2,1,0:T(8,128)}, u32[]{:S(2)}) copy-start(s32[2,16,512]{2,1,0:T(8,128)} %patch.3) | copy-start | bytes 196612
  20.1 8.1 %collective-permute-start.8 = (f32[2,144,128]{2,1,0:T(8,128)S(1)}, f32[2,144,128]{2,1,0:T(8,128)S(1)}, u32[]{:S(2)}, u32[]{:S(2)}) collective-permute-start(f32[2,144,128]{2,1,0:T(8,128)S(1)} %shard_map.90), channel_id=1, source_target_pairs={{0,2},{1,3},{2,0},{3,1},{4,6},{5,7},{6,4},{7,5},{8,10},{9,11},{10,... | collective-permute-start | bytes 442376 | tf_op jit(solution)/shard_map/ppermute | solution.py:663
  22.1 5.7 %collective-permute-start.9 = (f32[2,40,128]{2,1,0:T(8,128)S(1)}, f32[2,40,128]{2,1,0:T(8,128)S(1)}, u32[]{:S(2)}, u32[]{:S(2)}) collective-permute-start(f32[2,40,128]{2,1,0:T(8,128)S(1)} %collective-permute-done.6.after), channel_id=1, source_target_pairs={{0,2},{1,3},{2,0},{3,1},{4,6},{5,7},{6,4},{7,5},{8,10},{9,11},{10,... | collective-permute-start | bytes 122888 | tf_op jit(solution)/shard_map/ppermute | solution.py:665
  23.9 4.2 %collective-permute-start.10 = (f32[2,40,128]{2,1,0:T(8,128)S(1)}, f32[2,40,128]{2,1,0:T(8,128)S(1)}, u32[]{:S(2)}, u32[]{:S(2)}) collective-permute-start(f32[2,40,128]{2,1,0:T(8,128)S(1)} %collective-permute-done.7), channel_id=1, source_target_pairs={{0,2},{1,3},{2,0},{3,1},{4,6},{5,7},{6,4},{7,5},{8,10},{9,11},{10,... | collective-permute-start | bytes 122888 | tf_op jit(solution)/shard_map/ppermute | solution.py:664
  27.7 3.0 %copy-start = (f32[2,19,16,512]{3,2,1,0:T(8,128)S(1)}, f32[2,19,16,512]{3,2,1,0:T(8,128)}, u32[]{:S(2)}) copy-start(f32[2,19,16,512]{3,2,1,0:T(8,128)} %pops.1) | copy-start | bytes 3735556
  27.7 3.0 %copy-start.1 = (s32[2,16,512]{2,1,0:T(8,128)S(1)}, s32[2,16,512]{2,1,0:T(8,128)}, u32[]{:S(2)}) copy-start(s32[2,16,512]{2,1,0:T(8,128)} %mask.1) | copy-start | bytes 196612

commit v7 on v6

--- a/solution.py
+++ b/solution.py
@@ -654,20 +654,20 @@
     hop = []
     for q in range(m):
         for g in range(n):
-            to = g + 1 if q < 2 else g - 1
+            to = g + 1 if q >= 2 else g - 1
             hop.append((g * m + q, to * m + q if 0 <= to < n else g * m + (q ^ 2)))
-    is_low = lax.axis_index("yz") < 2
-    one = lax.ppermute(jnp.where(is_low, up, dn), ("gx", "yz"), hop)
-    two = lax.ppermute(jnp.where(is_low, dn, up), ("gx", "yz"), [(j, i) for i, j in hop])
+    rising = lax.axis_index("yz") >= 2
+    one = lax.ppermute(jnp.where(rising, up, dn), ("gx", "yz"), hop)
+    two = lax.ppermute(jnp.where(rising, dn, up), ("gx", "yz"), [(j, i) for i, j in hop])
     across = [(q, q ^ 2) for q in range(m)]
     ab_far = lax.ppermute(ab, "yz", across)
     one_far = lax.ppermute(one, "yz", across)
     two_far = lax.ppermute(two, "yz", across)
     l_near = jnp.concatenate(
-        [jnp.where(is_low, one, two), jnp.where(is_low, two, one)], axis=1
+        [jnp.where(rising, one, two), jnp.where(rising, two, one)], axis=1
     )
     l_far = jnp.concatenate(
-        [jnp.where(is_low, two_far, one_far), jnp.where(is_low, one_far, two_far)], axis=1
+        [jnp.where(rising, two_far, one_far), jnp.where(rising, one_far, two_far)], axis=1
     )
     both = jnp.concatenate(
         [jnp.concatenate([ab, l_near], axis=1), jnp.concatenate([ab_far, l_far], axis=1)],

time: 47.3 us -> 47.3 us (level)
  starting transfers between devices: 14.9 us -> 11.7 us
  waiting for transfers between devices: 4.52 us -> 7.68 us
    ppermute x2, starting transfers between devices: 3.08 us -> 1 us  [exchange(): one_far = lax.ppermute(one, 'yz', across)]
    ppermute x2, waiting for transfers between devices: 0.9 us -> 2.65 us  [exchange(): two_far = lax.ppermute(two, 'yz', across)]
    ppermute x2, starting transfers between devices: 4.03 us -> 2.72 us  [exchange(): ab_far = lax.ppermute(ab, 'yz', across)]
    ppermute x4, waiting for transfers between devices: 0.75 us -> 1.98 us  [the longest x2 1.46 us: exchange(): one = lax.ppermute(jnp.where(rising, up, dn), ('gx', 'yz'), hop)]
  transfers between devices with their start and end apart: 11 -> 11, of which waited for: 5 -> 7; matrix products, arithmetic and copies ran while one was open for 0% -> 0% of each run, Pallas kernels for 7% -> 7%
where the time goes in v7:
time: 47.3 us; the launch traced here: 47.1 us
  blocking collectives  14.3 us (30%)
  Pallas kernels  11.8 us (25%)
  starting transfers between devices  11.7 us (25%)
  waiting for transfers between devices  7.68 us (16%)
  between operations  0.79 us (2%)
  other arithmetic  0.72 us (2%)
    all_to_all x1, blocking collectives, body(): lax.all_to_all(sums.reshape(parts, patch_dev), ('gx', 'yz'), 0, 0, tiled=...  11.9 us
    pallas_call x7, Pallas kernels, call(): pl.pallas_call(kernel, out_shape=[jax.ShapeDtypeStruct(s, types.get(n, jn...  11.8 us
    ppermute x2, starting transfers between devices, exchange(): lax.ppermute(jnp.where(rising, dn, up), ('gx', 'yz'), [(j, i) for i, j in...  5.46 us
    ppermute x2, starting transfers between devices, exchange(): ab_far = lax.ppermute(ab, 'yz', across)  2.72 us
    ppermute x2, waiting for transfers between devices, exchange(): two_far = lax.ppermute(two, 'yz', across)  2.65 us
    all_gather x1, blocking collectives, exchange(): lax.all_gather(both, 'yz', axis=0, tiled=True, axis_index_groups=pairs)  2.46 us
    ppermute x2, starting transfers between devices, exchange(): two_far = lax.ppermute(two, 'yz', across)  2.31 us
    ppermute x2, waiting for transfers between devices, exchange(): one_far = lax.ppermute(one, 'yz', across)  2 us
  transfers between devices with their start and end apart: 11, of which 7 were waited for; matrix products, arithmetic and copies ran while one was open for 0% of the time, Pallas kernels for 7%

profile of v7, /device:TPU:0, one launch (start us, length us, event | category | flops | bytes accessed | tf_op | source)
XLA Modules:
  0.0 47.1 jit_solution(7227264276152185676)
XLA Ops:
  0.6 1.9 %shard_map.85 = (f32[2,19,16,512]{3,2,1,0:T(8,128)S(1)}, f32[2,16,512]{2,1,0:T(8,128)S(1)}, f32[2,16,512]{2,1,0:T(8,128)S(1)}, f32[2,24,128]{2,1,0:T(8,128)S(1)}, f32[2,24,128]{2,1,0:T(8,128)S(1)}) custom-call(f32[2,19,16,512]{3,2,1,0:T(8,128)} %pops.1, s32[2,16,512]{2,1,0:T(8,128)} %mask.1, f32[2,16,512]{2,1,0:T(8,128)} %frac_in.1, f32[2,16,512]{2,1,0:T(8,128)} %probe_in.1), custom_call_target="tpu_custom_call" | custom-call | tf_op jit(solution)/shard_map/pallas_call | solution.py:635
  2.6 3.0 %collective-permute-start = (f32[2,24,128]{2,1,0:T(8,128)S(1)}, f32[2,24,128]{2,1,0:T(8,128)S(1)}, u32[]{:S(2)}, u32[]{:S(2)}) collective-permute-start(f32[2,24,128]{2,1,0:T(8,128)S(1)} %get-tuple-element.50), channel_id=1, source_target_pairs={{2,0},{0,4},{4,8},{8,12},{12,16},{16,20},{20,24},{24,28},{3,1},{1,... | collective-permute-start | bytes 73736 | tf_op jit(solution)/shard_map/ppermute | solution.py:661
  5.6 0.1 collective-permute-start.1
  5.6 0.3 shard_map.87
  5.9 2.0 %collective-permute-start.2 = (f32[2,80,128]{2,1,0:T(8,128)S(1)}, f32[2,80,128]{2,1,0:T(8,128)S(1)}, u32[]{:S(2)}, u32[]{:S(2)}) collective-permute-start(f32[2,80,128]{2,1,0:T(8,128)S(1)} %shard_map.87), channel_id=1, source_target_pairs={{0,2},{1,3},{2,0},{3,1},{4,6},{5,7},{6,4},{7,5},{8,10},{9,11},{10,... | collective-permute-start | bytes 245768 | tf_op jit(solution)/shard_map/ppermute | solution.py:663
  8.0 0.0 collective-permute-done.after
  8.0 1.4 %collective-permute-start.3 = (f32[2,24,128]{2,1,0:T(8,128)S(1)}, f32[2,24,128]{2,1,0:T(8,128)S(1)}, u32[]{:S(2)}, u32[]{:S(2)}) collective-permute-start(f32[2,24,128]{2,1,0:T(8,128)S(1)} %collective-permute-done.after), channel_id=1, source_target_pairs={{0,2},{1,3},{2,0},{3,1},{4,6},{5,7},{6,4},{7,5},{8,10},{9,11},{10,... | collective-permute-start | bytes 73736 | tf_op jit(solution)/shard_map/ppermute | solution.py:665
  9.4 0.6 %collective-permute-start.4 = (f32[2,24,128]{2,1,0:T(8,128)S(1)}, f32[2,24,128]{2,1,0:T(8,128)S(1)}, u32[]{:S(2)}, u32[]{:S(2)}) collective-permute-start(f32[2,24,128]{2,1,0:T(8,128)S(1)} %collective-permute-done.1), channel_id=1, source_target_pairs={{0,2},{1,3},{2,0},{3,1},{4,6},{5,7},{6,4},{7,5},{8,10},{9,11},{10,... | collective-permute-start | bytes 73736 | tf_op jit(solution)/shard_map/ppermute | solution.py:664
  10.0 1.8 %collective-permute-done.3 = f32[2,24,128]{2,1,0:T(8,128)S(1)} collective-permute-done((f32[2,24,128]{2,1,0:T(8,128)S(1)}, f32[2,24,128]{2,1,0:T(8,128)S(1)}, u32[]{:S(2)}, u32[]{:S(2)}) %collective-permute-start.3) | collective-permute-done | bytes 24608 | tf_op jit(solution)/shard_map/ppermute | solution.py:665
  11.8 1.4 %collective-permute-done.4 = f32[2,24,128]{2,1,0:T(8,128)S(1)} collective-permute-done((f32[2,24,128]{2,1,0:T(8,128)S(1)}, f32[2,24,128]{2,1,0:T(8,128)S(1)}, u32[]{:S(2)}, u32[]{:S(2)}) %collective-permute-start.4) | collective-permute-done | bytes 24608 | tf_op jit(solution)/shard_map/ppermute | solution.py:664
  13.3 0.0 copy-start.3
  13.3 0.1 collective-permute-start.5
  13.4 0.5 %shard_map.86 = (f32[2,19,16,512]{3,2,1,0:T(8,128)S(1)}, f32[2,10,16,512]{3,2,1,0:T(8,128)S(1)}) custom-call(f32[2,19,16,512]{3,2,1,0:T(8,128)S(1)} %get-tuple-element.21.post, f32[2,16,512]{2,1,0:T(8,128)S(1)} %get-tuple-element.22.probe, f32[2,24,128]{2,1,0:T(8,128)S(1)} %collective-permute-done.after), custom_call_target="tpu_custom_call" | custom-call | tf_op jit(solution)/shard_map/pallas_call | solution.py:635
  13.9 1.0 %collective-permute-done.5 = f32[4,128,128]{2,1,0:T(8,128)S(1)} collective-permute-done((f32[4,128,128]{2,1,0:T(8,128)S(1)}, f32[4,128,128]{2,1,0:T(8,128)S(1)}, u32[]{:S(2)}, u32[]{:S(2)}) %collective-permute-start.5) | collective-permute-done | bytes 262176 | tf_op jit(solution)/shard_map/ppermute | solution.py:677
  15.0 2.6 %shard_map.88 = (f32[2,19,16,512]{3,2,1,0:T(8,128)S(1)}, f32[2,19,16,512]{3,2,1,0:T(8,128)S(1)}, f32[2,16,512]{2,1,0:T(8,128)S(1)}, f32[2,40,128]{2,1,0:T(8,128)S(1)}, f32[2,40,128]{2,1,0:T(8,128)S(1)}) custom-call(s32[64]{0:T(128)S(1)} %copy-done.3, f32[2,19,16,512]{3,2,1,0:T(8,128)S(1)} %get-tuple-element.25.moved, ...), custom_call_target="tpu_custom_call" | custom-call | tf_op jit(solution)/shard_map/pallas_call | solution.py:635
  17.5 2.5 %collective-permute-start.6 = (f32[2,40,128]{2,1,0:T(8,128)S(1)}, f32[2,40,128]{2,1,0:T(8,128)S(1)}, u32[]{:S(2)}, u32[]{:S(2)}) collective-permute-start(f32[2,40,128]{2,1,0:T(8,128)S(1)} %get-tuple-element.44), channel_id=1, source_target_pairs={{2,0},{0,4},{4,8},{8,12},{12,16},{16,20},{20,24},{24,28},{3,1},{1,... | collective-permute-start | bytes 122888 | tf_op jit(solution)/shard_map/ppermute | solution.py:661
  20.0 0.4 shard_map.90
  20.5 0.7 %collective-permute-start.8 = (f32[2,144,128]{2,1,0:T(8,128)S(1)}, f32[2,144,128]{2,1,0:T(8,128)S(1)}, u32[]{:S(2)}, u32[]{:S(2)}) collective-permute-start(f32[2,144,128]{2,1,0:T(8,128)S(1)} %shard_map.90), channel_id=1, source_target_pairs={{0,2},{1,3},{2,0},{3,1},{4,6},{5,7},{6,4},{7,5},{8,10},{9,11},{10,... | collective-permute-start | bytes 442376 | tf_op jit(solution)/shard_map/ppermute | solution.py:663
  21.2 0.5 %collective-permute-done.6.after = f32[2,40,128]{2,1,0:T(8,128)S(1)} collective-permute-done((f32[2,40,128]{2,1,0:T(8,128)S(1)}, f32[2,40,128]{2,1,0:T(8,128)S(1)}, u32[]{:S(2)}, u32[]{:S(2)}) %collective-permute-start.6) | collective-permute-done | bytes 40992 | tf_op jit(solution)/shard_map/ppermute | solution.py:661
  21.7 0.9 %collective-permute-start.9 = (f32[2,40,128]{2,1,0:T(8,128)S(1)}, f32[2,40,128]{2,1,0:T(8,128)S(1)}, u32[]{:S(2)}, u32[]{:S(2)}) collective-permute-start(f32[2,40,128]{2,1,0:T(8,128)S(1)} %collective-permute-done.6.after), channel_id=1, source_target_pairs={{0,2},{1,3},{2,0},{3,1},{4,6},{5,7},{6,4},{7,5},{8,10},{9,11},{10,... | collective-permute-start | bytes 122888 | tf_op jit(solution)/shard_map/ppermute | solution.py:665
  22.6 1.5 %collective-permute-done.7 = f32[2,40,128]{2,1,0:T(8,128)S(1)} collective-permute-done((f32[2,40,128]{2,1,0:T(8,128)S(1)}, f32[2,40,128]{2,1,0:T(8,128)S(1)}, u32[]{:S(2)}, u32[]{:S(2)}) %collective-permute-start.7) | collective-permute-done | bytes 40992 | tf_op jit(solution)/shard_map/ppermute | solution.py:660
  24.0 0.4 collective-permute-start.10
  24.4 2.1 %shard_map.89 = (f32[2,19,16,512]{3,2,1,0:T(8,128)S(1)}, f32[2,19,16,512]{3,2,1,0:T(8,128)S(1)}, bf16[2,16,128,512]{3,2,1,0:T(8,128)(2,1)S(1)}) custom-call(f32[2,19,16,512]{3,2,1,0:T(8,128)S(1)} %get-tuple-element.28.post1, f32[2,19,16,512]{3,2,1,0:T(8,128)S(1)} %get-tuple-element.29.adj1, s32[2,16,512]{2,1,0:T(8,128)S(1)} %copy-done.2, ...), custom_call_target="tpu_custom_call" | custom-call | tf_op jit(solution)/shard_map/pallas_call | solution.py:635
  26.6 0.0 copy-start
  26.6 0.0 copy-start.1
  26.6 0.9 %collective-permute-done.9 = f32[2,40,128]{2,1,0:T(8,128)S(1)} collective-permute-done((f32[2,40,128]{2,1,0:T(8,128)S(1)}, f32[2,40,128]{2,1,0:T(8,128)S(1)}, u32[]{:S(2)}, u32[]{:S(2)}) %collective-permute-start.9) | collective-permute-done | bytes 40992 | tf_op jit(solution)/shard_map/ppermute | solution.py:665
  27.5 0.6 %collective-permute-done.10 = f32[2,40,128]{2,1,0:T(8,128)S(1)} collective-permute-done((f32[2,40,128]{2,1,0:T(8,128)S(1)}, f32[2,40,128]{2,1,0:T(8,128)S(1)}, u32[]{:S(2)}, u32[]{:S(2)}) %collective-permute-start.10) | collective-permute-done | bytes 40992 | tf_op jit(solution)/shard_map/ppermute | solution.py:664
  28.1 2.5 %all_gather.3.around = f32[8,224,128]{2,1,0:T(8,128)S(1)} all-gather(f32[4,224,128]{2,1,0:T(8,128)S(1)} %maximum_maximum_fusion), channel_id=1, replica_groups={{0,1},{2,3},{4,5},{6,7},{8,9},{10,11},{12,13},{14,15},{16,17},{18,19},{..., dimensions={0}, use_global_device_ids=true | all-gather | bytes 1376256 | tf_op jit(solution)/shard_map/all_gather | solution.py:680
  30.6 4.0 %shard_map.91 = (f32[2,19,16,512]{3,2,1,0:T(8,128)}, f32[2,19,16,512]{3,2,1,0:T(8,128)}, f32[16,128]{1,0:T(8,128)S(1)}) custom-call(s32[64]{0:T(128)S(1)} %copy-done.3, f32[2,19,16,512]{3,2,1,0:T(8,128)S(1)} %get-tuple-element.32.moved, f32[2,19,16,512]{3,2,1,0:T(8,128)S(1)} %get-tuple-element.33.back, ...), custom_call_target="tpu_custom_call" | custom-call | tf_op jit(solution)/shard_map/pallas_call | solution.py:635
  34.6 0.1 all_to_all.6
  34.7 11.9 %all_to_all.9 = f32[32,1,64]{2,1,0:T(1,128)S(1)} all-to-all(f32[32,1,64]{2,1,0:T(1,128)S(1)} %bitcast.1), channel_id=1, replica_groups=mesh['gx'=8,'yz'=4] {'gx','yz'}, dimensions={0} | all-to-all | bytes 16384 | tf_op jit(solution)/shard_map/all_to_all | solution.py:756
  46.5 0.6 %reduce_sum.9 = f32[64]{0:T(128)} reduce(f32[32,1,64]{2,1,0:T(1,128)S(1)} %all_to_all.9, f32[]{:T(128)} %constant.2.clone.1), dimensions={0,1}, to_apply=%region_0.1 | reduce | flops 1984 | bytes 8452 | tf_op jit(solution)/shard_map/reduce_sum | solution.py:759
  (18 shorter events, 0.2 us)
Async XLA Ops:
  2.6 5.4 %collective-permute-start = (f32[2,24,128]{2,1,0:T(8,128)S(1)}, f32[2,24,128]{2,1,0:T(8,128)S(1)}, u32[]{:S(2)}, u32[]{:S(2)}) collective-permute-start(f32[2,24,128]{2,1,0:T(8,128)S(1)} %get-tuple-element.50), channel_id=1, source_target_pairs={{2,0},{0,4},{4,8},{8,12},{12,16},{16,20},{20,24},{24,28},{3,1},{1,... | collective-permute-start | bytes 73736 | tf_op jit(solution)/shard_map/ppermute | solution.py:661
  5.6 3.9 %collective-permute-start.1 = (f32[2,24,128]{2,1,0:T(8,128)S(1)}, f32[2,24,128]{2,1,0:T(8,128)S(1)}, u32[]{:S(2)}, u32[]{:S(2)}) collective-permute-start(f32[2,24,128]{2,1,0:T(8,128)S(1)} %get-tuple-element.49), channel_id=1, source_target_pairs={{0,2},{4,0},{8,4},{12,8},{16,12},{20,16},{24,20},{28,24},{1,3},{5,... | collective-permute-start | bytes 73736 | tf_op jit(solution)/shard_map/ppermute | solution.py:660
  5.9 7.3 %collective-permute-start.2 = (f32[2,80,128]{2,1,0:T(8,128)S(1)}, f32[2,80,128]{2,1,0:T(8,128)S(1)}, u32[]{:S(2)}, u32[]{:S(2)}) collective-permute-start(f32[2,80,128]{2,1,0:T(8,128)S(1)} %shard_map.87), channel_id=1, source_target_pairs={{0,2},{1,3},{2,0},{3,1},{4,6},{5,7},{6,4},{7,5},{8,10},{9,11},{10,... | collective-permute-start | bytes 245768 | tf_op jit(solution)/shard_map/ppermute | solution.py:663
  8.0 3.8 %collective-permute-start.3 = (f32[2,24,128]{2,1,0:T(8,128)S(1)}, f32[2,24,128]{2,1,0:T(8,128)S(1)}, u32[]{:S(2)}, u32[]{:S(2)}) collective-permute-start(f32[2,24,128]{2,1,0:T(8,128)S(1)} %collective-permute-done.after), channel_id=1, source_target_pairs={{0,2},{1,3},{2,0},{3,1},{4,6},{5,7},{6,4},{7,5},{8,10},{9,11},{10,... | collective-permute-start | bytes 73736 | tf_op jit(solution)/shard_map/ppermute | solution.py:665
  9.4 3.8 %collective-permute-start.4 = (f32[2,24,128]{2,1,0:T(8,128)S(1)}, f32[2,24,128]{2,1,0:T(8,128)S(1)}, u32[]{:S(2)}, u32[]{:S(2)}) collective-permute-start(f32[2,24,128]{2,1,0:T(8,128)S(1)} %collective-permute-done.1), channel_id=1, source_target_pairs={{0,2},{1,3},{2,0},{3,1},{4,6},{5,7},{6,4},{7,5},{8,10},{9,11},{10,... | collective-permute-start | bytes 73736 | tf_op jit(solution)/shard_map/ppermute | solution.py:664
  13.3 1.7 %copy-start.3 = (s32[64]{0:T(128)S(1)}, s32[64]{0:T(128)}, u32[]{:S(2)}) copy-start(s32[64]{0:T(128)} %pos.3) | copy-start | bytes 772
  13.3 1.6 %collective-permute-start.5 = (f32[4,128,128]{2,1,0:T(8,128)S(1)}, f32[4,128,128]{2,1,0:T(8,128)S(1)}, u32[]{:S(2)}, u32[]{:S(2)}) collective-permute-start(f32[4,128,128]{2,1,0:T(8,128)S(1)} %maximum_maximum_fusion.1), channel_id=1, source_target_pairs={{0,1},{1,0},{2,3},{3,2},{4,5},{5,4},{6,7},{7,6},{8,9},{9,8},{10,11... | collective-permute-start | bytes 786440 | tf_op jit(solution)/shard_map/ppermute | solution.py:677
  17.5 4.1 %collective-permute-start.6 = (f32[2,40,128]{2,1,0:T(8,128)S(1)}, f32[2,40,128]{2,1,0:T(8,128)S(1)}, u32[]{:S(2)}, u32[]{:S(2)}) collective-permute-start(f32[2,40,128]{2,1,0:T(8,128)S(1)} %get-tuple-element.44), channel_id=1, source_target_pairs={{2,0},{0,4},{4,8},{8,12},{12,16},{16,20},{20,24},{24,28},{3,1},{1,... | collective-permute-start | bytes 122888 | tf_op jit(solution)/shard_map/ppermute | solution.py:661
  20.0 4.0 %collective-permute-start.7 = (f32[2,40,128]{2,1,0:T(8,128)S(1)}, f32[2,40,128]{2,1,0:T(8,128)S(1)}, u32[]{:S(2)}, u32[]{:S(2)}) collective-permute-start(f32[2,40,128]{2,1,0:T(8,128)S(1)} %get-tuple-element.43), channel_id=1, source_target_pairs={{0,2},{4,0},{8,4},{12,8},{16,12},{20,16},{24,20},{28,24},{1,3},{5,... | collective-permute-start | bytes 122888 | tf_op jit(solution)/shard_map/ppermute | solution.py:660
  20.0 4.4 %copy-start.2 = (s32[2,16,512]{2,1,0:T(8,128)S(1)}, s32[2,16,512]{2,1,0:T(8,128)}, u32[]{:S(2)}) copy-start(s32[2,16,512]{2,1,0:T(8,128)} %patch.3) | copy-start | bytes 196612
  20.5 7.6 %collective-permute-start.8 = (f32[2,144,128]{2,1,0:T(8,128)S(1)}, f32[2,144,128]{2,1,0:T(8,128)S(1)}, u32[]{:S(2)}, u32[]{:S(2)}) collective-permute-start(f32[2,144,128]{2,1,0:T(8,128)S(1)} %shard_map.90), channel_id=1, source_target_pairs={{0,2},{1,3},{2,0},{3,1},{4,6},{5,7},{6,4},{7,5},{8,10},{9,11},{10,... | collective-permute-start | bytes 442376 | tf_op jit(solution)/shard_map/ppermute | solution.py:663
  21.7 5.8 %collective-permute-start.9 = (f32[2,40,128]{2,1,0:T(8,128)S(1)}, f32[2,40,128]{2,1,0:T(8,128)S(1)}, u32[]{:S(2)}, u32[]{:S(2)}) collective-permute-start(f32[2,40,128]{2,1,0:T(8,128)S(1)} %collective-permute-done.6.after), channel_id=1, source_target_pairs={{0,2},{1,3},{2,0},{3,1},{4,6},{5,7},{6,4},{7,5},{8,10},{9,11},{10,... | collective-permute-start | bytes 122888 | tf_op jit(solution)/shard_map/ppermute | solution.py:665
  24.0 4.0 %collective-permute-start.10 = (f32[2,40,128]{2,1,0:T(8,128)S(1)}, f32[2,40,128]{2,1,0:T(8,128)S(1)}, u32[]{:S(2)}, u32[]{:S(2)}) collective-permute-start(f32[2,40,128]{2,1,0:T(8,128)S(1)} %collective-permute-done.7), channel_id=1, source_target_pairs={{0,2},{1,3},{2,0},{3,1},{4,6},{5,7},{6,4},{7,5},{8,10},{9,11},{10,... | collective-permute-start | bytes 122888 | tf_op jit(solution)/shard_map/ppermute | solution.py:664
  26.6 4.0 %copy-start = (f32[2,19,16,512]{3,2,1,0:T(8,128)S(1)}, f32[2,19,16,512]{3,2,1,0:T(8,128)}, u32[]{:S(2)}) copy-start(f32[2,19,16,512]{3,2,1,0:T(8,128)} %pops.1) | copy-start | bytes 3735556
  26.6 4.0 %copy-start.1 = (s32[2,16,512]{2,1,0:T(8,128)S(1)}, s32[2,16,512]{2,1,0:T(8,128)}, u32[]{:S(2)}) copy-start(s32[2,16,512]{2,1,0:T(8,128)} %mask.1) | copy-start | bytes 196612

commit v8 on v7

--- a/solution.py
+++ b/solution.py
@@ -459,14 +459,9 @@
         pltpu.make_async_copy(src, dst, sems.at[n])
         for n, (src, dst) in enumerate(((mask_in, mask), (frac_in, frac), (probe_in, probe)))
     ]
-    halves = [(t, r) for t in range(count) for r in range(2)]
     large = [
-        pltpu.make_async_copy(
-            pops_in.at[t, :, pl.ds(8 * r, 8), :],
-            pops.at[t, :, pl.ds(8 * r, 8), :],
-            sems.at[len(small) + n],
-        )
-        for n, (t, r) in enumerate(halves)
+        pltpu.make_async_copy(pops_in.at[t], pops.at[t], sems.at[len(small) + t])
+        for t in range(count)
     ]
     for copy in small[:2] + large + small[2:]:
         copy.start()
@@ -476,8 +471,8 @@
 
     def collides(t):
         def run(r, c):
-            if c == 0:
-                large[halves.index((t, r))].wait()
+            if r == 0 and c == 0:
+                large[t].wait()
             rows = slice(8 * r, 8 * r + 8)
             lanes = slice(LANES * c, LANES * (c + 1))
             f = [pops[t, i, rows, lanes] for i in range(Q)]
@@ -705,7 +700,7 @@
             pltpu.VMEM(field, jnp.float32),
             pltpu.VMEM(plane, jnp.int32),
             pltpu.VMEM(plane, jnp.float32),
-            pltpu.SemaphoreType.DMA((3 + 2 * count,)),
+            pltpu.SemaphoreType.DMA((3 + count,)),
         ],
         tuple(
             pltpu.with_memory_space_constraint(x, pltpu.HBM)

time: 47.3 us -> 47.2 us (level)
  no operation moved by 1% of the time
where the time goes in v8:
time: 47.2 us; the launch traced here: 47 us
  blocking collectives  14.3 us (30%)
  Pallas kernels  11.8 us (25%)
  starting transfers between devices  11.7 us (25%)
  waiting for transfers between devices  7.68 us (16%)
  between operations  0.79 us (2%)
  other arithmetic  0.72 us (2%)
    all_to_all x1, blocking collectives, body(): lax.all_to_all(sums.reshape(parts, patch_dev), ('gx', 'yz'), 0, 0, tiled=...  11.9 us
    pallas_call x7, Pallas kernels, call(): pl.pallas_call(kernel, out_shape=[jax.ShapeDtypeStruct(s, types.get(n, jn...  11.8 us
    ppermute x2, starting transfers between devices, exchange(): lax.ppermute(jnp.where(rising, dn, up), ('gx', 'yz'), [(j, i) for i, j in...  5.46 us
    ppermute x2, starting transfers between devices, exchange(): ab_far = lax.ppermute(ab, 'yz', across)  2.72 us
    ppermute x2, waiting for transfers between devices, exchange(): two_far = lax.ppermute(two, 'yz', across)  2.65 us
    all_gather x1, blocking collectives, exchange(): lax.all_gather(both, 'yz', axis=0, tiled=True, axis_index_groups=pairs)  2.46 us
    ppermute x2, starting transfers between devices, exchange(): two_far = lax.ppermute(two, 'yz', across)  2.31 us
    ppermute x2, waiting for transfers between devices, exchange(): one_far = lax.ppermute(one, 'yz', across)  2 us
  transfers between devices with their start and end apart: 11, of which 7 were waited for; matrix products, arithmetic and copies ran while one was open for 0% of the time, Pallas kernels for 7%

profile of v8, /device:TPU:0, one launch (start us, length us, event | category | flops | bytes accessed | tf_op | source)
XLA Modules:
  0.0 47.0 jit_solution(14092228097877323401)
XLA Ops:
  0.6 1.9 %shard_map.85 = (f32[2,19,16,512]{3,2,1,0:T(8,128)S(1)}, f32[2,16,512]{2,1,0:T(8,128)S(1)}, f32[2,16,512]{2,1,0:T(8,128)S(1)}, f32[2,24,128]{2,1,0:T(8,128)S(1)}, f32[2,24,128]{2,1,0:T(8,128)S(1)}) custom-call(f32[2,19,16,512]{3,2,1,0:T(8,128)} %pops.1, s32[2,16,512]{2,1,0:T(8,128)} %mask.1, f32[2,16,512]{2,1,0:T(8,128)} %frac_in.1, f32[2,16,512]{2,1,0:T(8,128)} %probe_in.1), custom_call_target="tpu_custom_call" | custom-call | tf_op jit(solution)/shard_map/pallas_call | solution.py:630
  2.5 3.0 %collective-permute-start = (f32[2,24,128]{2,1,0:T(8,128)S(1)}, f32[2,24,128]{2,1,0:T(8,128)S(1)}, u32[]{:S(2)}, u32[]{:S(2)}) collective-permute-start(f32[2,24,128]{2,1,0:T(8,128)S(1)} %get-tuple-element.50), channel_id=1, source_target_pairs={{2,0},{0,4},{4,8},{8,12},{12,16},{16,20},{20,24},{24,28},{3,1},{1,... | collective-permute-start | bytes 73736 | tf_op jit(solution)/shard_map/ppermute | solution.py:656
  5.5 0.1 collective-permute-start.1
  5.6 0.3 shard_map.87
  5.9 2.0 %collective-permute-start.2 = (f32[2,80,128]{2,1,0:T(8,128)S(1)}, f32[2,80,128]{2,1,0:T(8,128)S(1)}, u32[]{:S(2)}, u32[]{:S(2)}) collective-permute-start(f32[2,80,128]{2,1,0:T(8,128)S(1)} %shard_map.87), channel_id=1, source_target_pairs={{0,2},{1,3},{2,0},{3,1},{4,6},{5,7},{6,4},{7,5},{8,10},{9,11},{10,... | collective-permute-start | bytes 245768 | tf_op jit(solution)/shard_map/ppermute | solution.py:658
  7.9 1.4 %collective-permute-start.3 = (f32[2,24,128]{2,1,0:T(8,128)S(1)}, f32[2,24,128]{2,1,0:T(8,128)S(1)}, u32[]{:S(2)}, u32[]{:S(2)}) collective-permute-start(f32[2,24,128]{2,1,0:T(8,128)S(1)} %collective-permute-done.after), channel_id=1, source_target_pairs={{0,2},{1,3},{2,0},{3,1},{4,6},{5,7},{6,4},{7,5},{8,10},{9,11},{10,... | collective-permute-start | bytes 73736 | tf_op jit(solution)/shard_map/ppermute | solution.py:660
  9.4 0.0 collective-permute-done.1
  9.4 0.6 %collective-permute-start.4 = (f32[2,24,128]{2,1,0:T(8,128)S(1)}, f32[2,24,128]{2,1,0:T(8,128)S(1)}, u32[]{:S(2)}, u32[]{:S(2)}) collective-permute-start(f32[2,24,128]{2,1,0:T(8,128)S(1)} %collective-permute-done.1), channel_id=1, source_target_pairs={{0,2},{1,3},{2,0},{3,1},{4,6},{5,7},{6,4},{7,5},{8,10},{9,11},{10,... | collective-permute-start | bytes 73736 | tf_op jit(solution)/shard_map/ppermute | solution.py:659
  10.0 1.8 %collective-permute-done.3 = f32[2,24,128]{2,1,0:T(8,128)S(1)} collective-permute-done((f32[2,24,128]{2,1,0:T(8,128)S(1)}, f32[2,24,128]{2,1,0:T(8,128)S(1)}, u32[]{:S(2)}, u32[]{:S(2)}) %collective-permute-start.3) | collective-permute-done | bytes 24608 | tf_op jit(solution)/shard_map/ppermute | solution.py:660
  11.8 1.4 %collective-permute-done.4 = f32[2,24,128]{2,1,0:T(8,128)S(1)} collective-permute-done((f32[2,24,128]{2,1,0:T(8,128)S(1)}, f32[2,24,128]{2,1,0:T(8,128)S(1)}, u32[]{:S(2)}, u32[]{:S(2)}) %collective-permute-start.4) | collective-permute-done | bytes 24608 | tf_op jit(solution)/shard_map/ppermute | solution.py:659
  13.2 0.0 copy-start.3
  13.3 0.1 collective-permute-start.5
  13.3 0.5 %shard_map.86 = (f32[2,19,16,512]{3,2,1,0:T(8,128)S(1)}, f32[2,10,16,512]{3,2,1,0:T(8,128)S(1)}) custom-call(f32[2,19,16,512]{3,2,1,0:T(8,128)S(1)} %get-tuple-element.21.post, f32[2,16,512]{2,1,0:T(8,128)S(1)} %get-tuple-element.22.probe, f32[2,24,128]{2,1,0:T(8,128)S(1)} %collective-permute-done.after), custom_call_target="tpu_custom_call" | custom-call | tf_op jit(solution)/shard_map/pallas_call | solution.py:630
  13.8 1.0 %collective-permute-done.5 = f32[4,128,128]{2,1,0:T(8,128)S(1)} collective-permute-done((f32[4,128,128]{2,1,0:T(8,128)S(1)}, f32[4,128,128]{2,1,0:T(8,128)S(1)}, u32[]{:S(2)}, u32[]{:S(2)}) %collective-permute-start.5) | collective-permute-done | bytes 262176 | tf_op jit(solution)/shard_map/ppermute | solution.py:672
  14.9 2.6 %shard_map.88 = (f32[2,19,16,512]{3,2,1,0:T(8,128)S(1)}, f32[2,19,16,512]{3,2,1,0:T(8,128)S(1)}, f32[2,16,512]{2,1,0:T(8,128)S(1)}, f32[2,40,128]{2,1,0:T(8,128)S(1)}, f32[2,40,128]{2,1,0:T(8,128)S(1)}) custom-call(s32[64]{0:T(128)S(1)} %copy-done.3, f32[2,19,16,512]{3,2,1,0:T(8,128)S(1)} %get-tuple-element.25.moved, ...), custom_call_target="tpu_custom_call" | custom-call | tf_op jit(solution)/shard_map/pallas_call | solution.py:630
  17.5 2.5 %collective-permute-start.6 = (f32[2,40,128]{2,1,0:T(8,128)S(1)}, f32[2,40,128]{2,1,0:T(8,128)S(1)}, u32[]{:S(2)}, u32[]{:S(2)}) collective-permute-start(f32[2,40,128]{2,1,0:T(8,128)S(1)} %get-tuple-element.44), channel_id=1, source_target_pairs={{2,0},{0,4},{4,8},{8,12},{12,16},{16,20},{20,24},{24,28},{3,1},{1,... | collective-permute-start | bytes 122888 | tf_op jit(solution)/shard_map/ppermute | solution.py:656
  20.0 0.4 shard_map.90
  20.4 0.7 %collective-permute-start.8 = (f32[2,144,128]{2,1,0:T(8,128)S(1)}, f32[2,144,128]{2,1,0:T(8,128)S(1)}, u32[]{:S(2)}, u32[]{:S(2)}) collective-permute-start(f32[2,144,128]{2,1,0:T(8,128)S(1)} %shard_map.90), channel_id=1, source_target_pairs={{0,2},{1,3},{2,0},{3,1},{4,6},{5,7},{6,4},{7,5},{8,10},{9,11},{10,... | collective-permute-start | bytes 442376 | tf_op jit(solution)/shard_map/ppermute | solution.py:658
  21.1 0.5 %collective-permute-done.6.after = f32[2,40,128]{2,1,0:T(8,128)S(1)} collective-permute-done((f32[2,40,128]{2,1,0:T(8,128)S(1)}, f32[2,40,128]{2,1,0:T(8,128)S(1)}, u32[]{:S(2)}, u32[]{:S(2)}) %collective-permute-start.6) | collective-permute-done | bytes 40992 | tf_op jit(solution)/shard_map/ppermute | solution.py:656
  21.6 0.9 %collective-permute-start.9 = (f32[2,40,128]{2,1,0:T(8,128)S(1)}, f32[2,40,128]{2,1,0:T(8,128)S(1)}, u32[]{:S(2)}, u32[]{:S(2)}) collective-permute-start(f32[2,40,128]{2,1,0:T(8,128)S(1)} %collective-permute-done.6.after), channel_id=1, source_target_pairs={{0,2},{1,3},{2,0},{3,1},{4,6},{5,7},{6,4},{7,5},{8,10},{9,11},{10,... | collective-permute-start | bytes 122888 | tf_op jit(solution)/shard_map/ppermute | solution.py:660
  22.5 1.5 %collective-permute-done.7 = f32[2,40,128]{2,1,0:T(8,128)S(1)} collective-permute-done((f32[2,40,128]{2,1,0:T(8,128)S(1)}, f32[2,40,128]{2,1,0:T(8,128)S(1)}, u32[]{:S(2)}, u32[]{:S(2)}) %collective-permute-start.7) | collective-permute-done | bytes 40992 | tf_op jit(solution)/shard_map/ppermute | solution.py:655
  24.0 0.4 collective-permute-start.10
  24.4 2.1 %shard_map.89 = (f32[2,19,16,512]{3,2,1,0:T(8,128)S(1)}, f32[2,19,16,512]{3,2,1,0:T(8,128)S(1)}, bf16[2,16,128,512]{3,2,1,0:T(8,128)(2,1)S(1)}) custom-call(f32[2,19,16,512]{3,2,1,0:T(8,128)S(1)} %get-tuple-element.28.post1, f32[2,19,16,512]{3,2,1,0:T(8,128)S(1)} %get-tuple-element.29.adj1, s32[2,16,512]{2,1,0:T(8,128)S(1)} %copy-done.2, ...), custom_call_target="tpu_custom_call" | custom-call | tf_op jit(solution)/shard_map/pallas_call | solution.py:630
  26.5 0.0 copy-start
  26.5 0.0 copy-start.1
  26.6 0.9 %collective-permute-done.9 = f32[2,40,128]{2,1,0:T(8,128)S(1)} collective-permute-done((f32[2,40,128]{2,1,0:T(8,128)S(1)}, f32[2,40,128]{2,1,0:T(8,128)S(1)}, u32[]{:S(2)}, u32[]{:S(2)}) %collective-permute-start.9) | collective-permute-done | bytes 40992 | tf_op jit(solution)/shard_map/ppermute | solution.py:660
  27.4 0.6 %collective-permute-done.10 = f32[2,40,128]{2,1,0:T(8,128)S(1)} collective-permute-done((f32[2,40,128]{2,1,0:T(8,128)S(1)}, f32[2,40,128]{2,1,0:T(8,128)S(1)}, u32[]{:S(2)}, u32[]{:S(2)}) %collective-permute-start.10) | collective-permute-done | bytes 40992 | tf_op jit(solution)/shard_map/ppermute | solution.py:659
  28.0 2.5 %all_gather.3.around = f32[8,224,128]{2,1,0:T(8,128)S(1)} all-gather(f32[4,224,128]{2,1,0:T(8,128)S(1)} %maximum_maximum_fusion), channel_id=1, replica_groups={{0,1},{2,3},{4,5},{6,7},{8,9},{10,11},{12,13},{14,15},{16,17},{18,19},{..., dimensions={0}, use_global_device_ids=true | all-gather | bytes 1376256 | tf_op jit(solution)/shard_map/all_gather | solution.py:675
  30.5 4.0 %shard_map.91 = (f32[2,19,16,512]{3,2,1,0:T(8,128)}, f32[2,19,16,512]{3,2,1,0:T(8,128)}, f32[16,128]{1,0:T(8,128)S(1)}) custom-call(s32[64]{0:T(128)S(1)} %copy-done.3, f32[2,19,16,512]{3,2,1,0:T(8,128)S(1)} %get-tuple-element.32.moved, f32[2,19,16,512]{3,2,1,0:T(8,128)S(1)} %get-tuple-element.33.back, ...), custom_call_target="tpu_custom_call" | custom-call | tf_op jit(solution)/shard_map/pallas_call | solution.py:630
  34.5 0.1 all_to_all.6
  34.6 11.9 %all_to_all.9 = f32[32,1,64]{2,1,0:T(1,128)S(1)} all-to-all(f32[32,1,64]{2,1,0:T(1,128)S(1)} %bitcast.1), channel_id=1, replica_groups=mesh['gx'=8,'yz'=4] {'gx','yz'}, dimensions={0} | all-to-all | bytes 16384 | tf_op jit(solution)/shard_map/all_to_all | solution.py:751
  46.5 0.6 %reduce_sum.9 = f32[64]{0:T(128)} reduce(f32[32,1,64]{2,1,0:T(1,128)S(1)} %all_to_all.9, f32[]{:T(128)} %constant.2.clone.1), dimensions={0,1}, to_apply=%region_0.1 | reduce | flops 1984 | bytes 8452 | tf_op jit(solution)/shard_map/reduce_sum | solution.py:754
  (18 shorter events, 0.2 us)
Async XLA Ops:
  2.5 5.4 %collective-permute-start = (f32[2,24,128]{2,1,0:T(8,128)S(1)}, f32[2,24,128]{2,1,0:T(8,128)S(1)}, u32[]{:S(2)}, u32[]{:S(2)}) collective-permute-start(f32[2,24,128]{2,1,0:T(8,128)S(1)} %get-tuple-element.50), channel_id=1, source_target_pairs={{2,0},{0,4},{4,8},{8,12},{12,16},{16,20},{20,24},{24,28},{3,1},{1,... | collective-permute-start | bytes 73736 | tf_op jit(solution)/shard_map/ppermute | solution.py:656
  5.5 3.9 %collective-permute-start.1 = (f32[2,24,128]{2,1,0:T(8,128)S(1)}, f32[2,24,128]{2,1,0:T(8,128)S(1)}, u32[]{:S(2)}, u32[]{:S(2)}) collective-permute-start(f32[2,24,128]{2,1,0:T(8,128)S(1)} %get-tuple-element.49), channel_id=1, source_target_pairs={{0,2},{4,0},{8,4},{12,8},{16,12},{20,16},{24,20},{28,24},{1,3},{5,... | collective-permute-start | bytes 73736 | tf_op jit(solution)/shard_map/ppermute | solution.py:655
  5.9 7.3 %collective-permute-start.2 = (f32[2,80,128]{2,1,0:T(8,128)S(1)}, f32[2,80,128]{2,1,0:T(8,128)S(1)}, u32[]{:S(2)}, u32[]{:S(2)}) collective-permute-start(f32[2,80,128]{2,1,0:T(8,128)S(1)} %shard_map.87), channel_id=1, source_target_pairs={{0,2},{1,3},{2,0},{3,1},{4,6},{5,7},{6,4},{7,5},{8,10},{9,11},{10,... | collective-permute-start | bytes 245768 | tf_op jit(solution)/shard_map/ppermute | solution.py:658
  7.9 3.8 %collective-permute-start.3 = (f32[2,24,128]{2,1,0:T(8,128)S(1)}, f32[2,24,128]{2,1,0:T(8,128)S(1)}, u32[]{:S(2)}, u32[]{:S(2)}) collective-permute-start(f32[2,24,128]{2,1,0:T(8,128)S(1)} %collective-permute-done.after), channel_id=1, source_target_pairs={{0,2},{1,3},{2,0},{3,1},{4,6},{5,7},{6,4},{7,5},{8,10},{9,11},{10,... | collective-permute-start | bytes 73736 | tf_op jit(solution)/shard_map/ppermute | solution.py:660
  9.4 3.8 %collective-permute-start.4 = (f32[2,24,128]{2,1,0:T(8,128)S(1)}, f32[2,24,128]{2,1,0:T(8,128)S(1)}, u32[]{:S(2)}, u32[]{:S(2)}) collective-permute-start(f32[2,24,128]{2,1,0:T(8,128)S(1)} %collective-permute-done.1), channel_id=1, source_target_pairs={{0,2},{1,3},{2,0},{3,1},{4,6},{5,7},{6,4},{7,5},{8,10},{9,11},{10,... | collective-permute-start | bytes 73736 | tf_op jit(solution)/shard_map/ppermute | solution.py:659
  13.2 1.7 %copy-start.3 = (s32[64]{0:T(128)S(1)}, s32[64]{0:T(128)}, u32[]{:S(2)}) copy-start(s32[64]{0:T(128)} %pos.3) | copy-start | bytes 772
  13.3 1.6 %collective-permute-start.5 = (f32[4,128,128]{2,1,0:T(8,128)S(1)}, f32[4,128,128]{2,1,0:T(8,128)S(1)}, u32[]{:S(2)}, u32[]{:S(2)}) collective-permute-start(f32[4,128,128]{2,1,0:T(8,128)S(1)} %maximum_maximum_fusion.1), channel_id=1, source_target_pairs={{0,1},{1,0},{2,3},{3,2},{4,5},{5,4},{6,7},{7,6},{8,9},{9,8},{10,11... | collective-permute-start | bytes 786440 | tf_op jit(solution)/shard_map/ppermute | solution.py:672
  17.5 4.1 %collective-permute-start.6 = (f32[2,40,128]{2,1,0:T(8,128)S(1)}, f32[2,40,128]{2,1,0:T(8,128)S(1)}, u32[]{:S(2)}, u32[]{:S(2)}) collective-permute-start(f32[2,40,128]{2,1,0:T(8,128)S(1)} %get-tuple-element.44), channel_id=1, source_target_pairs={{2,0},{0,4},{4,8},{8,12},{12,16},{16,20},{20,24},{24,28},{3,1},{1,... | collective-permute-start | bytes 122888 | tf_op jit(solution)/shard_map/ppermute | solution.py:656
  20.0 4.0 %collective-permute-start.7 = (f32[2,40,128]{2,1,0:T(8,128)S(1)}, f32[2,40,128]{2,1,0:T(8,128)S(1)}, u32[]{:S(2)}, u32[]{:S(2)}) collective-permute-start(f32[2,40,128]{2,1,0:T(8,128)S(1)} %get-tuple-element.43), channel_id=1, source_target_pairs={{0,2},{4,0},{8,4},{12,8},{16,12},{20,16},{24,20},{28,24},{1,3},{5,... | collective-permute-start | bytes 122888 | tf_op jit(solution)/shard_map/ppermute | solution.py:655
  20.0 4.4 %copy-start.2 = (s32[2,16,512]{2,1,0:T(8,128)S(1)}, s32[2,16,512]{2,1,0:T(8,128)}, u32[]{:S(2)}) copy-start(s32[2,16,512]{2,1,0:T(8,128)} %patch.3) | copy-start | bytes 196612
  20.4 7.6 %collective-permute-start.8 = (f32[2,144,128]{2,1,0:T(8,128)S(1)}, f32[2,144,128]{2,1,0:T(8,128)S(1)}, u32[]{:S(2)}, u32[]{:S(2)}) collective-permute-start(f32[2,144,128]{2,1,0:T(8,128)S(1)} %shard_map.90), channel_id=1, source_target_pairs={{0,2},{1,3},{2,0},{3,1},{4,6},{5,7},{6,4},{7,5},{8,10},{9,11},{10,... | collective-permute-start | bytes 442376 | tf_op jit(solution)/shard_map/ppermute | solution.py:658
  21.6 5.8 %collective-permute-start.9 = (f32[2,40,128]{2,1,0:T(8,128)S(1)}, f32[2,40,128]{2,1,0:T(8,128)S(1)}, u32[]{:S(2)}, u32[]{:S(2)}) collective-permute-start(f32[2,40,128]{2,1,0:T(8,128)S(1)} %collective-permute-done.6.after), channel_id=1, source_target_pairs={{0,2},{1,3},{2,0},{3,1},{4,6},{5,7},{6,4},{7,5},{8,10},{9,11},{10,... | collective-permute-start | bytes 122888 | tf_op jit(solution)/shard_map/ppermute | solution.py:660
  24.0 4.0 %collective-permute-start.10 = (f32[2,40,128]{2,1,0:T(8,128)S(1)}, f32[2,40,128]{2,1,0:T(8,128)S(1)}, u32[]{:S(2)}, u32[]{:S(2)}) collective-permute-start(f32[2,40,128]{2,1,0:T(8,128)S(1)} %collective-permute-done.7), channel_id=1, source_target_pairs={{0,2},{1,3},{2,0},{3,1},{4,6},{5,7},{6,4},{7,5},{8,10},{9,11},{10,... | collective-permute-start | bytes 122888 | tf_op jit(solution)/shard_map/ppermute | solution.py:659
  26.5 4.0 %copy-start = (f32[2,19,16,512]{3,2,1,0:T(8,128)S(1)}, f32[2,19,16,512]{3,2,1,0:T(8,128)}, u32[]{:S(2)}) copy-start(f32[2,19,16,512]{3,2,1,0:T(8,128)} %pops.1) | copy-start | bytes 3735556
  26.5 4.0 %copy-start.1 = (s32[2,16,512]{2,1,0:T(8,128)S(1)}, s32[2,16,512]{2,1,0:T(8,128)}, u32[]{:S(2)}) copy-start(s32[2,16,512]{2,1,0:T(8,128)} %mask.1) | copy-start | bytes 196612
